TPU v7x, 32 devices: a whole 2x2x4 slice. The times are simulated.
32 devices in a mesh: gx: 2 (over x), gy: 4 (over z), gz: 4 (over y, core).
Axes of the slice: x: 2, y: 2, z: 4, core: 2. Of those that a mesh axis runs over, the one named last changes fastest.
Arguments:
- right_side: float32 [64, 256, 512], P('gx', 'gy', 'gz'), may hold values from -25 to 25
- coarse_inverse: float32 [256, 256], P(('gx', 'gy', 'gz')), may hold values from -0.07 to 0.07, as said below
- sphere_rows: bfloat16 [1536, 128], P(('gx', 'gy', 'gz')), may hold values from 0.5 to 8
- margin_block: int32 [1536, 1], P(('gx', 'gy', 'gz')), may hold values from 0 to 15; in each aligned block of 48 rows (0 to 47, 48 to 95, ...) at most 6 rows name the same one
- margin_column: int32 [1536], P(('gx', 'gy', 'gz')), may hold values from 0 to 2047
Outputs:
- pressure: float32 [64, 256, 512], P('gx', 'gy', 'gz')
- preconditioned: float32 [64, 256, 512], P('gx', 'gy', 'gz')
Inputs may be any that keep to these rules, and one draw needn't show every extreme that they name: `margin_block`: in the rows of one device, no block is named by more than 6 rows, and some block is named by exactly 6. `coarse_inverse`: lower triangular with a positive diagonal.
All inputs are finite; a program needn't handle non-finite values.
Results may differ from a plain program's by a relative error of at most 0.0003.
Values may be sent and summed in bfloat16 or wider, within the bound.
No kernel may reach another device: no remote copies, remote signals or barrier semaphores. Data moves between devices by JAX's collectives and lax.ppermute only.
A program may use at most 64 MiB of HBM per device.

v0:
```python
import jax
import jax.numpy as jnp
from jax import lax
from jax.sharding import PartitionSpec as P

bound_low = 0.1
bound_high = 2.0


def with_halo(value, sides, width):
    for axis, dim in sides:
        size, length = (lax.axis_size(axis), value.shape[dim])
        up = [(i, (i + 1) % size) for i in range(size - 1)]
        down = [(j, i) for i, j in up]
        last = lax.slice_in_dim(value, length - width, length, axis=dim)
        initial = lax.slice_in_dim(value, 0, width, axis=dim)
        before = lax.ppermute(last, axis, up)
        after = lax.ppermute(initial, axis, down)
        value = jnp.concatenate([before, value, after], axis=dim)
    return value


def face_terms(density, padded):
    return (
        2.0 / (density + padded[:-2, 1:-1, 1:-1]),
        2.0 / (density + padded[2:, 1:-1, 1:-1]),
        2.0 / (density + padded[1:-1, :-2, 1:-1]),
        2.0 / (density + padded[1:-1, 2:, 1:-1]),
        2.0 / (density + padded[1:-1, 1:-1, :-2]),
        2.0 / (density + padded[1:-1, 1:-1, 2:]),
    )


def apply_operator(field, faces, diagonal):
    padded = with_halo(field, (("gx", 0), ("gy", 1), ("gz", 2)), 1)
    beside = faces[0] * padded[:-2, 1:-1, 1:-1] + faces[1] * padded[2:, 1:-1, 1:-1]
    beside = beside + faces[2] * padded[1:-1, :-2, 1:-1] + faces[3] * padded[1:-1, 2:, 1:-1]
    beside = beside + faces[4] * padded[1:-1, 1:-1, :-2] + faces[5] * padded[1:-1, 1:-1, 2:]
    return diagonal * field - beside


def chebyshev(residual, faces, diagonal):
    centre_value = 0.5 * (bound_high + bound_low)
    spread = 0.5 * (bound_high - bound_low)
    sigma_ratio = centre_value / spread
    weight_old = 1.0 / sigma_ratio
    update = residual / diagonal / centre_value
    result = update
    weight_new = 1.0 / (2.0 * sigma_ratio - weight_old)
    update = weight_new * weight_old * update + 2.0 * weight_new / spread * (
        (residual - apply_operator(result, faces, diagonal)) / diagonal
    )
    result = result + update
    return result


def coarse_part(residual, coarse_inverse):
    size_x, size_y, size_z = residual.shape
    slabs = coarse_inverse.shape[0]
    local_sums = jnp.sum(residual.reshape(size_x, size_y, slabs, size_z // slabs), axis=(0, 1, 3))
    block = coarse_inverse
    inner = jnp.dot(
        block,
        lax.all_gather(local_sums, ("gx", "gy", "gz"), axis=0, tiled=True),
        precision=lax.Precision.HIGHEST,
    )
    block = coarse_inverse
    coarse_values = lax.psum_scatter(
        jnp.dot(inner, block, precision=lax.Precision.HIGHEST),
        ("gx", "gy", "gz"),
        scatter_dimension=0,
        tiled=True,
    )
    spread_out = jnp.broadcast_to(
        coarse_values.reshape(1, 1, slabs, 1), (size_x, size_y, slabs, size_z // slabs)
    )
    return spread_out.reshape(size_x, size_y, size_z)


def gather_density(sphere_rows, margin_block, margin_column, columns, size_z):
    groups_y = lax.axis_size("gy")
    groups_z = lax.axis_size("gz")
    targets = groups_y * groups_z
    records = sphere_rows.shape[0]
    capacity = max(2, 2 * records // targets)
    target = margin_block[:, 0]
    onehot = (target[:, None] == jnp.arange(targets, dtype=jnp.int32)[None, :]).astype(jnp.int32)
    earlier = jnp.cumsum(onehot, axis=0) - onehot
    slot_index = jnp.sum(earlier * onehot, axis=1)
    position = target * capacity + slot_index
    send_rows = jnp.zeros((targets * capacity, size_z), jnp.bfloat16).at[position].set(sphere_rows)
    send_columns = jnp.zeros((targets * capacity,), jnp.int32).at[position].set(margin_column)
    got_rows, got_columns = (
        lax.all_to_all(
            send_rows.reshape(targets, capacity, size_z),
            ("gy", "gz"),
            split_axis=0,
            concat_axis=0,
            tiled=True,
        ),
        lax.all_to_all(
            send_columns.reshape(targets, capacity),
            ("gy", "gz"),
            split_axis=0,
            concat_axis=0,
            tiled=True,
        ),
    )
    added = (
        jnp.zeros((columns, size_z), jnp.float32)
        .at[got_columns.reshape(-1)]
        .add(got_rows.reshape(-1, size_z).astype(jnp.float32))
    )
    return 1.0 + added


def residual_inner(residual, preconditioned):
    return lax.psum(jnp.sum(residual * preconditioned), ("gx", "gy", "gz"))


def shards(right_side, coarse_inverse, sphere_rows, margin_block, margin_column):
    size_x, size_y, size_z = right_side.shape
    density = gather_density(
        sphere_rows, margin_block, margin_column, size_x * size_y, size_z
    ).reshape(size_x, size_y, size_z)
    padded = with_halo(density, (("gx", 0), ("gy", 1), ("gz", 2)), 1)
    faces = face_terms(density, padded)
    diagonal = faces[0] + faces[1] + faces[2] + faces[3] + faces[4] + faces[5]

    def precondition(residual):
        return chebyshev(residual, faces, diagonal) + coarse_part(residual, coarse_inverse)

    residual = right_side
    preconditioned = precondition(residual)
    direction = preconditioned
    gamma = residual_inner(residual, preconditioned)
    image = apply_operator(direction, faces, diagonal)
    alpha = gamma / lax.psum(jnp.sum(direction * image), ("gx", "gy", "gz"))
    pressure = alpha * direction
    residual = residual - alpha * image
    preconditioned = precondition(residual)
    return (pressure, preconditioned)


def solution(mesh):
    placed = (
        P("gx", "gy", "gz"),
        P(("gx", "gy", "gz"), None),
        P(("gx", "gy", "gz"), None),
        P(("gx", "gy", "gz"), None),
        P(("gx", "gy", "gz")),
    )
    return jax.shard_map(
        shards,
        mesh=mesh,
        in_specs=placed,
        out_specs=(P("gx", "gy", "gz"), P("gx", "gy", "gz")),
        check_vma=False,
    )
```

profile of v0, /device:TPU:0, one launch (start us, length us, event | category | flops | bytes accessed | tf_op | source)
XLA Modules:
  0.0 382.2 jit_solution(14687189784968215387)
XLA Ops:
  4.5 7.4 %all-to-all-start = ((s32[16,1,6]{2,1,0:T(1,128)}), s32[16,1,6]{2,1,0:T(1,128)S(1)}, u32[]{:S(2)}, u32[]{:S(2)}) async-start(s32[16,1,6]{2,1,0:T(1,128)} %bitcast.3), calls=%async_computation | async-start | bytes 16384 | tf_op jit(solution)/shard_map/all_to_all | solution.py:101
  13.5 4.8 %all-to-all-done = s32[16,1,6]{2,1,0:T(1,128)S(1)} async-done(((s32[16,1,6]{2,1,0:T(1,128)}), s32[16,1,6]{2,1,0:T(1,128)S(1)}, u32[]{:S(2)}, u32[]{:S(2)}) %all-to-all-start) | async-done | bytes 416 | tf_op jit(solution)/shard_map/all_to_all | solution.py:101
  18.3 3.5 all-to-all-start.1
  23.1 5.3 %all-to-all-done.1 = bf16[16,6,128]{2,1,0:T(8,128)(2,1)S(1)} async-done(((bf16[16,6,128]{2,1,0:T(8,128)(2,1)}), bf16[16,6,128]{2,1,0:T(8,128)(2,1)S(1)}, u32[]{:S(2)}, u32[]{:S(2)}) %all-to-all-start.1) | async-done | bytes 24608 | tf_op jit(solution)/shard_map/all_to_all | solution.py:94
  30.9 4.5 %collective-permute-start = (f32[1,64,128]{2,1,0:T(8,128)S(1)}, f32[1,64,128]{2,1,0:T(8,128)S(1)}, u32[]{:S(2)}, u32[]{:S(2)}) collective-permute-start(f32[1,64,128]{2,1,0:T(8,128)S(1)} %get-tuple-element.37), channel_id=1, source_target_pairs={{0,16},{1,17},{2,18},{3,19},{4,20},{5,21},{6,22},{7,23},{8,24},{9,... | collective-permute-start | bytes 98312 | tf_op jit(solution)/shard_map/ppermute | solution.py:17
  35.5 1.6 collective-permute-done
  38.4 4.5 %collective-permute-start.2 = (f32[34,1,128]{2,1,0:T(1,128)S(1)}, f32[34,1,128]{2,1,0:T(1,128)S(1)}, u32[]{:S(2)}, u32[]{:S(2)}) collective-permute-start(f32[34,1,128]{2,1,0:T(1,128)S(1)} %get-tuple-element.29), channel_id=1, source_target_pairs={{0,4},{4,8},{8,12},{1,5},{5,9},{9,13},{2,6},{6,10},{10,14},{3,7},{... | collective-permute-start | bytes 52232 | tf_op jit(solution)/shard_map/ppermute | solution.py:17
  45.9 1.8 copy.19
  49.6 3.2 collective-permute-start.4
  52.8 1.6 copy.20
  54.3 1.6 copy.18
  55.9 5.7 %broadcast_multiply_fusion.2 = (f32[32,64,128]{2,1,0:T(8,128)S(1)}, f32[32,64,128]{2,1,0:T(8,128)}, f32[32,64,128]{2,1,0:T(8,128)}) fusion(f32[32,64,128]{2,1,0:T(8,128)S(1)} %copy-done.1, f32[32,64,128]{2,1,0:T(8,128)S(1)} %bitcast.37, f32[1,64,128]{2,1,0:T(8,128)S(1)} %collective-permute-done, f32[1,64,128]{2,1,0:T(8,128)S(1)} %collective-permute-done.1, ...), kind=kLoop, calls=%fused_computation.147 | loop fusion | flops 9699328 | bytes 5361184 | tf_op jit(solution)/shard_map/div | solution.py:47
  61.7 4.2 %collective-permute-start.6 = (f32[1,64,128]{2,1,0:T(8,128)S(1)}, f32[1,64,128]{2,1,0:T(8,128)S(1)}, u32[]{:S(2)}, u32[]{:S(2)}) collective-permute-start(f32[1,64,128]{2,1,0:T(8,128)S(1)} %get-tuple-element.34), channel_id=1, source_target_pairs={{0,16},{1,17},{2,18},{3,19},{4,20},{5,21},{6,22},{7,23},{8,24},{9,... | collective-permute-start | bytes 98312 | tf_op jit(solution)/shard_map/ppermute | solution.py:17
  67.9 42.1 %all-reduce = f32[256]{0:T(256)S(1)} all-reduce(f32[256]{0:T(256)S(1)} %dynamic-update-slice), channel_id=1, replica_groups=mesh['gx'=2,'gy'=4,'gz'=4] {'gx','gy','gz'}, use_global_device_ids=true, to_apply=%add | all-reduce | flops 256 | bytes 2048
  110.1 1.8 collective-permute-start.8
  113.4 4.2 %collective-permute-done.9 = f32[34,1,128]{2,1,0:T(1,128)S(1)} collective-permute-done((f32[34,1,128]{2,1,0:T(1,128)S(1)}, f32[34,1,128]{2,1,0:T(1,128)S(1)}, u32[]{:S(2)}, u32[]{:S(2)}) %collective-permute-start.9) | collective-permute-done | bytes 17440 | tf_op jit(solution)/shard_map/ppermute | solution.py:18
  118.2 1.8 fusion.75
  120.0 2.5 copy.21
  125.0 3.0 collective-permute-start.10
  128.1 39.8 %all-reduce.2 = f32[256]{0:T(256)S(1)} all-reduce(f32[256]{0:T(256)S(1)} %bitcast.44), channel_id=2, replica_groups=mesh['gx'=2,'gy'=4,'gz'=4] {'gx','gy','gz'}, use_global_device_ids=true, to_apply=%region_7.8.clone | all-reduce | flops 256 | bytes 2048
  168.2 1.6 copy.22
  169.7 1.6 copy.24
  171.3 9.5 %fusion.58 = f32[32,64,128]{2,1,0:T(8,128)S(1)} fusion(f32[32,64,128]{2,1,0:T(8,128)} %copy-done.6, f32[32,64,128]{2,1,0:T(8,128)S(1)} %copy-done.1, f32[32,64,128]{2,1,0:T(8,128)} %get-tuple-element.13, f32[34,66,1]{2,1,0:T(8,128)} %copy.24, f32[34,1,128]{2,1,0:T(1,128)S(1)} %copy-done.11, f32[1,64,128]{2,1,0:T(8,128)S(1)} %collective-permute-done.7, ...), kind=kLoop, calls=%fused_computation.143 | loop fusion | flops 15728640 | bytes 6510624 | tf_op jit(solution)/shard_map/add | solution.py:131
  180.8 4.2 %collective-permute-start.12 = (f32[1,64,128]{2,1,0:T(8,128)S(1)}, f32[1,64,128]{2,1,0:T(8,128)S(1)}, u32[]{:S(2)}, u32[]{:S(2)}) collective-permute-start(f32[1,64,128]{2,1,0:T(8,128)S(1)} %get-tuple-element.32), channel_id=1, source_target_pairs={{0,16},{1,17},{2,18},{3,19},{4,20},{5,21},{6,22},{7,23},{8,24},{9,... | collective-permute-start | bytes 98312 | tf_op jit(solution)/shard_map/ppermute | solution.py:17
  185.0 1.5 collective-permute-start.13
  186.6 4.2 %collective-permute-done.13 = f32[1,64,128]{2,1,0:T(8,128)S(1)} collective-permute-done((f32[1,64,128]{2,1,0:T(8,128)S(1)}, f32[1,64,128]{2,1,0:T(8,128)S(1)}, u32[]{:S(2)}, u32[]{:S(2)}) %collective-permute-start.13) | collective-permute-done | bytes 32800 | tf_op jit(solution)/shard_map/ppermute | solution.py:18
  190.9 2.5 collective-permute-start.14
  194.8 4.2 %collective-permute-done.15 = f32[34,1,128]{2,1,0:T(1,128)S(1)} collective-permute-done((f32[34,1,128]{2,1,0:T(1,128)S(1)}, f32[34,1,128]{2,1,0:T(1,128)S(1)}, u32[]{:S(2)}, u32[]{:S(2)}) %collective-permute-start.15) | collective-permute-done | bytes 17440 | tf_op jit(solution)/shard_map/ppermute | solution.py:18
  199.2 1.8 fusion.74
  201.0 1.8 copy.25
  204.1 1.8 copy.27
  207.3 1.6 copy.26
  208.8 2.0 collective-permute-done.17
  210.8 1.6 copy.28
  212.4 7.7 %multiply_reduce_fusion = (f32[]{:T(128)}, f32[]{:T(128)}, f32[32,64,128]{2,1,0:T(8,128)}) fusion(f32[32,64,128]{2,1,0:T(8,128)S(1)} %fusion.58, f32[32,64,128]{2,1,0:T(8,128)S(1)} %copy-done.1, f32[32,64,128]{2,1,0:T(8,128)} %get-tuple-element.13, f32[34,66,1]{2,1,0:T(8,128)} %copy.28, f32[34,1,128]{2,1,0:T(1,128)S(1)} %collective-permute-done.15, ...), kind=kLoop, calls=%fused_computation.140 | loop fusion | flops 14680062 | bytes 6510120 | tf_op jit(solution)/shard_map/reduce_sum | solution.py:138
  220.1 40.0 %all-reduce.4 = (f32[]{:T(128)}, f32[]{:T(128)}) all-reduce(f32[]{:T(128)} %get-tuple-element.5, f32[]{:T(128)} %get-tuple-element.4), channel_id=1, replica_groups=mesh['gx'=2,'gy'=4,'gz'=4] {'gx','gy','gz'}, use_global_device_ids=true, to_apply=%region_9.10 | all-reduce | flops 2 | bytes 16 | tf_op jit(solution)/shard_map/psum | solution.py:118
  261.4 1.7 fusion.69
  264.0 4.2 %collective-permute-start.18 = (f32[1,64,128]{2,1,0:T(8,128)S(1)}, f32[1,64,128]{2,1,0:T(8,128)S(1)}, u32[]{:S(2)}, u32[]{:S(2)}) collective-permute-start(f32[1,64,128]{2,1,0:T(8,128)S(1)} %get-tuple-element.30), channel_id=1, source_target_pairs={{0,16},{1,17},{2,18},{3,19},{4,20},{5,21},{6,22},{7,23},{8,24},{9,... | collective-permute-start | bytes 98312 | tf_op jit(solution)/shard_map/ppermute | solution.py:17
  271.0 41.0 %all-reduce.1 = f32[256]{0:T(256)S(1)} all-reduce(f32[256]{0:T(256)S(1)} %dynamic-update-slice.1), channel_id=1, replica_groups=mesh['gx'=2,'gy'=4,'gz'=4] {'gx','gy','gz'}, use_global_device_ids=true, to_apply=%add.1 | all-reduce | flops 256 | bytes 2048
  312.0 3.4 collective-permute-start.20
  316.8 4.2 %collective-permute-done.21 = f32[34,1,128]{2,1,0:T(1,128)S(1)} collective-permute-done((f32[34,1,128]{2,1,0:T(1,128)S(1)}, f32[34,1,128]{2,1,0:T(1,128)S(1)}, u32[]{:S(2)}, u32[]{:S(2)}) %collective-permute-start.21) | collective-permute-done | bytes 17440 | tf_op jit(solution)/shard_map/ppermute | solution.py:18
  321.2 1.4 fusion.73
  322.6 1.8 copy.29
  326.3 3.0 collective-permute-start.22
  329.5 39.5 %all-reduce.3 = f32[256]{0:T(256)S(1)} all-reduce(f32[256]{0:T(256)S(1)} %bitcast.45), channel_id=3, replica_groups=mesh['gx'=2,'gy'=4,'gz'=4] {'gx','gy','gz'}, use_global_device_ids=true, to_apply=%region_14.15.clone | all-reduce | flops 256 | bytes 2048
  369.2 1.6 copy.30
  370.8 1.6 copy.32
  372.3 9.9 %fusion.59 = f32[32,64,128]{2,1,0:T(8,128)} fusion(f32[32,64,128]{2,1,0:T(8,128)} %copy-done.7, f32[32,64,128]{2,1,0:T(8,128)} %copy-done.8, f32[32,64,128]{2,1,0:T(8,128)S(1)} %copy-done.5, f32[34,66,1]{2,1,0:T(8,128)} %copy.32, f32[34,1,128]{2,1,0:T(1,128)S(1)} %collective-permute-done.21, f32[1,64,128]{2,1,0:T(8,128)S(1)} %collective-permute-done.19, ...), kind=kLoop, calls=%fused_computation.144 | loop fusion | flops 15728640 | bytes 6510624 | tf_op jit(solution)/shard_map/add | solution.py:131
  (105 shorter events, 34.0 us)
Async XLA Ops:
  0.6 112.6 %copy-start = (f32[8,256]{1,0:T(8,128)S(1)}, f32[8,256]{1,0:T(8,128)}, u32[]{:S(2)}) copy-start(f32[8,256]{1,0:T(8,128)} %param.6) | copy-start | bytes 24580
  4.5 13.8 %all-to-all-start = ((s32[16,1,6]{2,1,0:T(1,128)}), s32[16,1,6]{2,1,0:T(1,128)S(1)}, u32[]{:S(2)}, u32[]{:S(2)}) async-start(s32[16,1,6]{2,1,0:T(1,128)} %bitcast.3), calls=%async_computation | async-start | bytes 16384 | tf_op jit(solution)/shard_map/all_to_all | solution.py:101
  18.3 10.1 %all-to-all-start.1 = ((bf16[16,6,128]{2,1,0:T(8,128)(2,1)}), bf16[16,6,128]{2,1,0:T(8,128)(2,1)S(1)}, u32[]{:S(2)}, u32[]{:S(2)}) async-start(bf16[16,6,128]{2,1,0:T(8,128)(2,1)} %reshape.65), calls=%async_computation.1 | async-start | bytes 65536 | tf_op jit(solution)/shard_map/all_to_all | solution.py:94
  29.6 5.9 %collective-permute-start.1 = (f32[1,64,128]{2,1,0:T(8,128)S(1)}, f32[1,64,128]{2,1,0:T(8,128)S(1)}, u32[]{:S(2)}, u32[]{:S(2)}) collective-permute-start(f32[1,64,128]{2,1,0:T(8,128)S(1)} %get-tuple-element.36), channel_id=1, source_target_pairs={{16,0},{17,1},{18,2},{19,3},{20,4},{21,5},{22,6},{23,7},{24,8},{25... | collective-permute-start | bytes 98312 | tf_op jit(solution)/shard_map/ppermute | solution.py:18
  30.9 6.1 %collective-permute-start = (f32[1,64,128]{2,1,0:T(8,128)S(1)}, f32[1,64,128]{2,1,0:T(8,128)S(1)}, u32[]{:S(2)}, u32[]{:S(2)}) collective-permute-start(f32[1,64,128]{2,1,0:T(8,128)S(1)} %get-tuple-element.37), channel_id=1, source_target_pairs={{0,16},{1,17},{2,18},{3,19},{4,20},{5,21},{6,22},{7,23},{8,24},{9,... | collective-permute-start | bytes 98312 | tf_op jit(solution)/shard_map/ppermute | solution.py:17
  37.1 5.9 %collective-permute-start.3 = (f32[34,1,128]{2,1,0:T(1,128)S(1)}, f32[34,1,128]{2,1,0:T(1,128)S(1)}, u32[]{:S(2)}, u32[]{:S(2)}) collective-permute-start(f32[34,1,128]{2,1,0:T(1,128)S(1)} %get-tuple-element.28), channel_id=1, source_target_pairs={{4,0},{8,4},{12,8},{5,1},{9,5},{13,9},{6,2},{10,6},{14,10},{7,3},{... | collective-permute-start | bytes 52232 | tf_op jit(solution)/shard_map/ppermute | solution.py:18
  38.4 6.0 %collective-permute-start.2 = (f32[34,1,128]{2,1,0:T(1,128)S(1)}, f32[34,1,128]{2,1,0:T(1,128)S(1)}, u32[]{:S(2)}, u32[]{:S(2)}) collective-permute-start(f32[34,1,128]{2,1,0:T(1,128)S(1)} %get-tuple-element.29), channel_id=1, source_target_pairs={{0,4},{4,8},{8,12},{1,5},{5,9},{9,13},{2,6},{6,10},{10,14},{3,7},{... | collective-permute-start | bytes 52232 | tf_op jit(solution)/shard_map/ppermute | solution.py:17
  47.7 5.0 %collective-permute-start.5 = (f32[34,66,1]{1,0,2:T(8,128)S(1)}, f32[34,66,1]{1,0,2:T(8,128)S(1)}, u32[]{:S(2)}, u32[]{:S(2)}) collective-permute-start(f32[34,66,1]{1,0,2:T(8,128)S(1)} %copy.19), channel_id=1, source_target_pairs={{1,0},{2,1},{3,2},{5,4},{6,5},{7,6},{9,8},{10,9},{11,10},{13,12},{... | collective-permute-start | bytes 26936 | tf_op jit(solution)/shard_map/ppermute | solution.py:18
  49.6 6.3 %copy-start.1 = (f32[32,64,128]{2,1,0:T(8,128)S(1)}, f32[32,64,128]{2,1,0:T(8,128)}, u32[]{:S(2)}) copy-start(f32[32,64,128]{2,1,0:T(8,128)} %param.5) | copy-start | bytes 3145732
  49.6 4.7 %collective-permute-start.4 = (f32[34,66,1]{1,0,2:T(8,128)S(1)}, f32[34,66,1]{1,0,2:T(8,128)S(1)}, u32[]{:S(2)}, u32[]{:S(2)}) collective-permute-start(f32[34,66,1]{1,0,2:T(8,128)S(1)} %copy.17), channel_id=1, source_target_pairs={{0,1},{1,2},{2,3},{4,5},{5,6},{6,7},{8,9},{9,10},{10,11},{12,13},{... | collective-permute-start | bytes 26936 | tf_op jit(solution)/shard_map/ppermute | solution.py:17
  61.6 56.1 %copy-start.6 = (f32[32,64,128]{2,1,0:T(8,128)}, f32[32,64,128]{2,1,0:T(8,128)S(1)}, u32[]{:S(2)}) copy-start(f32[32,64,128]{2,1,0:T(8,128)S(1)} %get-tuple-element.11) | copy-start | bytes 3145732
  61.7 48.4 %collective-permute-start.6 = (f32[1,64,128]{2,1,0:T(8,128)S(1)}, f32[1,64,128]{2,1,0:T(8,128)S(1)}, u32[]{:S(2)}, u32[]{:S(2)}) collective-permute-start(f32[1,64,128]{2,1,0:T(8,128)S(1)} %get-tuple-element.34), channel_id=1, source_target_pairs={{0,16},{1,17},{2,18},{3,19},{4,20},{5,21},{6,22},{7,23},{8,24},{9,... | collective-permute-start | bytes 98312 | tf_op jit(solution)/shard_map/ppermute | solution.py:17
  65.9 44.2 %collective-permute-start.7 = (f32[1,64,128]{2,1,0:T(8,128)S(1)}, f32[1,64,128]{2,1,0:T(8,128)S(1)}, u32[]{:S(2)}, u32[]{:S(2)}) collective-permute-start(f32[1,64,128]{2,1,0:T(8,128)S(1)} %get-tuple-element.35), channel_id=1, source_target_pairs={{16,0},{17,1},{18,2},{19,3},{20,4},{21,5},{22,6},{23,7},{24,8},{25... | collective-permute-start | bytes 98312 | tf_op jit(solution)/shard_map/ppermute | solution.py:18
  110.1 3.3 collective-permute-start.8
  111.9 5.6 %collective-permute-start.9 = (f32[34,1,128]{2,1,0:T(1,128)S(1)}, f32[34,1,128]{2,1,0:T(1,128)S(1)}, u32[]{:S(2)}, u32[]{:S(2)}) collective-permute-start(f32[34,1,128]{2,1,0:T(1,128)S(1)} %get-tuple-element.27), channel_id=1, source_target_pairs={{4,0},{8,4},{12,8},{5,1},{9,5},{13,9},{6,2},{10,6},{14,10},{7,3},{... | collective-permute-start | bytes 52232 | tf_op jit(solution)/shard_map/ppermute | solution.py:18
  117.6 0.6 copy-start.10
  120.0 2.5 copy-start.9
  123.7 46.1 %collective-permute-start.11 = (f32[34,66,1]{1,0,2:T(8,128)}, f32[34,66,1]{1,0,2:T(8,128)S(1)}, u32[]{:S(2)}, u32[]{:S(2)}) collective-permute-start(f32[34,66,1]{1,0,2:T(8,128)} %copy.23), channel_id=1, source_target_pairs={{1,0},{2,1},{3,2},{5,4},{6,5},{7,6},{9,8},{10,9},{11,10},{13,12},{... | collective-permute-start | bytes 26936 | tf_op jit(solution)/shard_map/ppermute | solution.py:18
  125.0 43.2 %collective-permute-start.10 = (f32[34,66,1]{1,0,2:T(8,128)}, f32[34,66,1]{1,0,2:T(8,128)S(1)}, u32[]{:S(2)}, u32[]{:S(2)}) collective-permute-start(f32[34,66,1]{1,0,2:T(8,128)} %copy.21), channel_id=1, source_target_pairs={{0,1},{1,2},{2,3},{4,5},{5,6},{6,7},{8,9},{9,10},{10,11},{12,13},{... | collective-permute-start | bytes 26936 | tf_op jit(solution)/shard_map/ppermute | solution.py:17
  168.2 3.1 copy-start.11
  180.8 5.8 %collective-permute-start.12 = (f32[1,64,128]{2,1,0:T(8,128)S(1)}, f32[1,64,128]{2,1,0:T(8,128)S(1)}, u32[]{:S(2)}, u32[]{:S(2)}) collective-permute-start(f32[1,64,128]{2,1,0:T(8,128)S(1)} %get-tuple-element.32), channel_id=1, source_target_pairs={{0,16},{1,17},{2,18},{3,19},{4,20},{5,21},{6,22},{7,23},{8,24},{9,... | collective-permute-start | bytes 98312 | tf_op jit(solution)/shard_map/ppermute | solution.py:17
  185.0 5.8 %collective-permute-start.13 = (f32[1,64,128]{2,1,0:T(8,128)S(1)}, f32[1,64,128]{2,1,0:T(8,128)S(1)}, u32[]{:S(2)}, u32[]{:S(2)}) collective-permute-start(f32[1,64,128]{2,1,0:T(8,128)S(1)} %get-tuple-element.33), channel_id=1, source_target_pairs={{16,0},{17,1},{18,2},{19,3},{20,4},{21,5},{22,6},{23,7},{24,8},{25... | collective-permute-start | bytes 98312 | tf_op jit(solution)/shard_map/ppermute | solution.py:18
  190.9 4.0 %collective-permute-start.14 = (f32[34,1,128]{2,1,0:T(1,128)S(1)}, f32[34,1,128]{2,1,0:T(1,128)S(1)}, u32[]{:S(2)}, u32[]{:S(2)}) collective-permute-start(f32[34,1,128]{2,1,0:T(1,128)S(1)} %get-tuple-element.24), channel_id=1, source_target_pairs={{0,4},{4,8},{8,12},{1,5},{5,9},{9,13},{2,6},{6,10},{10,14},{3,7},{... | collective-permute-start | bytes 52232 | tf_op jit(solution)/shard_map/ppermute | solution.py:17
  193.4 5.6 %collective-permute-start.15 = (f32[34,1,128]{2,1,0:T(1,128)S(1)}, f32[34,1,128]{2,1,0:T(1,128)S(1)}, u32[]{:S(2)}, u32[]{:S(2)}) collective-permute-start(f32[34,1,128]{2,1,0:T(1,128)S(1)} %get-tuple-element.25), channel_id=1, source_target_pairs={{4,0},{8,4},{12,8},{5,1},{9,5},{13,9},{6,2},{10,6},{14,10},{7,3},{... | collective-permute-start | bytes 52232 | tf_op jit(solution)/shard_map/ppermute | solution.py:18
  202.8 4.4 %collective-permute-start.16 = (f32[34,66,1]{1,0,2:T(8,128)S(1)}, f32[34,66,1]{1,0,2:T(8,128)S(1)}, u32[]{:S(2)}, u32[]{:S(2)}) collective-permute-start(f32[34,66,1]{1,0,2:T(8,128)S(1)} %copy.25), channel_id=1, source_target_pairs={{0,1},{1,2},{2,3},{4,5},{5,6},{6,7},{8,9},{9,10},{10,11},{12,13},{... | collective-permute-start | bytes 26936 | tf_op jit(solution)/shard_map/ppermute | solution.py:17
  205.9 4.9 %collective-permute-start.17 = (f32[34,66,1]{1,0,2:T(8,128)S(1)}, f32[34,66,1]{1,0,2:T(8,128)S(1)}, u32[]{:S(2)}, u32[]{:S(2)}) collective-permute-start(f32[34,66,1]{1,0,2:T(8,128)S(1)} %copy.27), channel_id=1, source_target_pairs={{1,0},{2,1},{3,2},{5,4},{6,5},{7,6},{9,8},{10,9},{11,10},{13,12},{... | collective-permute-start | bytes 26936 | tf_op jit(solution)/shard_map/ppermute | solution.py:18
  261.3 1.7 copy-start.2
  261.4 1.8 copy-start.4
  263.0 1.0 copy-start.8
  264.0 57.0 %copy-start.7 = (f32[32,64,128]{2,1,0:T(8,128)}, f32[32,64,128]{2,1,0:T(8,128)S(1)}, u32[]{:S(2)}) copy-start(f32[32,64,128]{2,1,0:T(8,128)S(1)} %broadcast_multiply_fusion.1) | copy-start | bytes 3145732
  264.0 48.0 %collective-permute-start.18 = (f32[1,64,128]{2,1,0:T(8,128)S(1)}, f32[1,64,128]{2,1,0:T(8,128)S(1)}, u32[]{:S(2)}, u32[]{:S(2)}) collective-permute-start(f32[1,64,128]{2,1,0:T(8,128)S(1)} %get-tuple-element.30), channel_id=1, source_target_pairs={{0,16},{1,17},{2,18},{3,19},{4,20},{5,21},{6,22},{7,23},{8,24},{9,... | collective-permute-start | bytes 98312 | tf_op jit(solution)/shard_map/ppermute | solution.py:17
  268.2 43.8 %collective-permute-start.19 = (f32[1,64,128]{2,1,0:T(8,128)S(1)}, f32[1,64,128]{2,1,0:T(8,128)S(1)}, u32[]{:S(2)}, u32[]{:S(2)}) collective-permute-start(f32[1,64,128]{2,1,0:T(8,128)S(1)} %get-tuple-element.31), channel_id=1, source_target_pairs={{16,0},{17,1},{18,2},{19,3},{20,4},{21,5},{22,6},{23,7},{24,8},{25... | collective-permute-start | bytes 98312 | tf_op jit(solution)/shard_map/ppermute | solution.py:18
  312.0 4.8 %collective-permute-start.20 = (f32[34,1,128]{2,1,0:T(1,128)S(1)}, f32[34,1,128]{2,1,0:T(1,128)S(1)}, u32[]{:S(2)}, u32[]{:S(2)}) collective-permute-start(f32[34,1,128]{2,1,0:T(1,128)S(1)} %get-tuple-element.22), channel_id=1, source_target_pairs={{0,4},{4,8},{8,12},{1,5},{5,9},{9,13},{2,6},{6,10},{10,14},{3,7},{... | collective-permute-start | bytes 52232 | tf_op jit(solution)/shard_map/ppermute | solution.py:17
  315.4 5.6 %collective-permute-start.21 = (f32[34,1,128]{2,1,0:T(1,128)S(1)}, f32[34,1,128]{2,1,0:T(1,128)S(1)}, u32[]{:S(2)}, u32[]{:S(2)}) collective-permute-start(f32[34,1,128]{2,1,0:T(1,128)S(1)} %get-tuple-element.23), channel_id=1, source_target_pairs={{4,0},{8,4},{12,8},{5,1},{9,5},{13,9},{6,2},{10,6},{14,10},{7,3},{... | collective-permute-start | bytes 52232 | tf_op jit(solution)/shard_map/ppermute | solution.py:18
  325.0 45.8 %collective-permute-start.23 = (f32[34,66,1]{1,0,2:T(8,128)S(1)}, f32[34,66,1]{1,0,2:T(8,128)S(1)}, u32[]{:S(2)}, u32[]{:S(2)}) collective-permute-start(f32[34,66,1]{1,0,2:T(8,128)S(1)} %copy.31), channel_id=1, source_target_pairs={{1,0},{2,1},{3,2},{5,4},{6,5},{7,6},{9,8},{10,9},{11,10},{13,12},{... | collective-permute-start | bytes 26936 | tf_op jit(solution)/shard_map/ppermute | solution.py:18
  326.3 42.9 %collective-permute-start.22 = (f32[34,66,1]{1,0,2:T(8,128)S(1)}, f32[34,66,1]{1,0,2:T(8,128)S(1)}, u32[]{:S(2)}, u32[]{:S(2)}) collective-permute-start(f32[34,66,1]{1,0,2:T(8,128)S(1)} %copy.29), channel_id=1, source_target_pairs={{0,1},{1,2},{2,3},{4,5},{5,6},{6,7},{8,9},{9,10},{10,11},{12,13},{... | collective-permute-start | bytes 26936 | tf_op jit(solution)/shard_map/ppermute | solution.py:17
  369.2 3.2 copy-start.3
  369.2 3.2 copy-start.5
where the time goes:
time: 384 us; the launch traced here: 382 us
  blocking collectives  202 us (53%)
  starting transfers between devices  66.5 us (17%)
  other arithmetic  41.7 us (11%)
  local copies, waits for them, and re-layouts  36.6 us (10%)
  waiting for transfers between devices  32.2 us (8%)
    unnamed x4, blocking collectives  162 us
    psum x1, blocking collectives, residual_inner(): return lax.psum(jnp.sum(residual * preconditioned), ('gx', 'gy', 'gz'))  40 us
    ppermute x12, starting transfers between devices, with_halo(): before = lax.ppermute(last, axis, up)  39.9 us
    add x2, other arithmetic, precondition(): chebyshev(residual, faces, diagonal) + coarse_part(residual, coarse_inverse)  19.4 us
    ppermute x12, waiting for transfers between devices, with_halo(): after = lax.ppermute(initial, axis, down)  18.9 us
    ppermute x12, starting transfers between devices, with_halo(): after = lax.ppermute(initial, axis, down)  15.7 us
    slice x10, local copies, waits for them, and re-layouts, with_halo(): last = lax.slice_in_dim(value, length - width, length, axis=dim)  11.8 us
    reduce_sum x1, other arithmetic, shards(): alpha = gamma / lax.psum(jnp.sum(direction * image), ('gx', 'gy', 'gz'))  7.72 us
  transfers between devices with their start and end apart: 26, of which 11 were waited for; matrix products, arithmetic and copies ran while one was open for 4% of the time, Pallas kernels for 0%

commit v1 on v0

--- a/solution.py
+++ b/solution.py
@@ -54,23 +54,54 @@
     return result
 
 
-def coarse_part(residual, coarse_inverse):
+def doubling_steps():
+    steps = []
+    for axis in ("gy", "gx", "gz"):
+        size = lax.axis_size(axis)
+        stride = 1
+        while stride < size:
+            steps.append((axis, stride))
+            stride *= 2
+    return steps
+
+
+def gather_all(value):
+    sizes = {axis: lax.axis_size(axis) for axis in ("gx", "gy", "gz")}
+    value = value[None]
+    for axis in ("gy", "gx", "gz"):
+        size, stride = (sizes[axis], 1)
+        index = lax.axis_index(axis)
+        value = value[None]
+        while stride < size:
+            other = lax.ppermute(value, axis, [(i, i ^ stride) for i in range(size)])
+            upper = (index // stride) % 2
+            value = jnp.where(
+                upper == 1,
+                jnp.concatenate([other, value], axis=0),
+                jnp.concatenate([value, other], axis=0),
+            )
+            stride *= 2
+        value = value.reshape((-1,) + value.shape[2:]) if axis == "gy" else value
+    value = value.reshape((sizes["gz"], sizes["gx"], sizes["gy"]) + value.shape[3:])
+    value = jnp.moveaxis(value, 0, 2)
+    return value.reshape((-1,) + value.shape[3:])
+
+
+def sum_all(value):
+    for axis, stride in doubling_steps():
+        size = lax.axis_size(axis)
+        value = value + lax.ppermute(value, axis, [(i, i ^ stride) for i in range(size)])
+    return value
+
+
+def coarse_part(residual, whole_inverse, slabs):
     size_x, size_y, size_z = residual.shape
-    slabs = coarse_inverse.shape[0]
     local_sums = jnp.sum(residual.reshape(size_x, size_y, slabs, size_z // slabs), axis=(0, 1, 3))
-    block = coarse_inverse
-    inner = jnp.dot(
-        block,
-        lax.all_gather(local_sums, ("gx", "gy", "gz"), axis=0, tiled=True),
-        precision=lax.Precision.HIGHEST,
-    )
-    block = coarse_inverse
-    coarse_values = lax.psum_scatter(
-        jnp.dot(inner, block, precision=lax.Precision.HIGHEST),
-        ("gx", "gy", "gz"),
-        scatter_dimension=0,
-        tiled=True,
-    )
+    sums = gather_all(jnp.broadcast_to(local_sums[:, None], (slabs, 128)))[:, :, 0].reshape(-1)
+    inner = jnp.dot(whole_inverse, sums, precision=lax.Precision.HIGHEST)
+    place = (lax.axis_index("gx") * lax.axis_size("gy") + lax.axis_index("gy")) * lax.axis_size("gz") + lax.axis_index("gz")
+    own = lax.dynamic_slice_in_dim(whole_inverse, place * slabs, slabs, axis=1)
+    coarse_values = jnp.dot(inner, own, precision=lax.Precision.HIGHEST)
     spread_out = jnp.broadcast_to(
         coarse_values.reshape(1, 1, slabs, 1), (size_x, size_y, slabs, size_z // slabs)
     )
@@ -114,10 +145,6 @@
     return 1.0 + added
 
 
-def residual_inner(residual, preconditioned):
-    return lax.psum(jnp.sum(residual * preconditioned), ("gx", "gy", "gz"))
-
-
 def shards(right_side, coarse_inverse, sphere_rows, margin_block, margin_column):
     size_x, size_y, size_z = right_side.shape
     density = gather_density(
@@ -127,15 +154,19 @@
     faces = face_terms(density, padded)
     diagonal = faces[0] + faces[1] + faces[2] + faces[3] + faces[4] + faces[5]
 
+    slabs = coarse_inverse.shape[0]
+    whole_inverse = gather_all(coarse_inverse).reshape(-1, coarse_inverse.shape[1])
+
     def precondition(residual):
-        return chebyshev(residual, faces, diagonal) + coarse_part(residual, coarse_inverse)
+        return chebyshev(residual, faces, diagonal) + coarse_part(residual, whole_inverse, slabs)
 
     residual = right_side
     preconditioned = precondition(residual)
     direction = preconditioned
-    gamma = residual_inner(residual, preconditioned)
     image = apply_operator(direction, faces, diagonal)
-    alpha = gamma / lax.psum(jnp.sum(direction * image), ("gx", "gy", "gz"))
+    both = jnp.stack([jnp.sum(residual * preconditioned), jnp.sum(direction * image)])
+    both = sum_all(jnp.broadcast_to(both[:, None], (2, 128)))
+    alpha = both[0, 0] / both[1, 0]
     pressure = alpha * direction
     residual = residual - alpha * image
     preconditioned = precondition(residual)

time: 384 us -> 238 us (0.62)
  blocking collectives: 202 us -> 0 us
  starting transfers between devices: 66.5 us -> 85.7 us
  waiting for transfers between devices: 32.2 us -> 49.7 us
  other arithmetic: 41.7 us -> 54.1 us
  local copies, waits for them, and re-layouts: 36.6 us -> 42.6 us
    unnamed x4 -> x0, blocking collectives: 162 us -> none
    psum x1 -> x0, blocking collectives: 40 us -> none  [residual_inner(): return lax.psum(jnp.sum(residual * preconditioned), ('gx', 'gy', 'gz'))]
    ppermute x0 -> x20, starting transfers between devices: none -> 22.1 us  [the longest x15 18.6 us: gather_all(): other = lax.ppermute(value, axis, [(i, i ^ stride) for i in range(size)])]
    ppermute x0 -> x20, waiting for transfers between devices: none -> 21.2 us  [the longest x5 13.8 us: sum_all(): lax.ppermute(value, axis, [(i, i ^ stride) for i in range(size)])]
    select_n x0 -> x14, other arithmetic: none -> 7.74 us  [gather_all(): jnp.where(upper == 1, jnp.concatenate([other, value], axis=0), jnp.concat...]
    all_to_all x1, waiting for transfers between devices: 5.31 us -> 0.01 us  [gather_density(): lax.all_to_all(send_rows.reshape(targets, capacity, size_z), ('gy', 'gz')...]
    add x2 -> x7, other arithmetic: 19.4 us -> 20.1 us  [the longest x2 20 us: precondition(): chebyshev(residual, faces, diagonal)]
  transfers between devices with their start and end apart: 26 -> 46, of which waited for: 11 -> 19; matrix products, arithmetic and copies ran while one was open for 4% -> 22% of each run, Pallas kernels for 0% -> 0%
where the time goes in v1:
time: 238 us; the launch traced here: 236 us
  starting transfers between devices  85.7 us (36%)
  other arithmetic  54.1 us (23%)
  waiting for transfers between devices  49.7 us (21%)
  local copies, waits for them, and re-layouts  42.6 us (18%)
  between operations  2.92 us (1%)
    ppermute x12, starting transfers between devices, with_halo(): before = lax.ppermute(last, axis, up)  38.2 us
    ppermute x12, waiting for transfers between devices, with_halo(): after = lax.ppermute(initial, axis, down)  21.7 us
    add x2, other arithmetic, precondition(): chebyshev(residual, faces, diagonal)  20 us
    ppermute x15, starting transfers between devices, gather_all(): other = lax.ppermute(value, axis, [(i, i ^ stride) for i in range(size)])  18.6 us
    ppermute x12, starting transfers between devices, with_halo(): after = lax.ppermute(initial, axis, down)  15.7 us
    ppermute x5, waiting for transfers between devices, sum_all(): lax.ppermute(value, axis, [(i, i ^ stride) for i in range(size)])  13.8 us
    slice x10, local copies, waits for them, and re-layouts, with_halo(): last = lax.slice_in_dim(value, length - width, length, axis=dim)  12.3 us
    div x2, other arithmetic, chebyshev(): update = residual / diagonal / centre_value  8.18 us
  transfers between devices with their start and end apart: 46, of which 19 were waited for; matrix products, arithmetic and copies ran while one was open for 22% of the time, Pallas kernels for 0%

profile of v1, /device:TPU:0, one launch (start us, length us, event | category | flops | bytes accessed | tf_op | source)
XLA Modules:
  0.0 236.2 jit_solution(5749062305060365961)
XLA Ops:
  2.4 3.1 %collective-permute-start.17 = (f32[1,1,8,128]{3,2,1,0:T(8,128)S(1)}, f32[1,1,8,128]{3,2,1,0:T(8,128)S(1)}, u32[]{:S(2)}, u32[]{:S(2)}) collective-permute-start(f32[1,1,8,128]{3,2,1,0:T(8,128)S(1)} %broadcast_in_dim.51), channel_id=1, source_target_pairs={{0,4},{4,0},{8,12},{12,8},{1,5},{5,1},{9,13},{13,9},{2,6},{6,2},{1... | collective-permute-start | bytes 12296 | tf_op jit(solution)/shard_map/ppermute | solution.py:76
  9.4 6.3 %all-to-all-start = ((s32[16,1,6]{2,1,0:T(1,128)}), s32[16,1,6]{2,1,0:T(1,128)S(1)}, u32[]{:S(2)}, u32[]{:S(2)}) async-start(s32[16,1,6]{2,1,0:T(1,128)} %bitcast.3), calls=%async_computation | async-start | bytes 16384 | tf_op jit(solution)/shard_map/all_to_all | solution.py:132
  17.3 4.8 %all-to-all-done = s32[16,1,6]{2,1,0:T(1,128)S(1)} async-done(((s32[16,1,6]{2,1,0:T(1,128)}), s32[16,1,6]{2,1,0:T(1,128)S(1)}, u32[]{:S(2)}, u32[]{:S(2)}) %all-to-all-start) | async-done | bytes 416 | tf_op jit(solution)/shard_map/all_to_all | solution.py:132
  22.1 3.5 %all-to-all-start.1 = ((bf16[16,6,128]{2,1,0:T(8,128)(2,1)}), bf16[16,6,128]{2,1,0:T(8,128)(2,1)S(1)}, u32[]{:S(2)}, u32[]{:S(2)}) async-start(bf16[16,6,128]{2,1,0:T(8,128)(2,1)} %reshape.930), calls=%async_computation.1 | async-start | bytes 65536 | tf_op jit(solution)/shard_map/all_to_all | solution.py:125
  26.9 2.8 %collective-permute-start.18 = (f32[2,1,8,128]{3,2,1,0:T(8,128)S(1)}, f32[2,1,8,128]{3,2,1,0:T(8,128)S(1)}, u32[]{:S(2)}, u32[]{:S(2)}) collective-permute-start(f32[2,1,8,128]{3,2,1,0:T(8,128)S(1)} %maximum_select_fusion.14), channel_id=1, source_target_pairs={{0,8},{4,12},{8,0},{12,4},{1,9},{5,13},{9,1},{13,5},{2,10},{6,14},... | collective-permute-start | bytes 24584 | tf_op jit(solution)/shard_map/ppermute | solution.py:76
  38.6 4.5 %collective-permute-start = (f32[1,64,128]{2,1,0:T(8,128)S(1)}, f32[1,64,128]{2,1,0:T(8,128)S(1)}, u32[]{:S(2)}, u32[]{:S(2)}) collective-permute-start(f32[1,64,128]{2,1,0:T(8,128)S(1)} %get-tuple-element.35), channel_id=1, source_target_pairs={{0,16},{1,17},{2,18},{3,19},{4,20},{5,21},{6,22},{7,23},{8,24},{9,... | collective-permute-start | bytes 98312 | tf_op jit(solution)/shard_map/ppermute | solution.py:17
  46.1 4.5 %collective-permute-start.2 = (f32[34,1,128]{2,1,0:T(1,128)S(1)}, f32[34,1,128]{2,1,0:T(1,128)S(1)}, u32[]{:S(2)}, u32[]{:S(2)}) collective-permute-start(f32[34,1,128]{2,1,0:T(1,128)S(1)} %get-tuple-element.27), channel_id=1, source_target_pairs={{0,4},{4,8},{8,12},{1,5},{5,9},{9,13},{2,6},{6,10},{10,14},{3,7},{... | collective-permute-start | bytes 52232 | tf_op jit(solution)/shard_map/ppermute | solution.py:17
  54.9 2.2 collective-permute-start.4
  60.0 3.5 %collective-permute-start.21 = (f32[2,2,4,8,128]{4,3,0,2,1:T(8,128)}, f32[2,2,4,8,128]{4,3,0,2,1:T(8,128)}, u32[]{:S(2)}, u32[]{:S(2)}) collective-permute-start(f32[2,2,4,8,128]{4,3,0,2,1:T(8,128)} %maximum_select_fusion.5), channel_id=1, source_target_pairs={{0,2},{1,3},{2,0},{3,1},{4,6},{5,7},{6,4},{7,5},{8,10},{9,11},{10,... | collective-permute-start | bytes 196616 | tf_op jit(solution)/shard_map/ppermute | solution.py:76
  65.6 5.6 %broadcast_multiply_fusion.2 = (f32[32,64,128]{2,1,0:T(8,128)S(1)}, f32[32,64,128]{2,1,0:T(8,128)}, f32[32,64,128]{2,1,0:T(8,128)}) fusion(f32[32,64,128]{2,1,0:T(8,128)S(1)} %copy-done, f32[32,64,128]{2,1,0:T(8,128)S(1)} %bitcast.69, f32[1,64,128]{2,1,0:T(8,128)S(1)} %copy-done.8, f32[1,64,128]{2,1,0:T(8,128)S(1)} %copy-done.6, ...), kind=kLoop, calls=%fused_computation.149 | loop fusion | flops 9699328 | bytes 5361184 | tf_op jit(solution)/shard_map/div | solution.py:47
  71.2 4.2 %collective-permute-start.6 = (f32[1,64,128]{2,1,0:T(8,128)S(1)}, f32[1,64,128]{2,1,0:T(8,128)S(1)}, u32[]{:S(2)}, u32[]{:S(2)}) collective-permute-start(f32[1,64,128]{2,1,0:T(8,128)S(1)} %get-tuple-element.32), channel_id=1, source_target_pairs={{0,16},{1,17},{2,18},{3,19},{4,20},{5,21},{6,22},{7,23},{8,24},{9,... | collective-permute-start | bytes 98312 | tf_op jit(solution)/shard_map/ppermute | solution.py:17
  76.7 1.6 maximum_select_fusion.1
  78.4 2.9 %collective-permute-done.7 = f32[1,64,128]{2,1,0:T(8,128)S(1)} collective-permute-done((f32[1,64,128]{2,1,0:T(8,128)S(1)}, f32[1,64,128]{2,1,0:T(8,128)S(1)}, u32[]{:S(2)}, u32[]{:S(2)}) %collective-permute-start.7) | collective-permute-done | bytes 32800 | tf_op jit(solution)/shard_map/ppermute | solution.py:18
  81.3 4.2 %collective-permute-start.8 = (f32[34,1,128]{2,1,0:T(1,128)S(1)}, f32[34,1,128]{2,1,0:T(1,128)S(1)}, u32[]{:S(2)}, u32[]{:S(2)}) collective-permute-start(f32[34,1,128]{2,1,0:T(1,128)S(1)} %get-tuple-element.24), channel_id=1, source_target_pairs={{0,4},{4,8},{8,12},{1,5},{5,9},{9,13},{2,6},{6,10},{10,14},{3,7},{... | collective-permute-start | bytes 52232 | tf_op jit(solution)/shard_map/ppermute | solution.py:17
  86.8 1.6 maximum_select_fusion.2
  88.4 2.7 %collective-permute-done.9 = f32[34,1,128]{2,1,0:T(1,128)S(1)} collective-permute-done((f32[34,1,128]{2,1,0:T(1,128)S(1)}, f32[34,1,128]{2,1,0:T(1,128)S(1)}, u32[]{:S(2)}, u32[]{:S(2)}) %collective-permute-start.9) | collective-permute-done | bytes 17440 | tf_op jit(solution)/shard_map/ppermute | solution.py:18
  93.3 2.4 %copy.29 = f32[34,66,1]{1,0,2:T(8,128)} copy(f32[34,66,1]{2,1,0:T(8,128)} %get-tuple-element.16) | data formatting | bytes 17952 | tf_op jit(solution)/shard_map/slice | solution.py:15
  97.6 3.0 %collective-permute-start.10 = (f32[34,66,1]{1,0,2:T(8,128)}, f32[34,66,1]{1,0,2:T(8,128)S(1)}, u32[]{:S(2)}, u32[]{:S(2)}) collective-permute-start(f32[34,66,1]{1,0,2:T(8,128)} %copy.29), channel_id=1, source_target_pairs={{0,1},{1,2},{2,3},{4,5},{5,6},{6,7},{8,9},{9,10},{10,11},{12,13},{... | collective-permute-start | bytes 26936 | tf_op jit(solution)/shard_map/ppermute | solution.py:17
  106.7 9.8 %fusion.58 = f32[32,64,128]{2,1,0:T(8,128)S(1)} fusion(f32[32,64,128]{2,1,0:T(8,128)} %copy-done.4, f32[32,64,128]{2,1,0:T(8,128)S(1)} %copy-done, f32[32,64,128]{2,1,0:T(8,128)} %get-tuple-element.11, f32[34,66,1]{2,1,0:T(8,128)} %copy.32, f32[34,1,128]{2,1,0:T(1,128)} %copy-done.19, f32[1,64,128]{2,1,0:T(8,128)} %copy-done.14, ...), kind=kLoop, calls=%fused_computation.145 | loop fusion | flops 15728640 | bytes 6510624 | tf_op jit(solution)/shard_map/add | solution.py:161
  116.5 1.7 collective-permute-start.22
  119.8 4.4 %collective-permute-done.23 = f32[1,64,128]{2,1,0:T(8,128)S(1)} collective-permute-done((f32[1,64,128]{2,1,0:T(8,128)S(1)}, f32[1,64,128]{2,1,0:T(8,128)S(1)}, u32[]{:S(2)}, u32[]{:S(2)}) %collective-permute-start.23) | collective-permute-done | bytes 32800 | tf_op jit(solution)/shard_map/ppermute | solution.py:18
  124.2 3.5 %collective-permute-start.24 = (f32[34,1,128]{2,1,0:T(1,128)S(1)}, f32[34,1,128]{2,1,0:T(1,128)S(1)}, u32[]{:S(2)}, u32[]{:S(2)}) collective-permute-start(f32[34,1,128]{2,1,0:T(1,128)S(1)} %get-tuple-element.22), channel_id=1, source_target_pairs={{0,4},{4,8},{8,12},{1,5},{5,9},{9,13},{2,6},{6,10},{10,14},{3,7},{... | collective-permute-start | bytes 52232 | tf_op jit(solution)/shard_map/ppermute | solution.py:17
  129.2 4.2 %collective-permute-done.25 = f32[34,1,128]{2,1,0:T(1,128)S(1)} collective-permute-done((f32[34,1,128]{2,1,0:T(1,128)S(1)}, f32[34,1,128]{2,1,0:T(1,128)S(1)}, u32[]{:S(2)}, u32[]{:S(2)}) %collective-permute-start.25) | collective-permute-done | bytes 17440 | tf_op jit(solution)/shard_map/ppermute | solution.py:18
  134.1 1.8 fusion.82
  136.0 2.4 %copy.36 = f32[34,66,1]{1,0,2:T(8,128)} copy(f32[34,66,1]{2,1,0:T(8,128)} %get-tuple-element.14) | data formatting | bytes 17952 | tf_op jit(solution)/shard_map/slice | solution.py:15
  138.4 1.9 collective-permute-start.26
  140.2 2.4 %copy.38 = f32[34,66,1]{1,0,2:T(8,128)} copy(f32[34,66,1]{2,1,0:T(8,128)} %get-tuple-element.15) | data formatting | bytes 17952 | tf_op jit(solution)/shard_map/slice | solution.py:16
  144.0 2.3 copy.37
  146.3 3.3 %collective-permute-done.27 = f32[34,66,1]{1,0,2:T(8,128)} collective-permute-done((f32[34,66,1]{1,0,2:T(8,128)}, f32[34,66,1]{1,0,2:T(8,128)}, u32[]{:S(2)}, u32[]{:S(2)}) %collective-permute-start.27) | collective-permute-done | bytes 9008 | tf_op jit(solution)/shard_map/ppermute | solution.py:18
  149.5 2.3 copy.39
  151.8 7.0 %multiply_reduce_fusion.1 = (f32[]{:T(128)}, f32[]{:T(128)}, f32[32,64,128]{2,1,0:T(8,128)S(1)}) fusion(f32[32,64,128]{2,1,0:T(8,128)S(1)} %copy-done, f32[32,64,128]{2,1,0:T(8,128)S(1)} %fusion.58, f32[32,64,128]{2,1,0:T(8,128)} %get-tuple-element.11, f32[34,66,1]{2,1,0:T(8,128)} %copy.39, f32[34,1,128]{2,1,0:T(1,128)} %copy-done.21, ...), kind=kLoop, calls=%fused_computation.143 | loop fusion | flops 14680062 | bytes 6510120 | tf_op jit(solution)/shard_map/reduce_sum | solution.py:167
  160.6 3.0 %collective-permute-done.28 = f32[2,128]{1,0:T(2,128)S(1)} collective-permute-done((f32[2,128]{1,0:T(2,128)S(1)}, f32[2,128]{1,0:T(2,128)S(1)}, u32[]{:S(2)}, u32[]{:S(2)}) %collective-permute-start.28) | collective-permute-done | bytes 1056 | tf_op jit(solution)/shard_map/ppermute | solution.py:93
  163.7 4.5 %collective-permute-done.29 = f32[2,128]{1,0:T(2,128)S(1)} collective-permute-done((f32[2,128]{1,0:T(2,128)S(1)}, f32[2,128]{1,0:T(2,128)S(1)}, u32[]{:S(2)}, u32[]{:S(2)}) %collective-permute-start.29) | collective-permute-done | bytes 1056 | tf_op jit(solution)/shard_map/ppermute | solution.py:93
  168.2 3.6 %collective-permute-done.30 = f32[2,128]{1,0:T(2,128)S(1)} collective-permute-done((f32[2,128]{1,0:T(2,128)S(1)}, f32[2,128]{1,0:T(2,128)S(1)}, u32[]{:S(2)}, u32[]{:S(2)}) %collective-permute-start.30) | collective-permute-done | bytes 1056 | tf_op jit(solution)/shard_map/ppermute | solution.py:93
  173.0 2.9 %collective-permute-start.32 = (f32[2,128]{1,0:T(2,128)S(1)}, f32[2,128]{1,0:T(2,128)S(1)}, u32[]{:S(2)}, u32[]{:S(2)}) collective-permute-start(f32[2,128]{1,0:T(2,128)S(1)} %add.221), channel_id=1, source_target_pairs={{0,2},{1,3},{2,0},{3,1},{4,6},{5,7},{6,4},{7,5},{8,10},{9,11},{10,... | collective-permute-start | bytes 3080 | tf_op jit(solution)/shard_map/ppermute | solution.py:93
  181.5 2.6 %broadcast_multiply_fusion.1 = f32[32,64,128]{2,1,0:T(8,128)S(1)} fusion(f32[32,64,128]{2,1,0:T(8,128)} %get-tuple-element.7, f32[32,64,128]{2,1,0:T(8,128)} %get-tuple-element.11, f32[32,64,128]{2,1,0:T(8,128)} %get-tuple-element.10, f32[32,64,128]{2,1,0:T(8,128)S(1)} %bitcast.72, f32[1,64,128]{2,1,0:T(8,128)S(1)} %copy-done.8, ...), kind=kLoop, calls=%fused_computation.148 | loop fusion | flops 6029312 | bytes 5343232 | tf_op jit(solution)/shard_map/div | solution.py:47
  184.1 1.9 collective-permute-start.33
  187.5 4.5 %collective-permute-done.40 = f32[2,1,8,128]{3,2,1,0:T(8,128)S(1)} collective-permute-done((f32[2,1,8,128]{3,2,1,0:T(8,128)S(1)}, f32[2,1,8,128]{3,2,1,0:T(8,128)S(1)}, u32[]{:S(2)}, u32[]{:S(2)}) %collective-permute-start.40) | collective-permute-done | bytes 8224 | tf_op jit(solution)/shard_map/ppermute | solution.py:76
  192.0 2.6 %collective-permute-start.41 = (f32[1,4,8,128]{3,2,1,0:T(8,128)S(1)}, f32[1,4,8,128]{3,2,1,0:T(8,128)S(1)}, u32[]{:S(2)}, u32[]{:S(2)}) collective-permute-start(f32[1,4,8,128]{3,2,1,0:T(8,128)S(1)} %maximum_select_fusion.13), channel_id=1, source_target_pairs={{0,16},{16,0},{1,17},{17,1},{2,18},{18,2},{3,19},{19,3},{4,20},{20... | collective-permute-start | bytes 49160 | tf_op jit(solution)/shard_map/ppermute | solution.py:76
  194.7 3.4 %collective-permute-start.35 = (f32[34,1,128]{2,1,0:T(1,128)S(1)}, f32[34,1,128]{2,1,0:T(1,128)S(1)}, u32[]{:S(2)}, u32[]{:S(2)}) collective-permute-start(f32[34,1,128]{2,1,0:T(1,128)S(1)} %get-tuple-element.20), channel_id=1, source_target_pairs={{0,4},{4,8},{8,12},{1,5},{5,9},{9,13},{2,6},{6,10},{10,14},{3,7},{... | collective-permute-start | bytes 52232 | tf_op jit(solution)/shard_map/ppermute | solution.py:17
  199.5 4.2 %collective-permute-done.36 = f32[34,1,128]{2,1,0:T(1,128)S(1)} collective-permute-done((f32[34,1,128]{2,1,0:T(1,128)S(1)}, f32[34,1,128]{2,1,0:T(1,128)S(1)}, u32[]{:S(2)}, u32[]{:S(2)}) %collective-permute-start.36) | collective-permute-done | bytes 17440 | tf_op jit(solution)/shard_map/ppermute | solution.py:18
  203.9 1.8 fusion.81
  205.7 1.8 copy.40
  207.5 2.4 %copy.42 = f32[34,66,1]{1,0,2:T(8,128)} copy(f32[34,66,1]{2,1,0:T(8,128)} %get-tuple-element.13) | data formatting | bytes 17952 | tf_op jit(solution)/shard_map/slice | solution.py:16
  211.3 3.0 %collective-permute-start.37 = (f32[34,66,1]{1,0,2:T(8,128)S(1)}, f32[34,66,1]{1,0,2:T(8,128)S(1)}, u32[]{:S(2)}, u32[]{:S(2)}) collective-permute-start(f32[34,66,1]{1,0,2:T(8,128)S(1)} %copy.40), channel_id=1, source_target_pairs={{0,1},{1,2},{2,3},{4,5},{5,6},{6,7},{8,9},{9,10},{10,11},{12,13},{... | collective-permute-start | bytes 26936 | tf_op jit(solution)/shard_map/ppermute | solution.py:17
  214.9 2.6 %collective-permute-start.43 = (f32[2,2,4,8,128]{4,3,2,1,0:T(8,128)}, f32[2,2,4,8,128]{4,3,2,1,0:T(8,128)}, u32[]{:S(2)}, u32[]{:S(2)}) collective-permute-start(f32[2,2,4,8,128]{4,3,2,1,0:T(8,128)} %maximum_select_fusion.6), channel_id=1, source_target_pairs={{0,2},{1,3},{2,0},{3,1},{4,6},{5,7},{6,4},{7,5},{8,10},{9,11},{10,... | collective-permute-start | bytes 196616 | tf_op jit(solution)/shard_map/ppermute | solution.py:76
  220.1 2.4 %copy.43 = f32[34,66,1]{2,1,0:T(8,128)} copy(f32[34,66,1]{1,0,2:T(8,128)} %collective-permute-done.38) | data formatting | bytes 17952 | tf_op jit(solution)/shard_map/ppermute | solution.py:18
  225.8 10.2 %fusion.59 = f32[32,64,128]{2,1,0:T(8,128)} fusion(f32[32,64,128]{2,1,0:T(8,128)} %copy-done.3, f32[32,64,128]{2,1,0:T(8,128)} %get-tuple-element.7, f32[32,64,128]{2,1,0:T(8,128)S(1)} %copy-done.2, f32[34,66,1]{2,1,0:T(8,128)} %copy.43, f32[34,1,128]{2,1,0:T(1,128)} %copy-done.17, f32[1,64,128]{2,1,0:T(8,128)} %copy-done.13, ...), kind=kLoop, calls=%fused_computation.146 | loop fusion | flops 15728640 | bytes 6510624 | tf_op jit(solution)/shard_map/add | solution.py:161
  (193 shorter events, 65.2 us)
Async XLA Ops:
  0.6 29.2 %copy-start.22 = (f32[8,256]{1,0:T(8,128)S(1)}, f32[8,256]{1,0:T(8,128)}, u32[]{:S(2)}) copy-start(f32[8,256]{1,0:T(8,128)} %param.6) | copy-start | bytes 24580
  2.4 24.5 %collective-permute-start.17 = (f32[1,1,8,128]{3,2,1,0:T(8,128)S(1)}, f32[1,1,8,128]{3,2,1,0:T(8,128)S(1)}, u32[]{:S(2)}, u32[]{:S(2)}) collective-permute-start(f32[1,1,8,128]{3,2,1,0:T(8,128)S(1)} %broadcast_in_dim.51), channel_id=1, source_target_pairs={{0,4},{4,0},{8,12},{12,8},{1,5},{5,1},{9,13},{13,9},{2,6},{6,2},{1... | collective-permute-start | bytes 12296 | tf_op jit(solution)/shard_map/ppermute | solution.py:76
  5.5 24.3 %collective-permute-start.12 = (f32[1,1,8,256]{3,2,1,0:T(8,128)}, f32[1,1,8,256]{3,2,1,0:T(8,128)S(1)}, u32[]{:S(2)}, u32[]{:S(2)}) collective-permute-start(f32[1,1,8,256]{3,2,1,0:T(8,128)} %bitcast.84), channel_id=1, source_target_pairs={{0,4},{4,0},{8,12},{12,8},{1,5},{5,1},{9,13},{13,9},{2,6},{6,2},{1... | collective-permute-start | bytes 24584 | tf_op jit(solution)/shard_map/ppermute | solution.py:76
  9.4 12.7 %all-to-all-start = ((s32[16,1,6]{2,1,0:T(1,128)}), s32[16,1,6]{2,1,0:T(1,128)S(1)}, u32[]{:S(2)}, u32[]{:S(2)}) async-start(s32[16,1,6]{2,1,0:T(1,128)} %bitcast.3), calls=%async_computation | async-start | bytes 16384 | tf_op jit(solution)/shard_map/all_to_all | solution.py:132
  22.1 13.9 %all-to-all-start.1 = ((bf16[16,6,128]{2,1,0:T(8,128)(2,1)}), bf16[16,6,128]{2,1,0:T(8,128)(2,1)S(1)}, u32[]{:S(2)}, u32[]{:S(2)}) async-start(bf16[16,6,128]{2,1,0:T(8,128)(2,1)} %reshape.930), calls=%async_computation.1 | async-start | bytes 65536 | tf_op jit(solution)/shard_map/all_to_all | solution.py:125
  26.9 4.6 %collective-permute-start.18 = (f32[2,1,8,128]{3,2,1,0:T(8,128)S(1)}, f32[2,1,8,128]{3,2,1,0:T(8,128)S(1)}, u32[]{:S(2)}, u32[]{:S(2)}) collective-permute-start(f32[2,1,8,128]{3,2,1,0:T(8,128)S(1)} %maximum_select_fusion.14), channel_id=1, source_target_pairs={{0,8},{4,12},{8,0},{12,4},{1,9},{5,13},{9,1},{13,5},{2,10},{6,14},... | collective-permute-start | bytes 24584 | tf_op jit(solution)/shard_map/ppermute | solution.py:76
  29.8 4.7 %collective-permute-start.13 = (f32[2,1,8,256]{3,2,1,0:T(8,128)S(1)}, f32[2,1,8,256]{3,2,1,0:T(8,128)S(1)}, u32[]{:S(2)}, u32[]{:S(2)}) collective-permute-start(f32[2,1,8,256]{3,2,1,0:T(8,128)S(1)} %maximum_select_fusion.10), channel_id=1, source_target_pairs={{0,8},{4,12},{8,0},{12,4},{1,9},{5,13},{9,1},{13,5},{2,10},{6,14},... | collective-permute-start | bytes 49160 | tf_op jit(solution)/shard_map/ppermute | solution.py:76
  31.5 11.7 %collective-permute-start.19 = (f32[1,4,8,128]{3,2,1,0:T(8,128)S(1)}, f32[1,4,8,128]{3,2,1,0:T(8,128)S(1)}, u32[]{:S(2)}, u32[]{:S(2)}) collective-permute-start(f32[1,4,8,128]{3,2,1,0:T(8,128)S(1)} %maximum_select_fusion.12), channel_id=1, source_target_pairs={{0,16},{16,0},{1,17},{17,1},{2,18},{18,2},{3,19},{19,3},{4,20},{20... | collective-permute-start | bytes 49160 | tf_op jit(solution)/shard_map/ppermute | solution.py:76
  34.5 16.1 %collective-permute-start.14 = (f32[1,4,8,256]{3,2,1,0:T(8,128)S(1)}, f32[1,4,8,256]{3,2,1,0:T(8,128)S(1)}, u32[]{:S(2)}, u32[]{:S(2)}) collective-permute-start(f32[1,4,8,256]{3,2,1,0:T(8,128)S(1)} %maximum_select_fusion.7), channel_id=1, source_target_pairs={{0,16},{16,0},{1,17},{17,1},{2,18},{18,2},{3,19},{19,3},{4,20},{20... | collective-permute-start | bytes 98312 | tf_op jit(solution)/shard_map/ppermute | solution.py:76
  37.3 6.5 %collective-permute-start.1 = (f32[1,64,128]{2,1,0:T(8,128)S(1)}, f32[1,64,128]{2,1,0:T(8,128)S(1)}, u32[]{:S(2)}, u32[]{:S(2)}) collective-permute-start(f32[1,64,128]{2,1,0:T(8,128)S(1)} %get-tuple-element.34), channel_id=1, source_target_pairs={{16,0},{17,1},{18,2},{19,3},{20,4},{21,5},{22,6},{23,7},{24,8},{25... | collective-permute-start | bytes 98312 | tf_op jit(solution)/shard_map/ppermute | solution.py:18
  38.6 6.1 %collective-permute-start = (f32[1,64,128]{2,1,0:T(8,128)S(1)}, f32[1,64,128]{2,1,0:T(8,128)S(1)}, u32[]{:S(2)}, u32[]{:S(2)}) collective-permute-start(f32[1,64,128]{2,1,0:T(8,128)S(1)} %get-tuple-element.35), channel_id=1, source_target_pairs={{0,16},{1,17},{2,18},{3,19},{4,20},{5,21},{6,22},{7,23},{8,24},{9,... | collective-permute-start | bytes 98312 | tf_op jit(solution)/shard_map/ppermute | solution.py:17
  43.8 14.6 %collective-permute-start.20 = (f32[1,2,4,8,128]{4,3,0,2,1:T(8,128)}, f32[1,2,4,8,128]{4,3,0,2,1:T(8,128)}, u32[]{:S(2)}, u32[]{:S(2)}) collective-permute-start(f32[1,2,4,8,128]{4,3,0,2,1:T(8,128)} %maximum_select_fusion.8), channel_id=1, source_target_pairs={{0,1},{1,0},{2,3},{3,2},{4,5},{5,4},{6,7},{7,6},{8,9},{9,8},{10,11... | collective-permute-start | bytes 98312 | tf_op jit(solution)/shard_map/ppermute | solution.py:76
  44.8 6.5 %collective-permute-start.3 = (f32[34,1,128]{2,1,0:T(1,128)S(1)}, f32[34,1,128]{2,1,0:T(1,128)S(1)}, u32[]{:S(2)}, u32[]{:S(2)}) collective-permute-start(f32[34,1,128]{2,1,0:T(1,128)S(1)} %get-tuple-element.26), channel_id=1, source_target_pairs={{4,0},{8,4},{12,8},{5,1},{9,5},{13,9},{6,2},{10,6},{14,10},{7,3},{... | collective-permute-start | bytes 52232 | tf_op jit(solution)/shard_map/ppermute | solution.py:18
  46.1 6.0 %collective-permute-start.2 = (f32[34,1,128]{2,1,0:T(1,128)S(1)}, f32[34,1,128]{2,1,0:T(1,128)S(1)}, u32[]{:S(2)}, u32[]{:S(2)}) collective-permute-start(f32[34,1,128]{2,1,0:T(1,128)S(1)} %get-tuple-element.27), channel_id=1, source_target_pairs={{0,4},{4,8},{8,12},{1,5},{5,9},{9,13},{2,6},{6,10},{10,14},{3,7},{... | collective-permute-start | bytes 52232 | tf_op jit(solution)/shard_map/ppermute | solution.py:17
  51.3 25.4 %collective-permute-start.15 = (f32[1,2,4,8,256]{4,3,0,2,1:T(8,128)}, f32[1,2,4,8,256]{4,3,0,2,1:T(8,128)}, u32[]{:S(2)}, u32[]{:S(2)}) collective-permute-start(f32[1,2,4,8,256]{4,3,0,2,1:T(8,128)} %maximum_select_fusion.4), channel_id=1, source_target_pairs={{0,1},{1,0},{2,3},{3,2},{4,5},{5,4},{6,7},{7,6},{8,9},{9,8},{10,11... | collective-permute-start | bytes 196616 | tf_op jit(solution)/shard_map/ppermute | solution.py:76
  54.9 9.1 %collective-permute-start.4 = (f32[34,66,1]{1,0,2:T(8,128)S(1)}, f32[34,66,1]{1,0,2:T(8,128)S(1)}, u32[]{:S(2)}, u32[]{:S(2)}) collective-permute-start(f32[34,66,1]{1,0,2:T(8,128)S(1)} %copy.25), channel_id=1, source_target_pairs={{0,1},{1,2},{2,3},{4,5},{5,6},{6,7},{8,9},{9,10},{10,11},{12,13},{... | collective-permute-start | bytes 26936 | tf_op jit(solution)/shard_map/ppermute | solution.py:17
  57.2 6.3 %collective-permute-start.5 = (f32[34,66,1]{1,0,2:T(8,128)S(1)}, f32[34,66,1]{1,0,2:T(8,128)S(1)}, u32[]{:S(2)}, u32[]{:S(2)}) collective-permute-start(f32[34,66,1]{1,0,2:T(8,128)S(1)} %copy-done.23), channel_id=1, source_target_pairs={{1,0},{2,1},{3,2},{5,4},{6,5},{7,6},{9,8},{10,9},{11,10},{13,12},{... | collective-permute-start | bytes 26936 | tf_op jit(solution)/shard_map/ppermute | solution.py:18
  60.0 26.8 %collective-permute-start.21 = (f32[2,2,4,8,128]{4,3,0,2,1:T(8,128)}, f32[2,2,4,8,128]{4,3,0,2,1:T(8,128)}, u32[]{:S(2)}, u32[]{:S(2)}) collective-permute-start(f32[2,2,4,8,128]{4,3,0,2,1:T(8,128)} %maximum_select_fusion.5), channel_id=1, source_target_pairs={{0,2},{1,3},{2,0},{3,1},{4,6},{5,7},{6,4},{7,5},{8,10},{9,11},{10,... | collective-permute-start | bytes 196616 | tf_op jit(solution)/shard_map/ppermute | solution.py:76
  71.2 20.7 %copy-start.4 = (f32[32,64,128]{2,1,0:T(8,128)}, f32[32,64,128]{2,1,0:T(8,128)S(1)}, u32[]{:S(2)}) copy-start(f32[32,64,128]{2,1,0:T(8,128)S(1)} %get-tuple-element.9) | copy-start | bytes 3145732
  71.2 7.2 %collective-permute-start.6 = (f32[1,64,128]{2,1,0:T(8,128)S(1)}, f32[1,64,128]{2,1,0:T(8,128)S(1)}, u32[]{:S(2)}, u32[]{:S(2)}) collective-permute-start(f32[1,64,128]{2,1,0:T(8,128)S(1)} %get-tuple-element.32), channel_id=1, source_target_pairs={{0,16},{1,17},{2,18},{3,19},{4,20},{5,21},{6,22},{7,23},{8,24},{9,... | collective-permute-start | bytes 98312 | tf_op jit(solution)/shard_map/ppermute | solution.py:17
  75.4 5.8 %collective-permute-start.7 = (f32[1,64,128]{2,1,0:T(8,128)S(1)}, f32[1,64,128]{2,1,0:T(8,128)S(1)}, u32[]{:S(2)}, u32[]{:S(2)}) collective-permute-start(f32[1,64,128]{2,1,0:T(8,128)S(1)} %get-tuple-element.33), channel_id=1, source_target_pairs={{16,0},{17,1},{18,2},{19,3},{20,4},{21,5},{22,6},{23,7},{24,8},{25... | collective-permute-start | bytes 98312 | tf_op jit(solution)/shard_map/ppermute | solution.py:18
  78.3 26.5 %collective-permute-start.16 = (f32[2,2,4,8,256]{4,3,0,2,1:T(8,128)}, f32[2,2,4,8,256]{4,3,0,2,1:T(8,128)}, u32[]{:S(2)}, u32[]{:S(2)}) collective-permute-start(f32[2,2,4,8,256]{4,3,0,2,1:T(8,128)} %maximum_select_fusion.1), channel_id=1, source_target_pairs={{0,2},{1,3},{2,0},{3,1},{4,6},{5,7},{6,4},{7,5},{8,10},{9,11},{10,... | collective-permute-start | bytes 393224 | tf_op jit(solution)/shard_map/ppermute | solution.py:76
  81.3 7.1 %collective-permute-start.8 = (f32[34,1,128]{2,1,0:T(1,128)S(1)}, f32[34,1,128]{2,1,0:T(1,128)S(1)}, u32[]{:S(2)}, u32[]{:S(2)}) collective-permute-start(f32[34,1,128]{2,1,0:T(1,128)S(1)} %get-tuple-element.24), channel_id=1, source_target_pairs={{0,4},{4,8},{8,12},{1,5},{5,9},{9,13},{2,6},{6,10},{10,14},{3,7},{... | collective-permute-start | bytes 52232 | tf_op jit(solution)/shard_map/ppermute | solution.py:17
  85.5 5.6 %collective-permute-start.9 = (f32[34,1,128]{2,1,0:T(1,128)S(1)}, f32[34,1,128]{2,1,0:T(1,128)S(1)}, u32[]{:S(2)}, u32[]{:S(2)}) collective-permute-start(f32[34,1,128]{2,1,0:T(1,128)S(1)} %get-tuple-element.25), channel_id=1, source_target_pairs={{4,0},{8,4},{12,8},{5,1},{9,5},{13,9},{6,2},{10,6},{14,10},{7,3},{... | collective-permute-start | bytes 52232 | tf_op jit(solution)/shard_map/ppermute | solution.py:18
  96.3 7.0 %collective-permute-start.11 = (f32[34,66,1]{1,0,2:T(8,128)S(1)}, f32[34,66,1]{1,0,2:T(8,128)S(1)}, u32[]{:S(2)}, u32[]{:S(2)}) collective-permute-start(f32[34,66,1]{1,0,2:T(8,128)S(1)} %copy.31), channel_id=1, source_target_pairs={{1,0},{2,1},{3,2},{5,4},{6,5},{7,6},{9,8},{10,9},{11,10},{13,12},{... | collective-permute-start | bytes 26936 | tf_op jit(solution)/shard_map/ppermute | solution.py:18
  97.6 4.1 %collective-permute-start.10 = (f32[34,66,1]{1,0,2:T(8,128)}, f32[34,66,1]{1,0,2:T(8,128)S(1)}, u32[]{:S(2)}, u32[]{:S(2)}) collective-permute-start(f32[34,66,1]{1,0,2:T(8,128)} %copy.29), channel_id=1, source_target_pairs={{0,1},{1,2},{2,3},{4,5},{5,6},{6,7},{8,9},{9,10},{10,11},{12,13},{... | collective-permute-start | bytes 26936 | tf_op jit(solution)/shard_map/ppermute | solution.py:17
  116.5 3.3 %collective-permute-start.22 = (f32[1,64,128]{2,1,0:T(8,128)S(1)}, f32[1,64,128]{2,1,0:T(8,128)S(1)}, u32[]{:S(2)}, u32[]{:S(2)}) collective-permute-start(f32[1,64,128]{2,1,0:T(8,128)S(1)} %get-tuple-element.30), channel_id=1, source_target_pairs={{0,16},{1,17},{2,18},{3,19},{4,20},{5,21},{6,22},{7,23},{8,24},{9,... | collective-permute-start | bytes 98312 | tf_op jit(solution)/shard_map/ppermute | solution.py:17
  118.2 6.0 %collective-permute-start.23 = (f32[1,64,128]{2,1,0:T(8,128)S(1)}, f32[1,64,128]{2,1,0:T(8,128)S(1)}, u32[]{:S(2)}, u32[]{:S(2)}) collective-permute-start(f32[1,64,128]{2,1,0:T(8,128)S(1)} %get-tuple-element.31), channel_id=1, source_target_pairs={{16,0},{17,1},{18,2},{19,3},{20,4},{21,5},{22,6},{23,7},{24,8},{25... | collective-permute-start | bytes 98312 | tf_op jit(solution)/shard_map/ppermute | solution.py:18
  124.2 4.9 %collective-permute-start.24 = (f32[34,1,128]{2,1,0:T(1,128)S(1)}, f32[34,1,128]{2,1,0:T(1,128)S(1)}, u32[]{:S(2)}, u32[]{:S(2)}) collective-permute-start(f32[34,1,128]{2,1,0:T(1,128)S(1)} %get-tuple-element.22), channel_id=1, source_target_pairs={{0,4},{4,8},{8,12},{1,5},{5,9},{9,13},{2,6},{6,10},{10,14},{3,7},{... | collective-permute-start | bytes 52232 | tf_op jit(solution)/shard_map/ppermute | solution.py:17
  127.7 5.6 %collective-permute-start.25 = (f32[34,1,128]{2,1,0:T(1,128)S(1)}, f32[34,1,128]{2,1,0:T(1,128)S(1)}, u32[]{:S(2)}, u32[]{:S(2)}) collective-permute-start(f32[34,1,128]{2,1,0:T(1,128)S(1)} %get-tuple-element.23), channel_id=1, source_target_pairs={{4,0},{8,4},{12,8},{5,1},{9,5},{13,9},{6,2},{10,6},{14,10},{7,3},{... | collective-permute-start | bytes 52232 | tf_op jit(solution)/shard_map/ppermute | solution.py:18
  138.4 5.6 %collective-permute-start.26 = (f32[34,66,1]{1,0,2:T(8,128)}, f32[34,66,1]{1,0,2:T(8,128)}, u32[]{:S(2)}, u32[]{:S(2)}) collective-permute-start(f32[34,66,1]{1,0,2:T(8,128)} %copy.36), channel_id=1, source_target_pairs={{0,1},{1,2},{2,3},{4,5},{5,6},{6,7},{8,9},{9,10},{10,11},{12,13},{... | collective-permute-start | bytes 26936 | tf_op jit(solution)/shard_map/ppermute | solution.py:17
  142.7 6.9 %collective-permute-start.27 = (f32[34,66,1]{1,0,2:T(8,128)}, f32[34,66,1]{1,0,2:T(8,128)}, u32[]{:S(2)}, u32[]{:S(2)}) collective-permute-start(f32[34,66,1]{1,0,2:T(8,128)} %copy.38), channel_id=1, source_target_pairs={{1,0},{2,1},{3,2},{5,4},{6,5},{7,6},{9,8},{10,9},{11,10},{13,12},{... | collective-permute-start | bytes 26936 | tf_op jit(solution)/shard_map/ppermute | solution.py:18
  160.0 3.6 %collective-permute-start.28 = (f32[2,128]{1,0:T(2,128)S(1)}, f32[2,128]{1,0:T(2,128)S(1)}, u32[]{:S(2)}, u32[]{:S(2)}) collective-permute-start(f32[2,128]{1,0:T(2,128)S(1)} %broadcast_in_dim.56), channel_id=1, source_target_pairs={{0,4},{4,0},{8,12},{12,8},{1,5},{5,1},{9,13},{13,9},{2,6},{6,2},{1... | collective-permute-start | bytes 3080 | tf_op jit(solution)/shard_map/ppermute | solution.py:93
  163.7 4.5 %collective-permute-start.29 = (f32[2,128]{1,0:T(2,128)S(1)}, f32[2,128]{1,0:T(2,128)S(1)}, u32[]{:S(2)}, u32[]{:S(2)}) collective-permute-start(f32[2,128]{1,0:T(2,128)S(1)} %broadcast_add_fusion), channel_id=1, source_target_pairs={{0,8},{4,12},{8,0},{12,4},{1,9},{5,13},{9,1},{13,5},{2,10},{6,14},... | collective-permute-start | bytes 3080 | tf_op jit(solution)/shard_map/ppermute | solution.py:93
  168.2 3.6 %collective-permute-start.30 = (f32[2,128]{1,0:T(2,128)S(1)}, f32[2,128]{1,0:T(2,128)S(1)}, u32[]{:S(2)}, u32[]{:S(2)}) collective-permute-start(f32[2,128]{1,0:T(2,128)S(1)} %fusion.95), channel_id=1, source_target_pairs={{0,16},{16,0},{1,17},{17,1},{2,18},{18,2},{3,19},{19,3},{4,20},{20... | collective-permute-start | bytes 3080 | tf_op jit(solution)/shard_map/ppermute | solution.py:93
  171.8 1.2 collective-permute-start.31
  173.0 4.5 %collective-permute-start.32 = (f32[2,128]{1,0:T(2,128)S(1)}, f32[2,128]{1,0:T(2,128)S(1)}, u32[]{:S(2)}, u32[]{:S(2)}) collective-permute-start(f32[2,128]{1,0:T(2,128)S(1)} %add.221), channel_id=1, source_target_pairs={{0,2},{1,3},{2,0},{3,1},{4,6},{5,7},{6,4},{7,5},{8,10},{9,11},{10,... | collective-permute-start | bytes 3080 | tf_op jit(solution)/shard_map/ppermute | solution.py:93
  180.9 6.4 %collective-permute-start.39 = (f32[1,1,8,128]{3,2,1,0:T(8,128)S(1)}, f32[1,1,8,128]{3,2,1,0:T(8,128)S(1)}, u32[]{:S(2)}, u32[]{:S(2)}) collective-permute-start(f32[1,1,8,128]{3,2,1,0:T(8,128)S(1)} %broadcast_in_dim.57), channel_id=1, source_target_pairs={{0,4},{4,0},{8,12},{12,8},{1,5},{5,1},{9,13},{13,9},{2,6},{6,2},{1... | collective-permute-start | bytes 12296 | tf_op jit(solution)/shard_map/ppermute | solution.py:76
  184.1 10.5 %collective-permute-start.33 = (f32[1,64,128]{2,1,0:T(8,128)S(1)}, f32[1,64,128]{2,1,0:T(8,128)S(1)}, u32[]{:S(2)}, u32[]{:S(2)}) collective-permute-start(f32[1,64,128]{2,1,0:T(8,128)S(1)} %get-tuple-element.28), channel_id=1, source_target_pairs={{0,16},{1,17},{2,18},{3,19},{4,20},{5,21},{6,22},{7,23},{8,24},{9,... | collective-permute-start | bytes 98312 | tf_op jit(solution)/shard_map/ppermute | solution.py:17
  186.0 8.6 %collective-permute-start.34 = (f32[1,64,128]{2,1,0:T(8,128)S(1)}, f32[1,64,128]{2,1,0:T(8,128)S(1)}, u32[]{:S(2)}, u32[]{:S(2)}) collective-permute-start(f32[1,64,128]{2,1,0:T(8,128)S(1)} %get-tuple-element.29), channel_id=1, source_target_pairs={{16,0},{17,1},{18,2},{19,3},{20,4},{21,5},{22,6},{23,7},{24,8},{25... | collective-permute-start | bytes 98312 | tf_op jit(solution)/shard_map/ppermute | solution.py:18
  187.3 4.6 %collective-permute-start.40 = (f32[2,1,8,128]{3,2,1,0:T(8,128)S(1)}, f32[2,1,8,128]{3,2,1,0:T(8,128)S(1)}, u32[]{:S(2)}, u32[]{:S(2)}) collective-permute-start(f32[2,1,8,128]{3,2,1,0:T(8,128)S(1)} %maximum_select_fusion.16), channel_id=1, source_target_pairs={{0,8},{4,12},{8,0},{12,4},{1,9},{5,13},{9,1},{13,5},{2,10},{6,14},... | collective-permute-start | bytes 24584 | tf_op jit(solution)/shard_map/ppermute | solution.py:76
  192.0 7.4 %collective-permute-start.41 = (f32[1,4,8,128]{3,2,1,0:T(8,128)S(1)}, f32[1,4,8,128]{3,2,1,0:T(8,128)S(1)}, u32[]{:S(2)}, u32[]{:S(2)}) collective-permute-start(f32[1,4,8,128]{3,2,1,0:T(8,128)S(1)} %maximum_select_fusion.13), channel_id=1, source_target_pairs={{0,16},{16,0},{1,17},{17,1},{2,18},{18,2},{3,19},{19,3},{4,20},{20... | collective-permute-start | bytes 49160 | tf_op jit(solution)/shard_map/ppermute | solution.py:76
  194.7 4.8 %collective-permute-start.35 = (f32[34,1,128]{2,1,0:T(1,128)S(1)}, f32[34,1,128]{2,1,0:T(1,128)S(1)}, u32[]{:S(2)}, u32[]{:S(2)}) collective-permute-start(f32[34,1,128]{2,1,0:T(1,128)S(1)} %get-tuple-element.20), channel_id=1, source_target_pairs={{0,4},{4,8},{8,12},{1,5},{5,9},{9,13},{2,6},{6,10},{10,14},{3,7},{... | collective-permute-start | bytes 52232 | tf_op jit(solution)/shard_map/ppermute | solution.py:17
  198.1 5.6 %collective-permute-start.36 = (f32[34,1,128]{2,1,0:T(1,128)S(1)}, f32[34,1,128]{2,1,0:T(1,128)S(1)}, u32[]{:S(2)}, u32[]{:S(2)}) collective-permute-start(f32[34,1,128]{2,1,0:T(1,128)S(1)} %get-tuple-element.21), channel_id=1, source_target_pairs={{4,0},{8,4},{12,8},{5,1},{9,5},{13,9},{6,2},{10,6},{14,10},{7,3},{... | collective-permute-start | bytes 52232 | tf_op jit(solution)/shard_map/ppermute | solution.py:18
  199.4 14.9 %collective-permute-start.42 = (f32[1,2,4,8,128]{4,3,2,1,0:T(8,128)S(1)}, f32[1,2,4,8,128]{4,3,2,1,0:T(8,128)S(1)}, u32[]{:S(2)}, u32[]{:S(2)}) collective-permute-start(f32[1,2,4,8,128]{4,3,2,1,0:T(8,128)S(1)} %maximum_select_fusion.9), channel_id=1, source_target_pairs={{0,1},{1,0},{2,3},{3,2},{4,5},{5,4},{6,7},{7,6},{8,9},{9,8},{10,11... | collective-permute-start | bytes 98312 | tf_op jit(solution)/shard_map/ppermute | solution.py:76
  210.0 10.2 %collective-permute-start.38 = (f32[34,66,1]{1,0,2:T(8,128)}, f32[34,66,1]{1,0,2:T(8,128)}, u32[]{:S(2)}, u32[]{:S(2)}) collective-permute-start(f32[34,66,1]{1,0,2:T(8,128)} %copy.42), channel_id=1, source_target_pairs={{1,0},{2,1},{3,2},{5,4},{6,5},{7,6},{9,8},{10,9},{11,10},{13,12},{... | collective-permute-start | bytes 26936 | tf_op jit(solution)/shard_map/ppermute | solution.py:18
  211.3 7.3 %collective-permute-start.37 = (f32[34,66,1]{1,0,2:T(8,128)S(1)}, f32[34,66,1]{1,0,2:T(8,128)S(1)}, u32[]{:S(2)}, u32[]{:S(2)}) collective-permute-start(f32[34,66,1]{1,0,2:T(8,128)S(1)} %copy.40), channel_id=1, source_target_pairs={{0,1},{1,2},{2,3},{4,5},{5,6},{6,7},{8,9},{9,10},{10,11},{12,13},{... | collective-permute-start | bytes 26936 | tf_op jit(solution)/shard_map/ppermute | solution.py:17
  214.9 7.7 %collective-permute-start.43 = (f32[2,2,4,8,128]{4,3,2,1,0:T(8,128)}, f32[2,2,4,8,128]{4,3,2,1,0:T(8,128)}, u32[]{:S(2)}, u32[]{:S(2)}) collective-permute-start(f32[2,2,4,8,128]{4,3,2,1,0:T(8,128)} %maximum_select_fusion.6), channel_id=1, source_target_pairs={{0,2},{1,3},{2,0},{3,1},{4,6},{5,7},{6,4},{7,5},{8,10},{9,11},{10,... | collective-permute-start | bytes 196616 | tf_op jit(solution)/shard_map/ppermute | solution.py:76
  (22 other events, 123.6 us)

commit v2 on v0

v2 whole, which is shorter than its diff:
```python
import functools

import jax
import jax.numpy as jnp
from jax import lax
from jax.experimental import pallas as pl
from jax.experimental.pallas import tpu as pltpu
from jax.sharding import PartitionSpec as P

bound_low = 0.1
bound_high = 2.0
theta = 0.5 * (bound_high + bound_low)
delta = 0.5 * (bound_high - bound_low)
weight_first = delta / theta
weight_second = 1.0 / (2.0 * theta / delta - weight_first)
far = 2.0 * weight_second / delta
near = 1.0 + weight_second * weight_first + far * (theta - 1.0)

AXES = ("gx", "gy", "gz")
LANES = 128
REACH = 4
SUBS = 8
SLOT = 64
EXACT = lax.Precision.HIGHEST
VMEM = pl.BlockSpec(memory_space=pltpu.VMEM)


def lane_of(rows):
    return lax.broadcasted_iota(jnp.int32, (rows, LANES), 1)


def row_of(rows):
    return lax.broadcasted_iota(jnp.int32, (rows, LANES), 0)


def message_rows(records, halves):
    meta = 16 * pl.cdiv(3 + 3 * halves, 16)
    return records, records + 8 * halves, records + 16 * halves, meta


def place_sums(total, device, slabs):
    width = LANES // slabs
    base = lax.rem(device, width) * slabs
    source = lax.broadcasted_iota(jnp.int32, (LANES, LANES), 0)
    target = lax.broadcasted_iota(jnp.int32, (LANES, LANES), 1)
    first = (target - base) * width
    chosen = (source >= first) & (source < first + width) & (target >= base) & (target < base + slabs)
    return jnp.dot(total, chosen.astype(jnp.float32), precision=EXACT, preferred_element_type=jnp.float32)


def device_number(sizes):
    return (lax.axis_index("gx") * sizes[1] + lax.axis_index("gy")) * sizes[2] + lax.axis_index("gz")


def pack_kernel(sizes, residual_ref, inverse_ref, rows_ref, block_ref, column_ref, out_ref, index_ref):
    size_x, size_y, _ = residual_ref.shape
    slabs, subdomains = inverse_ref.shape
    records = rows_ref.shape[0]
    halves = subdomains // LANES
    high_at, low_at, meta_at, meta_rows = message_rows(records, halves)
    out_ref[0:records, :] = rows_ref[...]
    whole = jnp.concatenate([inverse_ref[:, h * LANES : (h + 1) * LANES] for h in range(halves)], axis=0)
    high = whole.astype(jnp.bfloat16)
    out_ref[high_at : high_at + 8 * halves, :] = high
    out_ref[low_at : low_at + 8 * halves, :] = (whole - high.astype(jnp.float32)).astype(jnp.bfloat16)

    index_ref[...] = jnp.zeros_like(index_ref)
    index_ref[0:1, 0:records] = block_ref[...].astype(jnp.float32) + 1.0
    column = column_ref[...].astype(jnp.float32)
    plane = jnp.floor((column + 0.5) * (1.0 / size_y))
    index_ref[1:2, 0:records] = plane + (lax.axis_index("gx") * size_x).astype(jnp.float32)
    index_ref[2:3, 0:records] = column - plane * size_y

    total = lax.fori_loop(
        1, size_x, lambda i, acc: acc + residual_ref[i], residual_ref[0], unroll=4
    )
    total = jnp.broadcast_to(jnp.sum(total, axis=0, keepdims=True), (8, LANES))
    device = device_number(sizes)
    sums = place_sums(total, device, slabs)[0:1]
    high = sums.astype(jnp.bfloat16).astype(jnp.float32)
    middle = (sums - high).astype(jnp.bfloat16).astype(jnp.float32)
    low = sums - high - middle
    half = device // (LANES // slabs)
    row = row_of(meta_rows)
    meta = jnp.where(row == 0, index_ref[0:1, :], 0.0)
    meta = jnp.where(row == 1, index_ref[1:2, :], meta)
    meta = jnp.where(row == 2, index_ref[2:3, :], meta)
    meta = jnp.where(row == 3 + half, high, meta)
    meta = jnp.where(row == 3 + halves + half, middle, meta)
    meta = jnp.where(row == 3 + 2 * halves + half, low, meta)
    out_ref[meta_at : meta_at + meta_rows, :] = meta.astype(jnp.bfloat16)


def margin_y_kernel(residual_ref, above_ref, below_ref, down_ref, up_ref):
    size_x, size_y, _ = residual_ref.shape
    row = row_of(8)

    def plane(x, at):
        tile = pl.ds(at, 8)
        if x < size_x:
            return residual_ref[x, tile, :]
        x -= size_x
        return above_ref[x, tile, :] if x < REACH else below_ref[x - REACH, tile, :]

    for pair in range((size_x + 2 * REACH) // 2):
        one, two = 2 * pair, 2 * pair + 1
        down_ref[pair] = jnp.where(row < 4, plane(one, 0), pltpu.roll(plane(two, 0), 4, 0))
        up_ref[pair] = jnp.where(row < 4, pltpu.roll(plane(two, size_y - 8), 4, 0), plane(one, size_y - 8))


def margin_z_kernel(residual_ref, above_ref, below_ref, after_ref, before_ref, wide_ref, edge_ref):
    size_x, size_y, _ = residual_ref.shape
    wide_y = size_y + 2 * REACH
    row = row_of(8)
    place = lane_of(wide_y) % 16
    sub_of = lane_of(wide_y) // 16
    for x in range(size_x + 2 * REACH):
        if x < size_x:
            wide_ref[x, 0:size_y, :] = residual_ref[x]
        elif x < size_x + REACH:
            wide_ref[x, 0:size_y, :] = above_ref[x - size_x]
        else:
            wide_ref[x, 0:size_y, :] = below_ref[x - size_x - REACH]
        after, before = after_ref[x // 2], before_ref[x // 2]
        if x % 2:
            after, before = pltpu.roll(after, 4, 0), pltpu.roll(before, 4, 0)
        wide_ref[x, size_y:wide_y, :] = jnp.where(row < 4, after, before)

    def group(g, carry):
        edge = jnp.zeros((wide_y, LANES), jnp.float32)
        for sub in range(SUBS):
            value = wide_ref[g * SUBS + sub]
            first = pltpu.roll(value, (sub * 16 + 4) % LANES, 1)
            last = pltpu.roll(value, (sub * 16 + 8 + 4) % LANES, 1)
            edge = jnp.where((sub_of == sub) & (place >= 4) & (place < 8), first, edge)
            edge = jnp.where((sub_of == sub) & (place >= 8) & (place < 12), last, edge)
        edge_ref[g] = edge
        return carry

    lax.fori_loop(0, edge_ref.shape[0], group, 0)


def coarse_solve(message_refs, high_at, low_at, halves, sums):
    def body(message_ref, i, total):
        high = message_ref[i, high_at : high_at + 8 * halves, :].astype(jnp.float32)
        low = message_ref[i, low_at : low_at + 8 * halves, :].astype(jnp.float32)
        rows = high + low
        tiles = [rows[8 * h : 8 * h + 8] for h in range(halves)]
        inner = sum(tiles[h] * sums[h] for h in range(halves))
        inner = jnp.sum(inner, axis=1, keepdims=True)
        return tuple(total[h] + inner * tiles[h] for h in range(halves))

    zero = jnp.zeros((8, LANES), jnp.float32)
    total = (zero,) * halves
    for ref in message_refs:
        total = lax.fori_loop(0, ref.shape[0], functools.partial(body, ref), total, unroll=8)
    return [jnp.broadcast_to(jnp.sum(t, axis=0, keepdims=True), (8, LANES)) for t in total]


def pick(values, device, slab, slabs):
    per_half = LANES // slabs
    half = device // per_half
    chosen = values[0]
    for h in range(1, len(values)):
        chosen = jnp.where(half == h, values[h], chosen)
    index = lax.rem(device, per_half) * slabs + slab
    return jnp.take_along_axis(chosen, index, axis=1)


def main_kernel(
    sizes, records, halves, slabs, size_x, size_y,
    message_ref, other_ref, wide_ref, edge_ref, lower_ref, upper_ref,
    direction_ref, applied_ref, stat_ref,
    key_ref, code_ref, turned_ref, left_ref, right_ref, added_ref,
    density_ref, x_ref, y_ref, z_ref, h_ref, u_ref, d_ref, inside_ref, coarse_ref,
):
    n_gx, n_gy, n_gz = sizes
    gx, gy, gz = (lax.axis_index(a) for a in AXES)
    half = message_ref.shape[0]
    wide_x, wide_y = size_x + 2 * REACH, size_y + 2 * REACH
    groups = wide_x // SUBS
    high_at, low_at, meta_at, meta_rows = message_rows(records, halves)
    f32, bf16 = jnp.float32, jnp.bfloat16
    lane = lane_of(wide_y)
    row = row_of(wide_y)
    place = lane % 16
    sub_of = lane // 16

    def roll(value, shift, axis):
        return pltpu.roll(value, shift, axis)

    def read_meta(i, total):
        for j, ref in enumerate((message_ref, other_ref)):
            tile = ref[i, meta_at : meta_at + meta_rows, :].astype(f32)
            for k in range(3):
                key_ref[k, pl.ds(i + j * half, 1), :] = tile[k : k + 1]
            total = total + tile
        return total

    total = lax.fori_loop(0, half, read_meta, jnp.zeros((meta_rows, LANES), f32), unroll=4)
    sums = [
        total[3 + h : 4 + h] + total[3 + halves + h : 4 + halves + h] + total[3 + 2 * halves + h : 4 + 2 * halves + h]
        for h in range(halves)
    ]
    coarse = coarse_solve((message_ref, other_ref), high_at, low_at, halves, sums)

    def there(ix, iy, iz):
        ok = (ix >= 0) & (ix < n_gx) & (iy >= 0) & (iy < n_gy) & (iz >= 0) & (iz < n_gz)
        return ok.astype(f32), jnp.where(ok, (ix * n_gy + iy) * n_gz + iz, 0)

    lane8 = lane_of(8)
    row8 = row_of(8)
    place8 = lane8 % 16
    constant = lambda k: jnp.full((8, LANES), k, jnp.int32)

    def main_values(ix, iy):
        ok, device = there(ix, iy, gz)
        return jnp.full((8, LANES), ok, f32), ok * pick(coarse, device, lane8 // (LANES // slabs), slabs)

    def edge_values(ix, iy):
        parts = []
        for iz, slab in ((gz - 1, slabs - 1), (gz, 0), (gz, slabs - 1), (gz + 1, 0)):
            ok, device = there(ix, iy, iz)
            parts.append((jnp.full((8, LANES), ok, f32), ok * pick(coarse, device, constant(slab), slabs)))
        out = []
        for k in range(2):
            value = jnp.where(place8 < 4, parts[0][k], parts[1][k])
            value = jnp.where(place8 >= 8, parts[2][k], value)
            out.append(jnp.where(place8 >= 12, parts[3][k], value))
        return out

    def fill(kind, values_at):
        own, after, before = values_at(gy), values_at(gy + 1), values_at(gy - 1)
        for k, ref in enumerate((inside_ref, coarse_ref)):
            ref[kind, 0:size_y, :] = jnp.concatenate([own[k]] * (size_y // 8), axis=0)
            ref[kind, size_y:wide_y, :] = jnp.where(row8 < 4, after[k], before[k])

    def beside_x(iy):
        above, below = edge_values(gx + 1, iy), edge_values(gx - 1, iy)
        return [jnp.where(lane8 < 4 * 16, a, b) for a, b in zip(above, below)]

    fill(0, lambda iy: main_values(gx, iy))
    fill(1, lambda iy: main_values(gx + 1, iy))
    fill(2, lambda iy: main_values(gx - 1, iy))
    fill(3, lambda iy: edge_values(gx, iy))
    fill(4, beside_x)

    block, plane, line = (key_ref[k, 0:half, :] + roll(key_ref[k, half : 2 * half, :], SLOT, 1) for k in range(3))
    valid = block > 0.5
    block = block - 1.0
    block_y = jnp.floor((block + 0.5) * (1.0 / n_gz))
    side = block - block_y * n_gz - gz.astype(f32)
    at_x = plane - (gx * size_x).astype(f32)
    at_y = (block_y - gy.astype(f32)) * size_y + line
    valid = valid & (at_x >= -REACH) & (at_x < size_x + REACH) & (at_y >= -REACH) & (at_y < size_y + REACH)
    at_x = jnp.where(at_x < 0, at_x + wide_x, at_x)
    at_y = jnp.where(at_y < 0, at_y + wide_y, at_y)
    at_group = jnp.floor((at_x + 0.5) * (1.0 / SUBS))
    at_sub = at_x - at_group * SUBS
    code_ref[...] = jnp.where(valid, at_group * wide_y + at_y, -1.0)
    turned_ref[...] = jnp.full(turned_ref.shape, -1.0, f32)
    turned_ref[0, 0:half, :] = jnp.where(side == 0, at_sub, -1.0)
    turned_ref[1, 0:half, :] = jnp.where((side >= -1) & (side <= 1), at_sub + SUBS * (side + 1), -1.0)
    turned_ref[0] = turned_ref[0].T
    turned_ref[1] = turned_ref[1].T

    chunk = min(half, 16)
    rows_all = left_ref.shape[0]
    row_number = lax.broadcasted_iota(jnp.int32, (rows_all, LANES), 0).astype(f32)
    source = lax.broadcasted_iota(jnp.int32, (LANES, LANES), 0)
    target = lax.broadcasted_iota(jnp.int32, (LANES, LANES), 1)
    wanted = jnp.where(target % 8 < 4, target % 4 + (LANES - 4), target % 4)
    chooser = (source == wanted).astype(bf16)
    kind = jnp.where(target % 16 < 4, 0, jnp.where(target % 16 < 12, 1, 2))
    edge_code = (target // 16 + SUBS * kind).astype(f32)

    for c in range(half // chunk):
        def build(q, carry, c=c):
            p = q + c * chunk
            at = pl.ds(pl.multiple_of(q * LANES, LANES), LANES)
            code = code_ref[pl.ds(p, 1), :]
            left_ref[:, at] = jnp.where(row_number == code, 1.0, 0.0).astype(bf16)
            rows = jnp.concatenate([message_ref[p, 0:SLOT, :], other_ref[p, 0:SLOT, :]], axis=0)
            turn = lax.rem(LANES - p, LANES)
            key = jnp.broadcast_to(roll(turned_ref[0], turn, 1)[:, 0:1], (LANES, LANES))
            edge_key = jnp.broadcast_to(roll(turned_ref[1], turn, 1)[:, 0:1], (LANES, LANES))
            wide_rows = rows.astype(f32)
            for sub in range(SUBS):
                right_ref[at, sub * LANES : (sub + 1) * LANES] = jnp.where(key == sub, wide_rows, 0.0).astype(bf16)
            edges = jnp.dot(rows, chooser, preferred_element_type=f32)
            right_ref[at, SUBS * LANES :] = jnp.where(edge_key == edge_code, edges, 0.0).astype(bf16)
            return carry

        lax.fori_loop(0, chunk, build, 0)
        for n in range(0, SUBS + 1, 2):
            columns = slice(n * LANES, min(n + 2, SUBS + 1) * LANES)
            product = jnp.dot(left_ref[...], right_ref[:, columns], preferred_element_type=f32)
            added_ref[:, columns] = product if c == 0 else added_ref[:, columns] + product

    def kind_of(x):
        return jnp.where(x < size_x, 0, jnp.where(x < size_x + REACH, 1, 2))

    for g in range(groups):
        lines = slice(g * wide_y, (g + 1) * wide_y)
        for sub in range(SUBS):
            x = g * SUBS + sub
            k = 0 if x < size_x else 1 if x < size_x + REACH else 2
            density_ref[x] = inside_ref[k] + added_ref[lines, sub * LANES : (sub + 1) * LANES]
        k = 3 if g < groups - 1 else 4
        density_ref[wide_x + g] = inside_ref[k] + added_ref[lines, SUBS * LANES :]

    def z_after(value, edges, sub):
        return jnp.where(lane == LANES - 1, roll(edges, 115 - 16 * sub, 1), roll(value, LANES - 1, 1))

    def z_before(value, edges, sub):
        return jnp.where(lane == 0, roll(edges, 125 - 16 * sub, 1), roll(value, 1, 1))

    def y_after(value):
        return roll(value, wide_y - 1, 0)

    def y_before(value):
        return roll(value, 1, 0)

    def edge_x_after(ref, g):
        other = ref[wide_x + (g + 1) % groups]
        return jnp.where(lane >= LANES - 16, roll(other, LANES - 16, 1), roll(ref[wide_x + g], LANES - 16, 1))

    def edge_x_before(ref, g):
        other = ref[wide_x + (g - 1) % groups]
        return jnp.where(lane < 16, roll(other, 16, 1), roll(ref[wide_x + g], 16, 1))

    def following(x):
        return jnp.where(x + 1 == wide_x, 0, x + 1)

    def preceding(x):
        return jnp.where(x == 0, wide_x - 1, x - 1)

    def beta(one, two):
        return 2.0 / jnp.maximum(one + two, 0.5)

    for g in range(groups):
        j = wide_x + g
        value = density_ref[j]
        x_ref[j] = beta(value, edge_x_after(density_ref, g))
        y_ref[j] = beta(value, y_after(value))
        z_ref[j] = beta(value, roll(value, LANES - 1, 1))

    for g in range(groups):
        j = wide_x + g
        k = 3 if g < groups - 1 else 4
        diagonal = x_ref[j] + edge_x_before(x_ref, g) + y_ref[j] + y_before(y_ref[j]) + z_ref[j] + roll(z_ref[j], 1, 1)
        h_ref[j] = inside_ref[k] / diagonal
        residual = edge_ref[g]
        residual = jnp.where(place < 4, roll(lower_ref[g], LANES - 8, 1), residual)
        residual = jnp.where(place >= 12, roll(upper_ref[g], 8, 1), residual)
        u_ref[j] = residual * h_ref[j] * (1.0 / theta)

    def faces(x, carry):
        value = density_ref[x]
        x_ref[x] = beta(value, density_ref[following(x)])
        y_ref[x] = beta(value, y_after(value))
        z_ref[x] = beta(value, z_after(value, density_ref[wide_x + x // SUBS], lax.rem(x, SUBS)))
        return carry

    lax.fori_loop(0, wide_x, faces, 0)

    def scale(x, carry):
        along_y, along_z = y_ref[x], z_ref[x]
        diagonal = x_ref[x] + x_ref[preceding(x)] + along_y + y_before(along_y)
        diagonal = diagonal + along_z + z_before(along_z, z_ref[wide_x + x // SUBS], lax.rem(x, SUBS))
        h = inside_ref[kind_of(x)] / diagonal
        h_ref[x] = h
        u_ref[x] = wide_ref[x] * h * (1.0 / theta)
        return carry

    lax.fori_loop(0, wide_x, scale, 0)

    def smooth(ref, x):
        value, along_y, along_z = ref[x], y_ref[x], z_ref[x]
        j, sub = wide_x + x // SUBS, lax.rem(x, SUBS)
        before = preceding(x)
        beside = x_ref[x] * ref[following(x)] + x_ref[before] * ref[before]
        beside = beside + along_y * y_after(value) + y_before(along_y * value)
        beside = beside + along_z * z_after(value, ref[j], sub) + z_before(along_z * value, z_ref[j] * ref[j], sub)
        return near * value + far * (h_ref[x] * beside)

    def edge_smooth(ref, g):
        j = wide_x + g
        value = ref[j]
        product = x_ref[j] * value
        before = x_ref[wide_x + (g - 1) % groups] * ref[wide_x + (g - 1) % groups]
        beside = x_ref[j] * edge_x_after(ref, g) + jnp.where(lane < 16, roll(before, 16, 1), roll(product, 16, 1))
        beside = beside + y_ref[j] * y_after(value) + y_before(y_ref[j] * value)
        beside = beside + z_ref[j] * roll(value, LANES - 1, 1) + roll(z_ref[j] * value, 1, 1)
        return near * value + far * (h_ref[j] * beside)

    for g in range(groups):
        d_ref[wide_x + g] = edge_smooth(u_ref, g) + coarse_ref[3 if g < groups - 1 else 4]

    def direct(x, carry):
        d_ref[x] = smooth(u_ref, x) + coarse_ref[kind_of(x)]
        return carry

    lax.fori_loop(0, wide_x, direct, 0)

    for g in range(groups):
        j = wide_x + g
        value = d_ref[j]
        flux_y = y_ref[j] * (value - y_after(value))
        flux_z = z_ref[j] * (value - roll(value, LANES - 1, 1))
        image = x_ref[j] * (value - edge_x_after(d_ref, g))
        image = image + edge_x_before(x_ref, g) * (value - edge_x_before(d_ref, g))
        image = image + (flux_y - y_before(flux_y)) + (flux_z - roll(flux_z, 1, 1))
        u_ref[j] = image * h_ref[j] * (1.0 / theta)

    def image_of(x):
        value = d_ref[x]
        j, sub = wide_x + x // SUBS, lax.rem(x, SUBS)
        before = preceding(x)
        edges = d_ref[j]
        edge_flux = z_ref[j] * (edges - roll(edges, LANES - 1, 1))
        flux_y = y_ref[x] * (value - y_after(value))
        flux_z = z_ref[x] * (value - z_after(value, edges, sub))
        image = x_ref[x] * (value - d_ref[following(x)]) + x_ref[before] * (value - d_ref[before])
        image = image + (flux_y - y_before(flux_y)) + (flux_z - z_before(flux_z, edge_flux, sub))
        u_ref[x] = image * h_ref[x] * (1.0 / theta)
        return value, image

    def image_own(x, carry):
        value, image = image_of(x)
        value, image = value[0:size_y], image[0:size_y]
        direction_ref[x] = value
        return (
            carry[0] + wide_ref[x, 0:size_y, :] * value,
            carry[1] + value * image,
            carry[2] + image,
        )

    zero = jnp.zeros((size_y, LANES), f32)
    found = lax.fori_loop(0, size_x, image_own, (zero, zero, zero))
    image_of(size_x)
    image_of(wide_x - 1)

    device = device_number(sizes)
    folded = [jnp.sum(f, axis=0, keepdims=True) for f in found]
    image_sums = place_sums(jnp.broadcast_to(folded[2], (8, LANES)), device, slabs)[0:1]
    gamma = jnp.sum(folded[0], axis=1, keepdims=True)
    curvature = jnp.sum(folded[1], axis=1, keepdims=True)
    last = jnp.where(lane8[0:1] == 0, gamma, jnp.where(lane8[0:1] == 1, curvature, 0.0))
    own_half = device // (LANES // slabs)

    def spread(i, carry):
        for h in range(halves):
            stat_ref[i, h : h + 1, :] = jnp.where(own_half == h, image_sums, 0.0)
        stat_ref[i, halves : halves + 1, :] = last
        return carry

    lax.fori_loop(0, stat_ref.shape[0], spread, 0, unroll=4)

    def second(x, carry):
        applied_ref[x] = smooth(u_ref, x)[0:size_y]
        return carry

    lax.fori_loop(0, size_x, second, 0)


def finish_kernel(
    sizes, records, halves, slabs,
    stat_ref, message_ref, other_ref, direction_ref, applied_ref, pressure_ref, preconditioned_ref,
):
    high_at, low_at, _, _ = message_rows(records, halves)
    total = lax.fori_loop(
        1, stat_ref.shape[0], lambda i, acc: acc + stat_ref[i], stat_ref[0], unroll=4
    )
    sums = [total[h : h + 1] for h in range(halves)]
    coarse = coarse_solve((message_ref, other_ref), high_at, low_at, halves, sums)
    lane8 = lane_of(8)
    own = pick(coarse, device_number(sizes), lane8 // (LANES // slabs), slabs)
    last = total[halves : halves + 1]
    alpha = last[:, 0:1] / last[:, 1:2]
    size_x, size_y, _ = direction_ref.shape
    alpha = jnp.broadcast_to(alpha, (size_y, LANES))
    own = jnp.concatenate([own] * (size_y // 8), axis=0)

    def body(x, carry):
        direction = direction_ref[x]
        pressure_ref[x] = alpha * direction
        preconditioned_ref[x] = direction - alpha * (applied_ref[x] + own)
        return carry

    lax.fori_loop(0, size_x, body, 0, unroll=2)


def cycle(value, axis, step):
    size = lax.axis_size(axis)
    return lax.ppermute(value, axis, [(i, (i + step) % size) for i in range(size)])


def exchange(value, axis, stride):
    size = lax.axis_size(axis)
    return lax.ppermute(value, axis, [(i, i ^ stride) for i in range(size)])


def doublings():
    steps = []
    for axis in ("gy", "gx", "gz"):
        strides = [1 << k for k in range(lax.axis_size(axis).bit_length() - 1)]
        steps += [(axis, stride) for stride in (strides[::-1] if axis == "gz" else strides)]
    return steps


def shards(sizes, right_side, coarse_inverse, sphere_rows, margin_block, margin_column):
    size_x, size_y, size_z = right_side.shape
    slabs, subdomains = coarse_inverse.shape
    records = sphere_rows.shape[0]
    halves = subdomains // LANES
    devices = sizes[0] * sizes[1] * sizes[2]
    wide_x, wide_y = size_x + 2 * REACH, size_y + 2 * REACH
    groups = wide_x // SUBS
    planes = wide_x + groups
    f32, bf16 = jnp.float32, jnp.bfloat16
    _, _, meta_at, meta_rows = message_rows(records, halves)
    shape = jax.ShapeDtypeStruct

    def call(kernel, out_shape, operands, scratch=()):
        many = isinstance(out_shape, tuple)
        return pl.pallas_call(
            kernel,
            out_shape=out_shape,
            in_specs=[VMEM] * len(operands),
            out_specs=tuple(VMEM for _ in out_shape) if many else VMEM,
            scratch_shapes=list(scratch),
        )(*operands)

    message = call(
        functools.partial(pack_kernel, sizes),
        shape((meta_at + meta_rows, LANES), bf16),
        (right_side, coarse_inverse, sphere_rows, margin_block.reshape(1, records), margin_column.reshape(1, records)),
        (pltpu.VMEM((8, LANES), f32),),
    )
    steps = doublings()
    held = message[None]
    received = exchange(held, *steps[0])
    first, last = right_side[:REACH], right_side[size_x - REACH :]
    if sizes[0] == 2:
        above = below = cycle(jnp.where(lax.axis_index("gx") == 0, last, first), "gx", 1)
    else:
        above, below = cycle(first, "gx", -1), cycle(last, "gx", 1)
    held, received, above, below = lax.optimization_barrier((held, received, above, below))
    held = jnp.concatenate([held, received], axis=0)
    received = exchange(held, *steps[1])
    pairs = shape((wide_x // 2, 8, LANES), f32)
    down, up = call(margin_y_kernel, (pairs, pairs), (right_side, above, below))
    after, before = cycle(down, "gy", -1), cycle(up, "gy", 1)
    held, received, after, before = lax.optimization_barrier((held, received, after, before))
    held = jnp.concatenate([held, received], axis=0)
    received = exchange(held, *steps[2])
    wide, edge = call(
        margin_z_kernel,
        (shape((wide_x, wide_y, LANES), f32), shape((groups, wide_y, LANES), f32)),
        (right_side, above, below, after, before),
    )
    held, received, edge = lax.optimization_barrier((held, received, edge))
    lower, upper = cycle(edge, "gz", 1), cycle(edge, "gz", -1)
    for step in steps[3:]:
        held = jnp.concatenate([held, received], axis=0)
        received = exchange(held, *step)

    half = devices // 2
    depth = min(half, 16) * LANES
    rows_all = 16 * pl.cdiv(groups * wide_y, 16)
    field = pltpu.VMEM((planes, wide_y, LANES), f32)
    kinds = pltpu.VMEM((5, wide_y, LANES), f32)
    block = shape((size_x, size_y, LANES), f32)
    direction, applied, stats = call(
        functools.partial(main_kernel, sizes, records, halves, slabs, size_x, size_y),
        (block, block, shape((devices, halves + 1, LANES), f32)),
        (held, received, wide, edge, lower, upper),
        (
            pltpu.VMEM((3, devices, LANES), f32),
            pltpu.VMEM((half, LANES), f32),
            pltpu.VMEM((2, LANES, LANES), f32),
            pltpu.VMEM((rows_all, depth), bf16),
            pltpu.VMEM((depth, (SUBS + 1) * LANES), bf16),
            pltpu.VMEM((rows_all, (SUBS + 1) * LANES), f32),
            field, field, field, field, field, field, field, kinds, kinds,
        ),
    )
    stats = lax.all_to_all(stats, AXES, 0, 0, tiled=True)
    return call(
        functools.partial(finish_kernel, sizes, records, halves, slabs),
        (block, block),
        (stats, held, received, direction, applied),
    )


def solution(mesh):
    placed = (
        P("gx", "gy", "gz"),
        P(("gx", "gy", "gz"), None),
        P(("gx", "gy", "gz"), None),
        P(("gx", "gy", "gz"), None),
        P(("gx", "gy", "gz")),
    )
    sizes = tuple(mesh.shape[axis] for axis in AXES)
    return jax.shard_map(
        functools.partial(shards, sizes),
        mesh=mesh,
        in_specs=placed,
        out_specs=(P("gx", "gy", "gz"), P("gx", "gy", "gz")),
        check_vma=False,
    )
```

time: 384 us -> 92.3 us (0.24)
  blocking collectives: 202 us -> 11.5 us
  starting transfers between devices: 66.5 us -> 13.1 us
  Pallas kernels: 0 us -> 45.3 us
  other arithmetic: 41.7 us -> 1.01 us
  local copies, waits for them, and re-layouts: 36.6 us -> 1.61 us
  waiting for transfers between devices: 32.2 us -> 18.8 us
    unnamed x4 -> x0, blocking collectives: 162 us -> none
    pallas_call x0 -> x5, Pallas kernels: none -> 45.3 us  [call(): pl.pallas_call(kernel, out_shape=out_shape, in_specs=[VMEM] * len(operand...]
    ppermute x24 -> x10, starting transfers between devices: 55.6 us -> 13.1 us  [the longest x5 8.26 us: cycle(): lax.ppermute(value, axis, [(i, (i + step) % size) for i in range(size)])]
    psum x1 -> x0, blocking collectives: 40 us -> none  [residual_inner(): return lax.psum(jnp.sum(residual * preconditioned), ('gx', 'gy', 'gz'))]
    add x2 -> x0, other arithmetic: 19.4 us -> none  [precondition(): chebyshev(residual, faces, diagonal) + coarse_part(residual, coarse_inverse)]
    slice x16 -> x0, local copies, waits for them, and re-layouts: 18.6 us -> none  [the longest x10 11.8 us: with_halo(): last = lax.slice_in_dim(value, length - width, length, axis=dim)]
    ppermute x8 -> x0, local copies, waits for them, and re-layouts: 12.5 us -> none  [the longest x4 6.29 us: with_halo(): before = lax.ppermute(last, axis, up)]
    all_to_all x0 -> x1, blocking collectives: none -> 11.5 us  [shards(): stats = lax.all_to_all(stats, AXES, 0, 0, tiled=True)]
  transfers between devices with their start and end apart: 26 -> 10, of which waited for: 11 -> 7; matrix products, arithmetic and copies ran while one was open for 4% -> 0% of each run, Pallas kernels for 0% -> 6%
where the time goes in v2:
time: 92.3 us; the launch traced here: 91.9 us
  Pallas kernels  45.3 us (49%)
  waiting for transfers between devices  18.8 us (20%)
  starting transfers between devices  13.1 us (14%)
  blocking collectives  11.5 us (12%)
  local copies, waits for them, and re-layouts  1.61 us (2%)
  other arithmetic  1.01 us (1%)
    pallas_call x5, Pallas kernels, call(): pl.pallas_call(kernel, out_shape=out_shape, in_specs=[VMEM] * len(operand...  45.3 us
    all_to_all x1, blocking collectives, shards(): stats = lax.all_to_all(stats, AXES, 0, 0, tiled=True)  11.5 us
    ppermute x5, waiting for transfers between devices, exchange(): return lax.ppermute(value, axis, [(i, i ^ stride) for i in range(size)])  11.2 us
    ppermute x5, starting transfers between devices, cycle(): lax.ppermute(value, axis, [(i, (i + step) % size) for i in range(size)])  8.26 us
    ppermute x5, waiting for transfers between devices, cycle(): lax.ppermute(value, axis, [(i, (i + step) % size) for i in range(size)])  7.58 us
    ppermute x5, starting transfers between devices, exchange(): return lax.ppermute(value, axis, [(i, i ^ stride) for i in range(size)])  4.84 us
  transfers between devices with their start and end apart: 10, of which 7 were waited for; matrix products, arithmetic and copies ran while one was open for 0% of the time, Pallas kernels for 6%

profile of v2, /device:TPU:0, one launch (start us, length us, event | category | flops | bytes accessed | tf_op | source)
XLA Modules:
  0.0 91.9 jit_solution(13721693340707251581)
XLA Ops:
  0.6 1.0 %slice_select_fusion = f32[4,64,128]{2,1,0:T(8,128)S(1)} fusion(f32[32,64,128]{2,1,0:T(8,128)} %residual_ref.5, pred[]{:T(512)S(6)} %eq.3), kind=kLoop, calls=%fused_computation.1 | loop fusion | flops 32768 | bytes 393217 | tf_op jit(solution)/shard_map/jit(_where)/select_n | solution.py:546
  1.6 3.0 %collective-permute-start.1 = (f32[4,64,128]{2,1,0:T(8,128)S(1)}, f32[4,64,128]{2,1,0:T(8,128)S(1)}, u32[]{:S(2)}, u32[]{:S(2)}) collective-permute-start(f32[4,64,128]{2,1,0:T(8,128)S(1)} %slice_select_fusion), channel_id=1, source_target_pairs={{0,16},{16,0},{1,17},{17,1},{2,18},{18,2},{3,19},{19,3},{4,20},{20... | collective-permute-start | bytes 393224 | tf_op jit(solution)/shard_map/ppermute | solution.py:496
  4.7 2.1 %shard_map.68 = bf16[96,128]{1,0:T(8,128)(2,1)} custom-call(f32[32,64,128]{2,1,0:T(8,128)} %residual_ref.5, f32[8,256]{1,0:T(8,128)} %inverse_ref.1, bf16[48,128]{1,0:T(8,128)(2,1)} %rows_ref.1, s32[1,48]{1,0:T(1,128)} %bitcast.5, s32[1,48]{1,0:T(1,128)} %bitcast.6), custom_call_target="tpu_custom_call" | custom-call | tf_op jit(solution)/shard_map/pallas_call | solution.py:527
  6.8 1.6 %collective-permute-start = (bf16[1,96,128]{2,1,0:T(8,128)(2,1)}, bf16[1,96,128]{2,1,0:T(8,128)(2,1)S(1)}, u32[]{:S(2)}, u32[]{:S(2)}) collective-permute-start(bf16[1,96,128]{2,1,0:T(8,128)(2,1)} %bitcast.3), channel_id=1, source_target_pairs={{0,4},{4,0},{8,12},{12,8},{1,5},{5,1},{9,13},{13,9},{2,6},{6,2},{1... | collective-permute-start | bytes 73736 | tf_op jit(solution)/shard_map/ppermute | solution.py:501
  8.4 2.5 %collective-permute-done = bf16[1,96,128]{2,1,0:T(8,128)(2,1)S(1)} collective-permute-done((bf16[1,96,128]{2,1,0:T(8,128)(2,1)}, bf16[1,96,128]{2,1,0:T(8,128)(2,1)S(1)}, u32[]{:S(2)}, u32[]{:S(2)}) %collective-permute-start) | collective-permute-done | bytes 24608 | tf_op jit(solution)/shard_map/ppermute | solution.py:501
  10.8 0.0 collective-permute-done.1.above_ref.below_ref
  10.8 0.0 copy-start
  10.8 0.7 constant_dynamic-update-slice_fusion.1
  11.6 0.0 copy-done
  11.6 2.0 %shard_map.69 = (f32[20,8,128]{2,1,0:T(8,128)}, f32[20,8,128]{2,1,0:T(8,128)}) custom-call(f32[32,64,128]{2,1,0:T(8,128)} %residual_ref.5, f32[4,64,128]{2,1,0:T(8,128)} %copy-done, f32[4,64,128]{2,1,0:T(8,128)} %copy-done), custom_call_target="tpu_custom_call" | custom-call | tf_op jit(solution)/shard_map/pallas_call | solution.py:527
  13.6 3.6 %collective-permute-start.3 = (f32[20,8,128]{2,1,0:T(8,128)}, f32[20,8,128]{2,1,0:T(8,128)S(1)}, u32[]{:S(2)}, u32[]{:S(2)}) collective-permute-start(f32[20,8,128]{2,1,0:T(8,128)} %get-tuple-element.24), channel_id=1, source_target_pairs={{0,12},{4,0},{8,4},{12,8},{1,13},{5,1},{9,5},{13,9},{2,14},{6,2},{... | collective-permute-start | bytes 245768 | tf_op jit(solution)/shard_map/ppermute | solution.py:496
  17.2 0.0 collective-permute-start.4
  17.2 1.0 %collective-permute-start.2 = (bf16[2,96,128]{2,1,0:T(8,128)(2,1)S(1)}, bf16[2,96,128]{2,1,0:T(8,128)(2,1)S(1)}, u32[]{:S(2)}, u32[]{:S(2)}) collective-permute-start(bf16[2,96,128]{2,1,0:T(8,128)(2,1)S(1)} %constant_dynamic-update-slice_fusion), channel_id=1, source_target_pairs={{0,8},{4,12},{8,0},{12,4},{1,9},{5,13},{9,1},{13,5},{2,10},{6,14},... | collective-permute-start | bytes 147464 | tf_op jit(solution)/shard_map/ppermute | solution.py:501
  18.2 4.0 %collective-permute-done.2 = bf16[2,96,128]{2,1,0:T(8,128)(2,1)S(1)} collective-permute-done((bf16[2,96,128]{2,1,0:T(8,128)(2,1)S(1)}, bf16[2,96,128]{2,1,0:T(8,128)(2,1)S(1)}, u32[]{:S(2)}, u32[]{:S(2)}) %collective-permute-start.2) | collective-permute-done | bytes 49184 | tf_op jit(solution)/shard_map/ppermute | solution.py:501
  22.3 0.0 collective-permute-done.3.after_ref
  22.3 0.0 copy-start.5
  22.3 1.4 %collective-permute-done.4.before_ref = f32[20,8,128]{2,1,0:T(8,128)S(1)} collective-permute-done((f32[20,8,128]{2,1,0:T(8,128)}, f32[20,8,128]{2,1,0:T(8,128)S(1)}, u32[]{:S(2)}, u32[]{:S(2)}) %collective-permute-start.4) | collective-permute-done | bytes 81952 | tf_op jit(solution)/shard_map/ppermute | solution.py:496
  23.6 0.0 copy-start.6
  23.7 0.6 collective-permute-start.5
  24.3 0.0 copy-done.5
  24.3 0.0 copy-done.6
  24.3 3.5 %shard_map.70 = (f32[40,72,128]{2,1,0:T(8,128)}, f32[5,72,128]{2,1,0:T(8,128)}) custom-call(f32[32,64,128]{2,1,0:T(8,128)} %residual_ref.5, f32[4,64,128]{2,1,0:T(8,128)} %copy-done, f32[4,64,128]{2,1,0:T(8,128)} %copy-done, f32[20,8,128]{2,1,0:T(8,128)} %copy-done.5, f32[20,8,128]{2,1,0:T(8,128)} %copy-done.6), custom_call_target="tpu_custom_call" | custom-call | tf_op jit(solution)/shard_map/pallas_call | solution.py:527
  27.8 0.6 collective-permute-done.5
  28.4 1.6 %collective-permute-start.6 = (bf16[8,96,128]{2,1,0:T(8,128)(2,1)S(1)}, bf16[8,96,128]{2,1,0:T(8,128)(2,1)S(1)}, u32[]{:S(2)}, u32[]{:S(2)}) collective-permute-start(bf16[8,96,128]{2,1,0:T(8,128)(2,1)S(1)} %pad_maximum_fusion), channel_id=1, source_target_pairs={{0,2},{1,3},{2,0},{3,1},{4,6},{5,7},{6,4},{7,5},{8,10},{9,11},{10,... | collective-permute-start | bytes 589832 | tf_op jit(solution)/shard_map/ppermute | solution.py:501
  30.0 4.1 %collective-permute-done.6 = bf16[8,96,128]{2,1,0:T(8,128)(2,1)S(1)} collective-permute-done((bf16[8,96,128]{2,1,0:T(8,128)(2,1)S(1)}, bf16[8,96,128]{2,1,0:T(8,128)(2,1)S(1)}, u32[]{:S(2)}, u32[]{:S(2)}) %collective-permute-start.6) | collective-permute-done | bytes 196640 | tf_op jit(solution)/shard_map/ppermute | solution.py:501
  34.1 0.0 copy-start.1
  34.1 0.1 collective-permute-start.7
  34.2 1.6 %collective-permute-start.9 = (f32[5,72,128]{2,1,0:T(8,128)}, f32[5,72,128]{2,1,0:T(8,128)S(1)}, u32[]{:S(2)}, u32[]{:S(2)}) collective-permute-start(f32[5,72,128]{2,1,0:T(8,128)} %get-tuple-element.34.edge_ref), channel_id=1, source_target_pairs={{0,3},{1,0},{2,1},{3,2},{4,7},{5,4},{6,5},{7,6},{8,11},{9,8},{10,9... | collective-permute-start | bytes 552968 | tf_op jit(solution)/shard_map/ppermute | solution.py:496
  35.8 0.0 collective-permute-start.8
  35.8 5.3 %collective-permute-done.9.upper_ref = f32[5,72,128]{2,1,0:T(8,128)S(1)} collective-permute-done((f32[5,72,128]{2,1,0:T(8,128)}, f32[5,72,128]{2,1,0:T(8,128)S(1)}, u32[]{:S(2)}, u32[]{:S(2)}) %collective-permute-start.9) | collective-permute-done | bytes 184352 | tf_op jit(solution)/shard_map/ppermute | solution.py:496
  41.1 0.0 copy-start.3
  41.1 0.9 %collective-permute-done.8.lower_ref = f32[5,72,128]{2,1,0:T(8,128)S(1)} collective-permute-done((f32[5,72,128]{2,1,0:T(8,128)}, f32[5,72,128]{2,1,0:T(8,128)S(1)}, u32[]{:S(2)}, u32[]{:S(2)}) %collective-permute-start.8) | collective-permute-done | bytes 184352 | tf_op jit(solution)/shard_map/ppermute | solution.py:496
  42.0 0.0 copy-start.4
  42.0 0.0 collective-permute-done.7.other_ref
  42.0 0.0 copy-start.2
  42.0 0.0 copy-done.1
  42.1 0.0 copy-done.3
  42.1 0.7 copy-done.4
  42.7 0.1 copy-done.2
  42.8 33.8 %shard_map.71 = (f32[32,64,128]{2,1,0:T(8,128)}, f32[32,64,128]{2,1,0:T(8,128)}, f32[32,3,128]{2,1,0:T(4,128)}) custom-call(bf16[16,96,128]{2,1,0:T(8,128)(2,1)} %copy-done.1, bf16[16,96,128]{2,1,0:T(8,128)(2,1)} %copy-done.2, f32[40,72,128]{2,1,0:T(8,128)} %get-tuple-element.33.wide_ref, f32[5,72,128]{2,1,0:T(8,128)} %get-tuple-element.34.edge_ref, ...), custom_call_target="tpu_custom_call" | custom-call | tf_op jit(solution)/shard_map/pallas_call | solution.py:527
  76.6 11.5 %all_to_all.5.stat_ref = f32[32,3,128]{2,1,0:T(4,128)} all-to-all(f32[32,3,128]{2,1,0:T(4,128)} %get-tuple-element.35), channel_id=1, replica_groups=mesh['gx'=2,'gy'=4,'gz'=4] {'gx','gy','gz'}, dimensions={0} | all-to-all | bytes 98304 | tf_op jit(solution)/shard_map/all_to_all | solution.py:589
  88.1 3.8 %shard_map.72 = (f32[32,64,128]{2,1,0:T(8,128)}, f32[32,64,128]{2,1,0:T(8,128)}) custom-call(f32[32,3,128]{2,1,0:T(4,128)} %all_to_all.5.stat_ref, bf16[16,96,128]{2,1,0:T(8,128)(2,1)} %copy-done.1, bf16[16,96,128]{2,1,0:T(8,128)(2,1)} %copy-done.2, f32[32,64,128]{2,1,0:T(8,128)} %get-tuple-element.36.direction_ref, f32[32,64,128]{2,1,0:T(8,128)} %get-tuple-element.37.applied_ref), custom_call_target="tpu_custom_call" | custom-call | tf_op jit(solution)/shard_map/pallas_call | solution.py:527
  (7 shorter events, 0.1 us)
Async XLA Ops:
  1.6 9.2 %collective-permute-start.1 = (f32[4,64,128]{2,1,0:T(8,128)S(1)}, f32[4,64,128]{2,1,0:T(8,128)S(1)}, u32[]{:S(2)}, u32[]{:S(2)}) collective-permute-start(f32[4,64,128]{2,1,0:T(8,128)S(1)} %slice_select_fusion), channel_id=1, source_target_pairs={{0,16},{16,0},{1,17},{17,1},{2,18},{18,2},{3,19},{19,3},{4,20},{20... | collective-permute-start | bytes 393224 | tf_op jit(solution)/shard_map/ppermute | solution.py:496
  6.8 4.0 %collective-permute-start = (bf16[1,96,128]{2,1,0:T(8,128)(2,1)}, bf16[1,96,128]{2,1,0:T(8,128)(2,1)S(1)}, u32[]{:S(2)}, u32[]{:S(2)}) collective-permute-start(bf16[1,96,128]{2,1,0:T(8,128)(2,1)} %bitcast.3), channel_id=1, source_target_pairs={{0,4},{4,0},{8,12},{12,8},{1,5},{5,1},{9,13},{13,9},{2,6},{6,2},{1... | collective-permute-start | bytes 73736 | tf_op jit(solution)/shard_map/ppermute | solution.py:501
  10.8 0.7 copy-start
  13.6 8.7 %collective-permute-start.3 = (f32[20,8,128]{2,1,0:T(8,128)}, f32[20,8,128]{2,1,0:T(8,128)S(1)}, u32[]{:S(2)}, u32[]{:S(2)}) collective-permute-start(f32[20,8,128]{2,1,0:T(8,128)} %get-tuple-element.24), channel_id=1, source_target_pairs={{0,12},{4,0},{8,4},{12,8},{1,13},{5,1},{9,5},{13,9},{2,14},{6,2},{... | collective-permute-start | bytes 245768 | tf_op jit(solution)/shard_map/ppermute | solution.py:496
  17.2 6.4 %collective-permute-start.4 = (f32[20,8,128]{2,1,0:T(8,128)}, f32[20,8,128]{2,1,0:T(8,128)S(1)}, u32[]{:S(2)}, u32[]{:S(2)}) collective-permute-start(f32[20,8,128]{2,1,0:T(8,128)} %get-tuple-element.25), channel_id=1, source_target_pairs={{0,4},{4,8},{8,12},{12,0},{1,5},{5,9},{9,13},{13,1},{2,6},{6,10},{... | collective-permute-start | bytes 245768 | tf_op jit(solution)/shard_map/ppermute | solution.py:496
  17.2 5.1 %collective-permute-start.2 = (bf16[2,96,128]{2,1,0:T(8,128)(2,1)S(1)}, bf16[2,96,128]{2,1,0:T(8,128)(2,1)S(1)}, u32[]{:S(2)}, u32[]{:S(2)}) collective-permute-start(bf16[2,96,128]{2,1,0:T(8,128)(2,1)S(1)} %constant_dynamic-update-slice_fusion), channel_id=1, source_target_pairs={{0,8},{4,12},{8,0},{12,4},{1,9},{5,13},{9,1},{13,5},{2,10},{6,14},... | collective-permute-start | bytes 147464 | tf_op jit(solution)/shard_map/ppermute | solution.py:501
  22.3 2.0 %copy-start.5 = (f32[20,8,128]{2,1,0:T(8,128)}, f32[20,8,128]{2,1,0:T(8,128)S(1)}, u32[]{:S(2)}) copy-start(f32[20,8,128]{2,1,0:T(8,128)S(1)} %collective-permute-done.3.after_ref) | copy-start | bytes 245764
  23.6 0.6 copy-start.6
  23.7 4.7 %collective-permute-start.5 = (bf16[4,96,128]{2,1,0:T(8,128)(2,1)S(1)}, bf16[4,96,128]{2,1,0:T(8,128)(2,1)S(1)}, u32[]{:S(2)}, u32[]{:S(2)}) collective-permute-start(bf16[4,96,128]{2,1,0:T(8,128)(2,1)S(1)} %constant_dynamic-update-slice_fusion.2), channel_id=1, source_target_pairs={{0,16},{16,0},{1,17},{17,1},{2,18},{18,2},{3,19},{19,3},{4,20},{20... | collective-permute-start | bytes 294920 | tf_op jit(solution)/shard_map/ppermute | solution.py:501
  28.4 5.7 %collective-permute-start.6 = (bf16[8,96,128]{2,1,0:T(8,128)(2,1)S(1)}, bf16[8,96,128]{2,1,0:T(8,128)(2,1)S(1)}, u32[]{:S(2)}, u32[]{:S(2)}) collective-permute-start(bf16[8,96,128]{2,1,0:T(8,128)(2,1)S(1)} %pad_maximum_fusion), channel_id=1, source_target_pairs={{0,2},{1,3},{2,0},{3,1},{4,6},{5,7},{6,4},{7,5},{8,10},{9,11},{10,... | collective-permute-start | bytes 589832 | tf_op jit(solution)/shard_map/ppermute | solution.py:501
  34.1 7.9 %copy-start.1 = (bf16[16,96,128]{2,1,0:T(8,128)(2,1)}, bf16[16,96,128]{2,1,0:T(8,128)(2,1)S(1)}, u32[]{:S(2)}) copy-start(bf16[16,96,128]{2,1,0:T(8,128)(2,1)S(1)} %constant_dynamic-update-slice_fusion.4.message_ref) | copy-start | bytes 1179652
  34.1 7.9 %collective-permute-start.7 = (bf16[16,96,128]{2,1,0:T(8,128)(2,1)S(1)}, bf16[16,96,128]{2,1,0:T(8,128)(2,1)S(1)}, u32[]{:S(2)}, u32[]{:S(2)}) collective-permute-start(bf16[16,96,128]{2,1,0:T(8,128)(2,1)S(1)} %constant_dynamic-update-slice_fusion.4.message_ref), channel_id=1, source_target_pairs={{0,1},{1,0},{2,3},{3,2},{4,5},{5,4},{6,7},{7,6},{8,9},{9,8},{10,11... | collective-permute-start | bytes 1179656 | tf_op jit(solution)/shard_map/ppermute | solution.py:501
  34.2 6.9 %collective-permute-start.9 = (f32[5,72,128]{2,1,0:T(8,128)}, f32[5,72,128]{2,1,0:T(8,128)S(1)}, u32[]{:S(2)}, u32[]{:S(2)}) collective-permute-start(f32[5,72,128]{2,1,0:T(8,128)} %get-tuple-element.34.edge_ref), channel_id=1, source_target_pairs={{0,3},{1,0},{2,1},{3,2},{4,7},{5,4},{6,5},{7,6},{8,11},{9,8},{10,9... | collective-permute-start | bytes 552968 | tf_op jit(solution)/shard_map/ppermute | solution.py:496
  35.8 6.2 %collective-permute-start.8 = (f32[5,72,128]{2,1,0:T(8,128)}, f32[5,72,128]{2,1,0:T(8,128)S(1)}, u32[]{:S(2)}, u32[]{:S(2)}) collective-permute-start(f32[5,72,128]{2,1,0:T(8,128)} %get-tuple-element.34.edge_ref), channel_id=1, source_target_pairs={{0,1},{1,2},{2,3},{3,0},{4,5},{5,6},{6,7},{7,4},{8,9},{9,10},{10,1... | collective-permute-start | bytes 552968 | tf_op jit(solution)/shard_map/ppermute | solution.py:496
  41.1 0.9 %copy-start.3 = (f32[5,72,128]{2,1,0:T(8,128)}, f32[5,72,128]{2,1,0:T(8,128)S(1)}, u32[]{:S(2)}) copy-start(f32[5,72,128]{2,1,0:T(8,128)S(1)} %collective-permute-done.9.upper_ref) | copy-start | bytes 552964
  42.0 0.7 copy-start.4
  42.0 0.8 copy-start.2

commit v3 on v2

--- a/solution.py
+++ b/solution.py
@@ -6,6 +6,7 @@
 from jax.experimental import pallas as pl
 from jax.experimental.pallas import tpu as pltpu
 from jax.sharding import PartitionSpec as P
+
 
 bound_low = 0.1
 bound_high = 2.0
@@ -96,48 +97,54 @@
     row = row_of(8)
 
     def plane(x, at):
-        tile = pl.ds(at, 8)
         if x < size_x:
-            return residual_ref[x, tile, :]
+            return residual_ref[x, pl.ds(at, 8), :]
         x -= size_x
-        return above_ref[x, tile, :] if x < REACH else below_ref[x - REACH, tile, :]
+        return above_ref[x, pl.ds(at, 8), :] if x < REACH else below_ref[x - REACH, pl.ds(at, 8), :]
 
     for pair in range((size_x + 2 * REACH) // 2):
-        one, two = 2 * pair, 2 * pair + 1
-        down_ref[pair] = jnp.where(row < 4, plane(one, 0), pltpu.roll(plane(two, 0), 4, 0))
-        up_ref[pair] = jnp.where(row < 4, pltpu.roll(plane(two, size_y - 8), 4, 0), plane(one, size_y - 8))
-
-
-def margin_z_kernel(residual_ref, above_ref, below_ref, after_ref, before_ref, wide_ref, edge_ref):
-    size_x, size_y, _ = residual_ref.shape
-    wide_y = size_y + 2 * REACH
+        low = [plane(2 * pair + k, 0) for k in range(2)]
+        high = [plane(2 * pair + k, size_y - 8) for k in range(2)]
+        down_ref[pair] = jnp.where(row < 4, low[0], pltpu.roll(low[1], 4, 0))
+        up_ref[pair] = jnp.where(row < 4, pltpu.roll(high[1], 4, 0), high[0])
+
+
+def edge_group(values):
+    rows = values[0].shape[0]
+    place, sub_of = lane_of(rows) % 16, lane_of(rows) // 16
+    edge = jnp.zeros((rows, LANES), jnp.float32)
+    for sub, value in enumerate(values):
+        first = pltpu.roll(value, (sub * 16 + 4) % LANES, 1)
+        last = pltpu.roll(value, (sub * 16 + 12) % LANES, 1)
+        edge = jnp.where((sub_of == sub) & (place >= 4) & (place < 8), first, edge)
+        edge = jnp.where((sub_of == sub) & (place >= 8) & (place < 12), last, edge)
+    return edge
+
+
+def edge_own_kernel(residual_ref, above_ref, below_ref, edge_ref):
+    groups = edge_ref.shape[0]
+
+    def group(g, carry):
+        edge_ref[g] = edge_group([residual_ref[g * SUBS + sub] for sub in range(SUBS)])
+        return carry
+
+    lax.fori_loop(0, groups - 1, group, 0)
+    edge_ref[groups - 1] = edge_group([ref[i] for ref in (above_ref, below_ref) for i in range(REACH)])
+
+
+def edge_tail_kernel(part_ref, after_ref, before_ref, tail_ref, edge_ref):
+    groups, size_y, _ = part_ref.shape
     row = row_of(8)
-    place = lane_of(wide_y) % 16
-    sub_of = lane_of(wide_y) // 16
-    for x in range(size_x + 2 * REACH):
-        if x < size_x:
-            wide_ref[x, 0:size_y, :] = residual_ref[x]
-        elif x < size_x + REACH:
-            wide_ref[x, 0:size_y, :] = above_ref[x - size_x]
-        else:
-            wide_ref[x, 0:size_y, :] = below_ref[x - size_x - REACH]
-        after, before = after_ref[x // 2], before_ref[x // 2]
-        if x % 2:
-            after, before = pltpu.roll(after, 4, 0), pltpu.roll(before, 4, 0)
-        wide_ref[x, size_y:wide_y, :] = jnp.where(row < 4, after, before)
-
-    def group(g, carry):
-        edge = jnp.zeros((wide_y, LANES), jnp.float32)
-        for sub in range(SUBS):
-            value = wide_ref[g * SUBS + sub]
-            first = pltpu.roll(value, (sub * 16 + 4) % LANES, 1)
-            last = pltpu.roll(value, (sub * 16 + 8 + 4) % LANES, 1)
-            edge = jnp.where((sub_of == sub) & (place >= 4) & (place < 8), first, edge)
-            edge = jnp.where((sub_of == sub) & (place >= 8) & (place < 12), last, edge)
-        edge_ref[g] = edge
-        return carry
-
-    lax.fori_loop(0, edge_ref.shape[0], group, 0)
+    for g in range(groups):
+        tails = []
+        for x in range(g * SUBS, g * SUBS + SUBS):
+            after, before = after_ref[x // 2], before_ref[x // 2]
+            if x % 2:
+                after, before = pltpu.roll(after, 4, 0), pltpu.roll(before, 4, 0)
+            tails.append(jnp.where(row < 4, after, before))
+            tail_ref[x] = tails[-1]
+        edge_ref[g, 0:size_y, :] = part_ref[g]
+        edge_ref[g, size_y:, :] = edge_group(tails)
 
 
 def coarse_solve(message_refs, high_at, low_at, halves, sums):
@@ -169,10 +176,10 @@
 
 def main_kernel(
     sizes, records, halves, slabs, size_x, size_y,
-    message_ref, other_ref, wide_ref, edge_ref, lower_ref, upper_ref,
+    message_ref, other_ref, residual_ref, above_ref, below_ref, tail_ref, edge_ref, lower_ref, upper_ref,
     direction_ref, applied_ref, stat_ref,
     key_ref, code_ref, turned_ref, left_ref, right_ref, added_ref,
-    density_ref, x_ref, y_ref, z_ref, h_ref, u_ref, d_ref, inside_ref, coarse_ref,
+    density_ref, x_ref, y_ref, z_ref, h_ref, u_ref, d_ref, inside_ref, coarse_ref, first_ref, second_ref, third_ref, fourth_ref,
 ):
     n_gx, n_gy, n_gz = sizes
     gx, gy, gz = (lax.axis_index(a) for a in AXES)
@@ -184,7 +191,6 @@
     lane = lane_of(wide_y)
     row = row_of(wide_y)
     place = lane % 16
-    sub_of = lane // 16
 
     def roll(value, shift, axis):
         return pltpu.roll(value, shift, axis)
@@ -297,9 +303,6 @@
             product = jnp.dot(left_ref[...], right_ref[:, columns], preferred_element_type=f32)
             added_ref[:, columns] = product if c == 0 else added_ref[:, columns] + product
 
-    def kind_of(x):
-        return jnp.where(x < size_x, 0, jnp.where(x < size_x + REACH, 1, 2))
-
     for g in range(groups):
         lines = slice(g * wide_y, (g + 1) * wide_y)
         for sub in range(SUBS):
@@ -309,31 +312,49 @@
         k = 3 if g < groups - 1 else 4
         density_ref[wide_x + g] = inside_ref[k] + added_ref[lines, SUBS * LANES :]
 
-    def z_after(value, edges, sub):
-        return jnp.where(lane == LANES - 1, roll(edges, 115 - 16 * sub, 1), roll(value, LANES - 1, 1))
-
-    def z_before(value, edges, sub):
-        return jnp.where(lane == 0, roll(edges, 125 - 16 * sub, 1), roll(value, 1, 1))
-
     def y_after(value):
         return roll(value, wide_y - 1, 0)
 
     def y_before(value):
         return roll(value, 1, 0)
 
-    def edge_x_after(ref, g):
-        other = ref[wide_x + (g + 1) % groups]
-        return jnp.where(lane >= LANES - 16, roll(other, LANES - 16, 1), roll(ref[wide_x + g], LANES - 16, 1))
-
-    def edge_x_before(ref, g):
-        other = ref[wide_x + (g - 1) % groups]
-        return jnp.where(lane < 16, roll(other, 16, 1), roll(ref[wide_x + g], 16, 1))
-
-    def following(x):
-        return jnp.where(x + 1 == wide_x, 0, x + 1)
-
-    def preceding(x):
-        return jnp.where(x == 0, wide_x - 1, x - 1)
+    def joined(after, before):
+        return jnp.where(place == 13, roll(before, 10, 1), after)
+
+    def z_after(value, edges):
+        return jnp.where(lane == LANES - 1, edges, roll(value, LANES - 1, 1))
+
+    def z_before(value, edges):
+        return jnp.where(lane == 0, edges, roll(value, 1, 1))
+
+    def edge_x_after(value, other):
+        return jnp.where(lane >= LANES - 16, roll(other, LANES - 16, 1), roll(value, LANES - 16, 1))
+
+    def edge_x_before(value, other):
+        return jnp.where(lane < 16, roll(other, 16, 1), roll(value, 16, 1))
+
+    def sweep(reach, body, carry, joined_ref, beside=None):
+        def turned(g, sub):
+            return roll(joined_ref[g], 115 - 16 * sub, 1)
+
+        for x in range(-reach, 0):
+            after = wide_x + x + 1 if x < -1 else 0
+            carry = body(wide_x + x, after, 2, turned(groups - 1, SUBS + x), carry)
+
+        def group(g, carry):
+            if beside:
+                beside(g, jnp.where(g == 0, groups - 1, g - 1), g + 1, 3)
+            for sub in range(SUBS):
+                x = g * SUBS + sub
+                carry = body(x, x + 1, 0, turned(g, sub), carry)
+            return carry
+
+        carry = lax.fori_loop(0, groups - 1, group, carry)
+        if beside:
+            beside(groups - 1, groups - 2, 0, 4)
+        for x in range(reach):
+            carry = body(size_x + x, size_x + x + 1, 1, turned(groups - 1, x), carry)
+        return carry
 
     def beta(one, two):
         return 2.0 / jnp.maximum(one + two, 0.5)
@@ -341,105 +362,96 @@
     for g in range(groups):
         j = wide_x + g
         value = density_ref[j]
-        x_ref[j] = beta(value, edge_x_after(density_ref, g))
+        x_ref[j] = beta(value, edge_x_after(value, density_ref[wide_x + (g + 1) % groups]))
         y_ref[j] = beta(value, y_after(value))
         z_ref[j] = beta(value, roll(value, LANES - 1, 1))
 
     for g in range(groups):
         j = wide_x + g
-        k = 3 if g < groups - 1 else 4
-        diagonal = x_ref[j] + edge_x_before(x_ref, g) + y_ref[j] + y_before(y_ref[j]) + z_ref[j] + roll(z_ref[j], 1, 1)
-        h_ref[j] = inside_ref[k] / diagonal
+        before_x = edge_x_before(x_ref[j], x_ref[wide_x + (g - 1) % groups])
+        diagonal = x_ref[j] + before_x + y_ref[j] + y_before(y_ref[j]) + z_ref[j] + roll(z_ref[j], 1, 1)
+        h = inside_ref[3 if g < groups - 1 else 4] / diagonal
+        h_ref[j] = h
         residual = edge_ref[g]
         residual = jnp.where(place < 4, roll(lower_ref[g], LANES - 8, 1), residual)
         residual = jnp.where(place >= 12, roll(upper_ref[g], 8, 1), residual)
-        u_ref[j] = residual * h_ref[j] * (1.0 / theta)
-
-    def faces(x, carry):
-        value = density_ref[x]
-        x_ref[x] = beta(value, density_ref[following(x)])
-        y_ref[x] = beta(value, y_after(value))
-        z_ref[x] = beta(value, z_after(value, density_ref[wide_x + x // SUBS], lax.rem(x, SUBS)))
-        return carry
-
-    lax.fori_loop(0, wide_x, faces, 0)
-
-    def scale(x, carry):
-        along_y, along_z = y_ref[x], z_ref[x]
-        diagonal = x_ref[x] + x_ref[preceding(x)] + along_y + y_before(along_y)
-        diagonal = diagonal + along_z + z_before(along_z, z_ref[wide_x + x // SUBS], lax.rem(x, SUBS))
-        h = inside_ref[kind_of(x)] / diagonal
-        h_ref[x] = h
-        u_ref[x] = wide_ref[x] * h * (1.0 / theta)
-        return carry
-
-    lax.fori_loop(0, wide_x, scale, 0)
-
-    def smooth(ref, x):
-        value, along_y, along_z = ref[x], y_ref[x], z_ref[x]
-        j, sub = wide_x + x // SUBS, lax.rem(x, SUBS)
-        before = preceding(x)
-        beside = x_ref[x] * ref[following(x)] + x_ref[before] * ref[before]
+        u_ref[j] = residual * h * (1.0 / theta)
+        first_ref[g] = joined(density_ref[j], z_ref[j])
+
+    def edge_direct(g, before_g, after_g, k):
+        j, before_j, after_j = wide_x + g, wide_x + before_g, wide_x + after_g
+        value, along_x, along_y, along_z = u_ref[j], x_ref[j], y_ref[j], z_ref[j]
+        product_z = along_z * value
+        beside = along_x * edge_x_after(value, u_ref[after_j])
+        beside = beside + edge_x_before(along_x * value, x_ref[before_j] * u_ref[before_j])
         beside = beside + along_y * y_after(value) + y_before(along_y * value)
-        beside = beside + along_z * z_after(value, ref[j], sub) + z_before(along_z * value, z_ref[j] * ref[j], sub)
-        return near * value + far * (h_ref[x] * beside)
-
-    def edge_smooth(ref, g):
-        j = wide_x + g
-        value = ref[j]
-        product = x_ref[j] * value
-        before = x_ref[wide_x + (g - 1) % groups] * ref[wide_x + (g - 1) % groups]
-        beside = x_ref[j] * edge_x_after(ref, g) + jnp.where(lane < 16, roll(before, 16, 1), roll(product, 16, 1))
-        beside = beside + y_ref[j] * y_after(value) + y_before(y_ref[j] * value)
-        beside = beside + z_ref[j] * roll(value, LANES - 1, 1) + roll(z_ref[j] * value, 1, 1)
-        return near * value + far * (h_ref[j] * beside)
-
-    for g in range(groups):
-        d_ref[wide_x + g] = edge_smooth(u_ref, g) + coarse_ref[3 if g < groups - 1 else 4]
-
-    def direct(x, carry):
-        d_ref[x] = smooth(u_ref, x) + coarse_ref[kind_of(x)]
-        return carry
-
-    lax.fori_loop(0, wide_x, direct, 0)
-
-    for g in range(groups):
-        j = wide_x + g
-        value = d_ref[j]
+        beside = beside + along_z * roll(value, LANES - 1, 1) + roll(product_z, 1, 1)
+        d_ref[j] = near * value + far * (h_ref[j] * beside) + coarse_ref[k]
+        second_ref[g] = joined(value, product_z)
+
+    def edge_image(g, before_g, after_g, k):
+        j, before_j, after_j = wide_x + g, wide_x + before_g, wide_x + after_g
+        value, before = d_ref[j], d_ref[before_j]
+        flux_x = x_ref[j] * (value - edge_x_after(value, d_ref[after_j]))
         flux_y = y_ref[j] * (value - y_after(value))
         flux_z = z_ref[j] * (value - roll(value, LANES - 1, 1))
-        image = x_ref[j] * (value - edge_x_after(d_ref, g))
-        image = image + edge_x_before(x_ref, g) * (value - edge_x_before(d_ref, g))
+        image = flux_x + edge_x_before(x_ref[j], x_ref[before_j]) * (value - edge_x_before(value, before))
         image = image + (flux_y - y_before(flux_y)) + (flux_z - roll(flux_z, 1, 1))
-        u_ref[j] = image * h_ref[j] * (1.0 / theta)
-
-    def image_of(x):
+        image = image * h_ref[j] * (1.0 / theta)
+        third_ref[g] = joined(value, flux_z)
+        fourth_ref[g] = joined(image, z_ref[j] * image)
+
+    def faces(x, after, k, edges, before):
+        value = density_ref[x]
+        along_x = beta(value, density_ref[after])
+        along_y = beta(value, y_after(value))
+        along_z = beta(value, z_after(value, edges))
+        diagonal = before + along_x + along_y + y_before(along_y) + along_z + z_before(along_z, edges)
+        h = inside_ref[k] / diagonal
+        x_ref[x], y_ref[x], z_ref[x], h_ref[x] = along_x, along_y, along_z, h
+        residual = (residual_ref, above_ref, below_ref)[k][x - (0, size_x, size_x + REACH)[k]]
+        u_ref[x, 0:size_y, :] = residual * h[0:size_y] * (1.0 / theta)
+        u_ref[x, size_y:wide_y, :] = tail_ref[x] * h[size_y:wide_y] * (1.0 / theta)
+        return along_x
+
+    sweep(REACH, faces, jnp.ones((wide_y, LANES), f32), first_ref, edge_direct)
+
+    def smooth(x, after, edges, before):
+        value, along_x, along_y, along_z = u_ref[x], x_ref[x], y_ref[x], z_ref[x]
+        beside = before + along_x * u_ref[after]
+        beside = beside + along_y * y_after(value) + y_before(along_y * value)
+        beside = beside + along_z * z_after(value, edges) + z_before(along_z * value, edges)
+        return near * value + far * (h_ref[x] * beside), along_x * value
+
+    def direct(x, after, k, edges, before):
+        value, product = smooth(x, after, edges, before)
+        d_ref[x] = value + coarse_ref[k]
+        return product
+
+    outer = wide_x - 3
+    sweep(2, direct, x_ref[outer] * u_ref[outer], second_ref, edge_image)
+
+    def image_of(x, after, k, edges, carry):
+        before, *found = carry
         value = d_ref[x]
-        j, sub = wide_x + x // SUBS, lax.rem(x, SUBS)
-        before = preceding(x)
-        edges = d_ref[j]
-        edge_flux = z_ref[j] * (edges - roll(edges, LANES - 1, 1))
+        flux_x = x_ref[x] * (value - d_ref[after])
         flux_y = y_ref[x] * (value - y_after(value))
-        flux_z = z_ref[x] * (value - z_after(value, edges, sub))
-        image = x_ref[x] * (value - d_ref[following(x)]) + x_ref[before] * (value - d_ref[before])
-        image = image + (flux_y - y_before(flux_y)) + (flux_z - z_before(flux_z, edge_flux, sub))
+        flux_z = z_ref[x] * (value - z_after(value, edges))
+        image = (flux_x - before) + (flux_y - y_before(flux_y)) + (flux_z - z_before(flux_z, edges))
         u_ref[x] = image * h_ref[x] * (1.0 / theta)
-        return value, image
-
-    def image_own(x, carry):
-        value, image = image_of(x)
-        value, image = value[0:size_y], image[0:size_y]
-        direction_ref[x] = value
-        return (
-            carry[0] + wide_ref[x, 0:size_y, :] * value,
-            carry[1] + value * image,
-            carry[2] + image,
-        )
-
-    zero = jnp.zeros((size_y, LANES), f32)
-    found = lax.fori_loop(0, size_x, image_own, (zero, zero, zero))
-    image_of(size_x)
-    image_of(wide_x - 1)
+        if k == 0:
+            value, image = value[0:size_y], image[0:size_y]
+            direction_ref[x] = value
+            parts = (residual_ref[x] * value, value * image, image)
+            found = [
+                total + sum(part[8 * i : 8 * i + 8] for i in range(size_y // 8))
+                for total, part in zip(found, parts)
+            ]
+        return (flux_x, *found)
+
+    outer = wide_x - 2
+    zero = jnp.zeros((8, LANES), f32)
+    _, *found = sweep(1, image_of, (x_ref[outer] * (d_ref[outer] - d_ref[outer + 1]), zero, zero, zero), third_ref)
 
     device = device_number(sizes)
     folded = [jnp.sum(f, axis=0, keepdims=True) for f in found]
@@ -457,11 +469,12 @@
 
     lax.fori_loop(0, stat_ref.shape[0], spread, 0, unroll=4)
 
-    def second(x, carry):
-        applied_ref[x] = smooth(u_ref, x)[0:size_y]
-        return carry
-
-    lax.fori_loop(0, size_x, second, 0)
+    def second(x, after, k, edges, before):
+        value, product = smooth(x, after, edges, before)
+        applied_ref[x] = value[0:size_y]
+        return product
+
+    sweep(0, second, x_ref[wide_x - 1] * u_ref[wide_x - 1], fourth_ref)
 
 
 def finish_kernel(
@@ -510,7 +523,7 @@
 
 
 def shards(sizes, right_side, coarse_inverse, sphere_rows, margin_block, margin_column):
-    size_x, size_y, size_z = right_side.shape
+    size_x, size_y, _ = right_side.shape
     slabs, subdomains = coarse_inverse.shape
     records = sphere_rows.shape[0]
     halves = subdomains // LANES
@@ -522,25 +535,30 @@
     _, _, meta_at, meta_rows = message_rows(records, halves)
     shape = jax.ShapeDtypeStruct
 
-    def call(kernel, out_shape, operands, scratch=()):
-        many = isinstance(out_shape, tuple)
+    def call(kernel, out_shape, operands, scratch=(), results=pltpu.VMEM, mib=8):
+        outs = [results(o.shape, o.dtype) for o in out_shape]
         return pl.pallas_call(
             kernel,
-            out_shape=out_shape,
+            out_shape=outs,
             in_specs=[VMEM] * len(operands),
-            out_specs=tuple(VMEM for _ in out_shape) if many else VMEM,
+            out_specs=[VMEM] * len(outs),
             scratch_shapes=list(scratch),
-        )(*operands)
-
-    message = call(
+            compiler_params=pltpu.CompilerParams(vmem_limit_bytes=mib << 20),
+        )(*(pltpu.with_memory_space_constraint(o, pltpu.VMEM) for o in operands))
+
+    (message,) = call(
         functools.partial(pack_kernel, sizes),
-        shape((meta_at + meta_rows, LANES), bf16),
+        (shape((meta_at + meta_rows, LANES), bf16),),
         (right_side, coarse_inverse, sphere_rows, margin_block.reshape(1, records), margin_column.reshape(1, records)),
         (pltpu.VMEM((8, LANES), f32),),
     )
     steps = doublings()
+
+    def join(k, held):
+        return exchange(held, *steps[k])
+
     held = message[None]
-    received = exchange(held, *steps[0])
+    received = join(0, held)
     first, last = right_side[:REACH], right_side[size_x - REACH :]
     if sizes[0] == 2:
         above = below = cycle(jnp.where(lax.axis_index("gx") == 0, last, first), "gx", 1)
@@ -548,34 +566,37 @@
         above, below = cycle(first, "gx", -1), cycle(last, "gx", 1)
     held, received, above, below = lax.optimization_barrier((held, received, above, below))
     held = jnp.concatenate([held, received], axis=0)
-    received = exchange(held, *steps[1])
+    received = join(1, held)
     pairs = shape((wide_x // 2, 8, LANES), f32)
     down, up = call(margin_y_kernel, (pairs, pairs), (right_side, above, below))
-    after, before = cycle(down, "gy", -1), cycle(up, "gy", 1)
+    after = cycle(down, "gy", -1)
+    before = cycle(up, "gy", 1)
+    (part,) = call(edge_own_kernel, (shape((groups, size_y, LANES), f32),), (right_side, above, below))
     held, received, after, before = lax.optimization_barrier((held, received, after, before))
     held = jnp.concatenate([held, received], axis=0)
-    received = exchange(held, *steps[2])
-    wide, edge = call(
-        margin_z_kernel,
-        (shape((wide_x, wide_y, LANES), f32), shape((groups, wide_y, LANES), f32)),
-        (right_side, above, below, after, before),
-    )
-    held, received, edge = lax.optimization_barrier((held, received, edge))
-    lower, upper = cycle(edge, "gz", 1), cycle(edge, "gz", -1)
-    for step in steps[3:]:
+    received = join(2, held)
+    tail, edge = call(
+        edge_tail_kernel,
+        (shape((wide_x, 8, LANES), f32), shape((groups, wide_y, LANES), f32)),
+        (part, after, before),
+    )
+    lower = cycle(edge, "gz", 1)
+    upper = cycle(edge, "gz", -1)
+    for k in range(3, len(steps)):
         held = jnp.concatenate([held, received], axis=0)
-        received = exchange(held, *step)
+        received = join(k, held)
 
     half = devices // 2
     depth = min(half, 16) * LANES
     rows_all = 16 * pl.cdiv(groups * wide_y, 16)
     field = pltpu.VMEM((planes, wide_y, LANES), f32)
+    margin = pltpu.VMEM((groups, wide_y, LANES), f32)
     kinds = pltpu.VMEM((5, wide_y, LANES), f32)
     block = shape((size_x, size_y, LANES), f32)
     direction, applied, stats = call(
         functools.partial(main_kernel, sizes, records, halves, slabs, size_x, size_y),
         (block, block, shape((devices, halves + 1, LANES), f32)),
-        (held, received, wide, edge, lower, upper),
+        (held, received, right_side, above, below, tail, edge, lower, upper),
         (
             pltpu.VMEM((3, devices, LANES), f32),
             pltpu.VMEM((half, LANES), f32),
@@ -584,13 +605,16 @@
             pltpu.VMEM((depth, (SUBS + 1) * LANES), bf16),
             pltpu.VMEM((rows_all, (SUBS + 1) * LANES), f32),
             field, field, field, field, field, field, field, kinds, kinds,
+            margin, margin, margin, margin,
         ),
+        mib=28,
     )
     stats = lax.all_to_all(stats, AXES, 0, 0, tiled=True)
     return call(
         functools.partial(finish_kernel, sizes, records, halves, slabs),
         (block, block),
         (stats, held, received, direction, applied),
+        results=shape,
     )
 
 
@@ -603,8 +627,12 @@
         P(("gx", "gy", "gz")),
     )
     sizes = tuple(mesh.shape[axis] for axis in AXES)
+
+    def body(*operands):
+        return shards(sizes, *operands)
+
     return jax.shard_map(
-        functools.partial(shards, sizes),
+        body,
         mesh=mesh,
         in_specs=placed,
         out_specs=(P("gx", "gy", "gz"), P("gx", "gy", "gz")),

time: 92.3 us -> 70 us (0.76)
  Pallas kernels: 45.3 us -> 20.2 us
  waiting for transfers between devices: 18.8 us -> 21.7 us
    pallas_call x5 -> x6, Pallas kernels: 45.3 us -> 20.2 us  [call(): pl.pallas_call(kernel, out_shape=outs, in_specs=[VMEM] * len(operands), o...]
    ppermute x5, waiting for transfers between devices: 11.2 us -> 14.5 us  [exchange(): return lax.ppermute(value, axis, [(i, i ^ stride) for i in range(size)])]
    unnamed x18 -> x16, local copies, waits for them, and re-layouts: 1.57 us -> 1.93 us
  transfers between devices with their start and end apart: 10 -> 10, of which waited for: 7 -> 7; matrix products, arithmetic and copies ran while one was open for 0% -> 0% of each run, Pallas kernels for 6% -> 2%
where the time goes in v3:
time: 70 us; the launch traced here: 69.8 us
  waiting for transfers between devices  21.7 us (31%)
  Pallas kernels  20.2 us (29%)
  starting transfers between devices  13.2 us (19%)
  blocking collectives  11 us (16%)
  local copies, waits for them, and re-layouts  1.97 us (3%)
  other arithmetic  1.03 us (1%)
  between operations  0.73 us (1%)
    pallas_call x6, Pallas kernels, call(): pl.pallas_call(kernel, out_shape=outs, in_specs=[VMEM] * len(operands), o...  20.2 us
    ppermute x5, waiting for transfers between devices, exchange(): return lax.ppermute(value, axis, [(i, i ^ stride) for i in range(size)])  14.5 us
    all_to_all x1, blocking collectives, shards(): stats = lax.all_to_all(stats, AXES, 0, 0, tiled=True)  11 us
    ppermute x5, starting transfers between devices, cycle(): lax.ppermute(value, axis, [(i, (i + step) % size) for i in range(size)])  8.36 us
    ppermute x5, waiting for transfers between devices, cycle(): lax.ppermute(value, axis, [(i, (i + step) % size) for i in range(size)])  7.16 us
    ppermute x5, starting transfers between devices, exchange(): return lax.ppermute(value, axis, [(i, i ^ stride) for i in range(size)])  4.84 us
    unnamed x16, local copies, waits for them, and re-layouts  1.93 us
  transfers between devices with their start and end apart: 10, of which 7 were waited for; matrix products, arithmetic and copies ran while one was open for 0% of the time, Pallas kernels for 2%

profile of v3, /device:TPU:0, one launch (start us, length us, event | category | flops | bytes accessed | tf_op | source)
XLA Modules:
  0.0 69.8 jit_solution(488428311814415170)
XLA Ops:
  0.6 0.0 copy-start.2
  0.6 0.0 copy-start.3
  0.7 1.0 %slice_select_fusion = f32[4,64,128]{2,1,0:T(8,128)S(1)} fusion(f32[32,64,128]{2,1,0:T(8,128)} %residual_ref.7, pred[]{:T(512)S(6)} %eq.3), kind=kLoop, calls=%fused_computation.1 | loop fusion | flops 32768 | bytes 393217 | tf_op jit(solution)/shard_map/jit(_where)/select_n | solution.py:564
  1.7 3.0 %collective-permute-start.1 = (f32[4,64,128]{2,1,0:T(8,128)S(1)}, f32[4,64,128]{2,1,0:T(8,128)S(1)}, u32[]{:S(2)}, u32[]{:S(2)}) collective-permute-start(f32[4,64,128]{2,1,0:T(8,128)S(1)} %slice_select_fusion), channel_id=1, source_target_pairs={{0,16},{16,0},{1,17},{17,1},{2,18},{18,2},{3,19},{19,3},{4,20},{20... | collective-permute-start | bytes 393224 | tf_op jit(solution)/shard_map/ppermute | solution.py:509
  4.7 0.0 copy-start.4
  4.7 0.0 copy-start.5
  4.7 0.0 copy-done.2
  4.7 0.0 copy-done.3
  4.7 0.6 copy-done.4
  5.3 0.0 copy-done.5
  5.4 0.0 copy-start
  5.4 1.2 %copy-done = f32[32,64,128]{2,1,0:T(8,128)S(1)} copy-done((f32[32,64,128]{2,1,0:T(8,128)S(1)}, f32[32,64,128]{2,1,0:T(8,128)}, u32[]{:S(2)}) %copy-start) | copy-done | bytes 1048600
  6.6 0.0 copy-start.1
  6.6 0.3 shard_map.68
  6.9 1.6 %collective-permute-start = (bf16[1,96,128]{2,1,0:T(8,128)(2,1)S(1)}, bf16[1,96,128]{2,1,0:T(8,128)(2,1)S(1)}, u32[]{:S(2)}, u32[]{:S(2)}) collective-permute-start(bf16[1,96,128]{2,1,0:T(8,128)(2,1)S(1)} %bitcast.3), channel_id=1, source_target_pairs={{0,4},{4,0},{8,12},{12,8},{1,5},{5,1},{9,13},{13,9},{2,6},{6,2},{1... | collective-permute-start | bytes 73736 | tf_op jit(solution)/shard_map/ppermute | solution.py:514
  8.4 2.2 %collective-permute-done = bf16[1,96,128]{2,1,0:T(8,128)(2,1)S(1)} collective-permute-done((bf16[1,96,128]{2,1,0:T(8,128)(2,1)S(1)}, bf16[1,96,128]{2,1,0:T(8,128)(2,1)S(1)}, u32[]{:S(2)}, u32[]{:S(2)}) %collective-permute-start) | collective-permute-done | bytes 24608 | tf_op jit(solution)/shard_map/ppermute | solution.py:514
  10.7 0.0 collective-permute-done.1.above_ref.below_ref
  10.7 0.0 copy-done.1
  10.7 3.7 %collective-permute-start.3 = (f32[20,8,128]{2,1,0:T(8,128)S(1)}, f32[20,8,128]{2,1,0:T(8,128)S(1)}, u32[]{:S(2)}, u32[]{:S(2)}) collective-permute-start(f32[20,8,128]{2,1,0:T(8,128)S(1)} %get-tuple-element.21), channel_id=1, source_target_pairs={{0,12},{4,0},{8,4},{12,8},{1,13},{5,1},{9,5},{13,9},{2,14},{6,2},{... | collective-permute-start | bytes 245768 | tf_op jit(solution)/shard_map/ppermute | solution.py:509
  14.4 0.0 collective-permute-start.4
  14.4 1.0 %collective-permute-start.2 = (bf16[2,96,128]{2,1,0:T(8,128)(2,1)S(1)}, bf16[2,96,128]{2,1,0:T(8,128)(2,1)S(1)}, u32[]{:S(2)}, u32[]{:S(2)}) collective-permute-start(bf16[2,96,128]{2,1,0:T(8,128)(2,1)S(1)} %constant_dynamic-update-slice_fusion), channel_id=1, source_target_pairs={{0,8},{4,12},{8,0},{12,4},{1,9},{5,13},{9,1},{13,5},{2,10},{6,14},... | collective-permute-start | bytes 147464 | tf_op jit(solution)/shard_map/ppermute | solution.py:514
  15.4 4.0 %collective-permute-done.2 = bf16[2,96,128]{2,1,0:T(8,128)(2,1)S(1)} collective-permute-done((bf16[2,96,128]{2,1,0:T(8,128)(2,1)S(1)}, bf16[2,96,128]{2,1,0:T(8,128)(2,1)S(1)}, u32[]{:S(2)}, u32[]{:S(2)}) %collective-permute-start.2) | collective-permute-done | bytes 49184 | tf_op jit(solution)/shard_map/ppermute | solution.py:514
  19.5 0.0 collective-permute-done.3.after_ref
  19.5 1.2 %collective-permute-done.4.before_ref = f32[20,8,128]{2,1,0:T(8,128)S(1)} collective-permute-done((f32[20,8,128]{2,1,0:T(8,128)S(1)}, f32[20,8,128]{2,1,0:T(8,128)S(1)}, u32[]{:S(2)}, u32[]{:S(2)}) %collective-permute-start.4) | collective-permute-done | bytes 81952 | tf_op jit(solution)/shard_map/ppermute | solution.py:509
  20.6 0.6 collective-permute-start.5
  21.3 4.1 %collective-permute-done.5 = bf16[4,96,128]{2,1,0:T(8,128)(2,1)S(1)} collective-permute-done((bf16[4,96,128]{2,1,0:T(8,128)(2,1)S(1)}, bf16[4,96,128]{2,1,0:T(8,128)(2,1)S(1)}, u32[]{:S(2)}, u32[]{:S(2)}) %collective-permute-start.5) | collective-permute-done | bytes 98336 | tf_op jit(solution)/shard_map/ppermute | solution.py:514
  25.4 1.6 %collective-permute-start.6 = (bf16[8,96,128]{2,1,0:T(8,128)(2,1)S(1)}, bf16[8,96,128]{2,1,0:T(8,128)(2,1)S(1)}, u32[]{:S(2)}, u32[]{:S(2)}) collective-permute-start(bf16[8,96,128]{2,1,0:T(8,128)(2,1)S(1)} %pad_maximum_fusion), channel_id=1, source_target_pairs={{0,2},{1,3},{2,0},{3,1},{4,6},{5,7},{6,4},{7,5},{8,10},{9,11},{10,... | collective-permute-start | bytes 589832 | tf_op jit(solution)/shard_map/ppermute | solution.py:514
  27.0 4.1 %collective-permute-done.6 = bf16[8,96,128]{2,1,0:T(8,128)(2,1)S(1)} collective-permute-done((bf16[8,96,128]{2,1,0:T(8,128)(2,1)S(1)}, bf16[8,96,128]{2,1,0:T(8,128)(2,1)S(1)}, u32[]{:S(2)}, u32[]{:S(2)}) %collective-permute-start.6) | collective-permute-done | bytes 196640 | tf_op jit(solution)/shard_map/ppermute | solution.py:514
  31.1 0.1 collective-permute-start.7
  31.2 1.0 %shard_map.70.part_ref = f32[5,64,128]{2,1,0:T(8,128)S(1)} custom-call(f32[32,64,128]{2,1,0:T(8,128)S(1)} %copy-done.1, f32[4,64,128]{2,1,0:T(8,128)S(1)} %collective-permute-done.1.above_ref.below_ref, f32[4,64,128]{2,1,0:T(8,128)S(1)} %collective-permute-done.1.above_ref.below_ref), custom_call_target="tpu_custom_call" | custom-call | tf_op jit(solution)/shard_map/pallas_call | solution.py:540
  32.2 0.2 shard_map.71
  32.4 1.7 %collective-permute-start.9 = (f32[5,72,128]{2,1,0:T(8,128)S(1)}, f32[5,72,128]{2,1,0:T(8,128)S(1)}, u32[]{:S(2)}, u32[]{:S(2)}) collective-permute-start(f32[5,72,128]{2,1,0:T(8,128)S(1)} %get-tuple-element.28.edge_ref), channel_id=1, source_target_pairs={{0,3},{1,0},{2,1},{3,2},{4,7},{5,4},{6,5},{7,6},{8,11},{9,8},{10,9... | collective-permute-start | bytes 552968 | tf_op jit(solution)/shard_map/ppermute | solution.py:509
  34.0 0.0 collective-permute-start.8
  34.0 5.0 %collective-permute-done.9.upper_ref = f32[5,72,128]{2,1,0:T(8,128)S(1)} collective-permute-done((f32[5,72,128]{2,1,0:T(8,128)S(1)}, f32[5,72,128]{2,1,0:T(8,128)S(1)}, u32[]{:S(2)}, u32[]{:S(2)}) %collective-permute-start.9) | collective-permute-done | bytes 184352 | tf_op jit(solution)/shard_map/ppermute | solution.py:509
  39.0 1.0 %collective-permute-done.8.lower_ref = f32[5,72,128]{2,1,0:T(8,128)S(1)} collective-permute-done((f32[5,72,128]{2,1,0:T(8,128)S(1)}, f32[5,72,128]{2,1,0:T(8,128)S(1)}, u32[]{:S(2)}, u32[]{:S(2)}) %collective-permute-start.8) | collective-permute-done | bytes 184352 | tf_op jit(solution)/shard_map/ppermute | solution.py:509
  40.0 0.0 collective-permute-done.7.other_ref
  40.0 16.8 %shard_map.72 = (f32[32,64,128]{2,1,0:T(8,128)S(1)}, f32[32,64,128]{2,1,0:T(8,128)S(1)}, f32[32,3,128]{2,1,0:T(4,128)S(1)}) custom-call(bf16[16,96,128]{2,1,0:T(8,128)(2,1)S(1)} %constant_dynamic-update-slice_fusion.2.message_ref, bf16[16,96,128]{2,1,0:T(8,128)(2,1)S(1)} %collective-permute-done.7.other_ref, f32[32,64,128]{2,1,0:T(8,128)S(1)} %copy-done.1, ...), custom_call_target="tpu_custom_call" | custom-call | tf_op jit(solution)/shard_map/pallas_call | solution.py:540
  56.8 11.0 %all_to_all.5.stat_ref = f32[32,3,128]{2,1,0:T(4,128)S(1)} all-to-all(f32[32,3,128]{2,1,0:T(4,128)S(1)} %get-tuple-element.29), channel_id=1, replica_groups=mesh['gx'=2,'gy'=4,'gz'=4] {'gx','gy','gz'}, dimensions={0} | all-to-all | bytes 98304 | tf_op jit(solution)/shard_map/all_to_all | solution.py:612
  67.8 2.0 %shard_map.73 = (f32[32,64,128]{2,1,0:T(8,128)}, f32[32,64,128]{2,1,0:T(8,128)}) custom-call(f32[32,3,128]{2,1,0:T(4,128)S(1)} %all_to_all.5.stat_ref, bf16[16,96,128]{2,1,0:T(8,128)(2,1)S(1)} %constant_dynamic-update-slice_fusion.2.message_ref, bf16[16,96,128]{2,1,0:T(8,128)(2,1)S(1)} %collective-permute-done.7.other_ref, ...), custom_call_target="tpu_custom_call" | custom-call | tf_op jit(solution)/shard_map/pallas_call | solution.py:540
  (9 shorter events, 0.1 us)
Async XLA Ops:
  0.6 4.1 %copy-start.2 = (bf16[48,128]{1,0:T(8,128)(2,1)S(1)}, bf16[48,128]{1,0:T(8,128)(2,1)}, u32[]{:S(2)}) copy-start(bf16[48,128]{1,0:T(8,128)(2,1)} %rows_ref.1) | copy-start | bytes 36868
  0.6 4.0 %copy-start.3 = (f32[8,256]{1,0:T(8,128)S(1)}, f32[8,256]{1,0:T(8,128)}, u32[]{:S(2)}) copy-start(f32[8,256]{1,0:T(8,128)} %inverse_ref.1) | copy-start | bytes 24580
  1.7 9.0 %collective-permute-start.1 = (f32[4,64,128]{2,1,0:T(8,128)S(1)}, f32[4,64,128]{2,1,0:T(8,128)S(1)}, u32[]{:S(2)}, u32[]{:S(2)}) collective-permute-start(f32[4,64,128]{2,1,0:T(8,128)S(1)} %slice_select_fusion), channel_id=1, source_target_pairs={{0,16},{16,0},{1,17},{17,1},{2,18},{18,2},{3,19},{19,3},{4,20},{20... | collective-permute-start | bytes 393224 | tf_op jit(solution)/shard_map/ppermute | solution.py:509
  4.7 0.7 copy-start.4
  4.7 0.7 copy-start.5
  5.4 1.2 %copy-start = (f32[32,64,128]{2,1,0:T(8,128)S(1)}, f32[32,64,128]{2,1,0:T(8,128)}, u32[]{:S(2)}) copy-start(f32[32,64,128]{2,1,0:T(8,128)} %residual_ref.7) | copy-start | bytes 3145732
  6.6 4.1 %copy-start.1 = (f32[32,64,128]{2,1,0:T(8,128)S(1)}, f32[32,64,128]{2,1,0:T(8,128)}, u32[]{:S(2)}) copy-start(f32[32,64,128]{2,1,0:T(8,128)} %residual_ref.7) | copy-start | bytes 3145732
  6.9 3.8 %collective-permute-start = (bf16[1,96,128]{2,1,0:T(8,128)(2,1)S(1)}, bf16[1,96,128]{2,1,0:T(8,128)(2,1)S(1)}, u32[]{:S(2)}, u32[]{:S(2)}) collective-permute-start(bf16[1,96,128]{2,1,0:T(8,128)(2,1)S(1)} %bitcast.3), channel_id=1, source_target_pairs={{0,4},{4,0},{8,12},{12,8},{1,5},{5,1},{9,13},{13,9},{2,6},{6,2},{1... | collective-permute-start | bytes 73736 | tf_op jit(solution)/shard_map/ppermute | solution.py:514
  10.7 8.7 %collective-permute-start.3 = (f32[20,8,128]{2,1,0:T(8,128)S(1)}, f32[20,8,128]{2,1,0:T(8,128)S(1)}, u32[]{:S(2)}, u32[]{:S(2)}) collective-permute-start(f32[20,8,128]{2,1,0:T(8,128)S(1)} %get-tuple-element.21), channel_id=1, source_target_pairs={{0,12},{4,0},{8,4},{12,8},{1,13},{5,1},{9,5},{13,9},{2,14},{6,2},{... | collective-permute-start | bytes 245768 | tf_op jit(solution)/shard_map/ppermute | solution.py:509
  14.4 6.2 %collective-permute-start.4 = (f32[20,8,128]{2,1,0:T(8,128)S(1)}, f32[20,8,128]{2,1,0:T(8,128)S(1)}, u32[]{:S(2)}, u32[]{:S(2)}) collective-permute-start(f32[20,8,128]{2,1,0:T(8,128)S(1)} %get-tuple-element.22), channel_id=1, source_target_pairs={{0,4},{4,8},{8,12},{12,0},{1,5},{5,9},{9,13},{13,1},{2,6},{6,10},{... | collective-permute-start | bytes 245768 | tf_op jit(solution)/shard_map/ppermute | solution.py:509
  14.4 5.1 %collective-permute-start.2 = (bf16[2,96,128]{2,1,0:T(8,128)(2,1)S(1)}, bf16[2,96,128]{2,1,0:T(8,128)(2,1)S(1)}, u32[]{:S(2)}, u32[]{:S(2)}) collective-permute-start(bf16[2,96,128]{2,1,0:T(8,128)(2,1)S(1)} %constant_dynamic-update-slice_fusion), channel_id=1, source_target_pairs={{0,8},{4,12},{8,0},{12,4},{1,9},{5,13},{9,1},{13,5},{2,10},{6,14},... | collective-permute-start | bytes 147464 | tf_op jit(solution)/shard_map/ppermute | solution.py:514
  20.6 4.7 %collective-permute-start.5 = (bf16[4,96,128]{2,1,0:T(8,128)(2,1)S(1)}, bf16[4,96,128]{2,1,0:T(8,128)(2,1)S(1)}, u32[]{:S(2)}, u32[]{:S(2)}) collective-permute-start(bf16[4,96,128]{2,1,0:T(8,128)(2,1)S(1)} %pad_maximum_fusion.1), channel_id=1, source_target_pairs={{0,16},{16,0},{1,17},{17,1},{2,18},{18,2},{3,19},{19,3},{4,20},{20... | collective-permute-start | bytes 294920 | tf_op jit(solution)/shard_map/ppermute | solution.py:514
  25.4 5.7 %collective-permute-start.6 = (bf16[8,96,128]{2,1,0:T(8,128)(2,1)S(1)}, bf16[8,96,128]{2,1,0:T(8,128)(2,1)S(1)}, u32[]{:S(2)}, u32[]{:S(2)}) collective-permute-start(bf16[8,96,128]{2,1,0:T(8,128)(2,1)S(1)} %pad_maximum_fusion), channel_id=1, source_target_pairs={{0,2},{1,3},{2,0},{3,1},{4,6},{5,7},{6,4},{7,5},{8,10},{9,11},{10,... | collective-permute-start | bytes 589832 | tf_op jit(solution)/shard_map/ppermute | solution.py:514
  31.1 8.9 %collective-permute-start.7 = (bf16[16,96,128]{2,1,0:T(8,128)(2,1)S(1)}, bf16[16,96,128]{2,1,0:T(8,128)(2,1)S(1)}, u32[]{:S(2)}, u32[]{:S(2)}) collective-permute-start(bf16[16,96,128]{2,1,0:T(8,128)(2,1)S(1)} %constant_dynamic-update-slice_fusion.2.message_ref), channel_id=1, source_target_pairs={{0,1},{1,0},{2,3},{3,2},{4,5},{5,4},{6,7},{7,6},{8,9},{9,8},{10,11... | collective-permute-start | bytes 1179656 | tf_op jit(solution)/shard_map/ppermute | solution.py:514
  32.4 6.6 %collective-permute-start.9 = (f32[5,72,128]{2,1,0:T(8,128)S(1)}, f32[5,72,128]{2,1,0:T(8,128)S(1)}, u32[]{:S(2)}, u32[]{:S(2)}) collective-permute-start(f32[5,72,128]{2,1,0:T(8,128)S(1)} %get-tuple-element.28.edge_ref), channel_id=1, source_target_pairs={{0,3},{1,0},{2,1},{3,2},{4,7},{5,4},{6,5},{7,6},{8,11},{9,8},{10,9... | collective-permute-start | bytes 552968 | tf_op jit(solution)/shard_map/ppermute | solution.py:509
  34.0 6.0 %collective-permute-start.8 = (f32[5,72,128]{2,1,0:T(8,128)S(1)}, f32[5,72,128]{2,1,0:T(8,128)S(1)}, u32[]{:S(2)}, u32[]{:S(2)}) collective-permute-start(f32[5,72,128]{2,1,0:T(8,128)S(1)} %get-tuple-element.28.edge_ref), channel_id=1, source_target_pairs={{0,1},{1,2},{2,3},{3,0},{4,5},{5,6},{6,7},{7,4},{8,9},{9,10},{10,1... | collective-permute-start | bytes 552968 | tf_op jit(solution)/shard_map/ppermute | solution.py:509

commit v4 on v3

--- a/solution.py
+++ b/solution.py
@@ -20,6 +20,7 @@
 AXES = ("gx", "gy", "gz")
 LANES = 128
 REACH = 4
+DEEP = 3
 SUBS = 8
 SLOT = 64
 EXACT = lax.Precision.HIGHEST
@@ -32,6 +33,11 @@
 
 def row_of(rows):
     return lax.broadcasted_iota(jnp.int32, (rows, LANES), 0)
+
+
+def by_parity(axis, one, two):
+    even = lax.axis_index(axis) % 2 == 0
+    return jnp.where(even, one, two), jnp.where(even, two, one)
 
 
 def message_rows(records, halves):
@@ -53,13 +59,20 @@
     return (lax.axis_index("gx") * sizes[1] + lax.axis_index("gy")) * sizes[2] + lax.axis_index("gz")
 
 
-def pack_kernel(sizes, residual_ref, inverse_ref, rows_ref, block_ref, column_ref, out_ref, index_ref):
+def pack_kernel(sizes, residual_ref, inverse_ref, rows_ref, block_ref, column_ref, out_ref, *rest):
+    *margin_refs, index_ref = rest
     size_x, size_y, _ = residual_ref.shape
     slabs, subdomains = inverse_ref.shape
     records = rows_ref.shape[0]
     halves = subdomains // LANES
     high_at, low_at, meta_at, meta_rows = message_rows(records, halves)
     out_ref[0:records, :] = rows_ref[...]
+    own = (slice(0, DEEP), slice(size_x - DEEP, size_x))
+    if len(margin_refs) == 1:
+        is_first = lax.axis_index("gx") == 0
+        margin_refs[0][...] = jnp.where(is_first, residual_ref[own[1]], residual_ref[own[0]])
+    else:
+        margin_refs[0][...], margin_refs[1][...] = residual_ref[own[0]], residual_ref[own[1]]
     whole = jnp.concatenate([inverse_ref[:, h * LANES : (h + 1) * LANES] for h in range(halves)], axis=0)
     high = whole.astype(jnp.bfloat16)
     out_ref[high_at : high_at + 8 * halves, :] = high
@@ -92,7 +105,11 @@
     out_ref[meta_at : meta_at + meta_rows, :] = meta.astype(jnp.bfloat16)
 
 
-def margin_y_kernel(residual_ref, above_ref, below_ref, down_ref, up_ref):
+def beside(i, above_ref, below_ref):
+    return above_ref.at[min(i, DEEP - 1)] if i < REACH else below_ref.at[max(i - 2 * REACH + DEEP, 0)]
+
+
+def margin_y_kernel(residual_ref, above_ref, below_ref, within_ref, across_ref):
     size_x, size_y, _ = residual_ref.shape
     row = row_of(8)
 
@@ -100,13 +117,14 @@
         if x < size_x:
             return residual_ref[x, pl.ds(at, 8), :]
         x -= size_x
-        return above_ref[x, pl.ds(at, 8), :] if x < REACH else below_ref[x - REACH, pl.ds(at, 8), :]
+        return beside(x, above_ref, below_ref)[pl.ds(at, 8), :]
 
     for pair in range((size_x + 2 * REACH) // 2):
         low = [plane(2 * pair + k, 0) for k in range(2)]
         high = [plane(2 * pair + k, size_y - 8) for k in range(2)]
-        down_ref[pair] = jnp.where(row < 4, low[0], pltpu.roll(low[1], 4, 0))
-        up_ref[pair] = jnp.where(row < 4, pltpu.roll(high[1], 4, 0), high[0])
+        down = jnp.where(row < 4, low[0], pltpu.roll(low[1], 4, 0))
+        up = jnp.where(row < 4, pltpu.roll(high[1], 4, 0), high[0])
+        within_ref[pair], across_ref[pair] = by_parity("gy", up, down)
 
 
 def edge_group(values):
@@ -129,22 +147,28 @@
         return carry
 
     lax.fori_loop(0, groups - 1, group, 0)
-    edge_ref[groups - 1] = edge_group([ref[i] for ref in (above_ref, below_ref) for i in range(REACH)])
-
-
-def edge_tail_kernel(part_ref, after_ref, before_ref, tail_ref, edge_ref):
+    edge_ref[groups - 1] = edge_group([beside(i, above_ref, below_ref)[...] for i in range(2 * REACH)])
+
+
+def edge_tail_kernel(part_ref, within_ref, across_ref, tail_ref, edge_ref, down_ref, up_ref):
     groups, size_y, _ = part_ref.shape
     row = row_of(8)
+    place = lane_of(size_y + 2 * REACH) % 16
+    down = up = jnp.zeros(down_ref.shape, jnp.float32)
     for g in range(groups):
         tails = []
         for x in range(g * SUBS, g * SUBS + SUBS):
-            after, before = after_ref[x // 2], before_ref[x // 2]
+            after, before = by_parity("gy", within_ref[x // 2], across_ref[x // 2])
             if x % 2:
                 after, before = pltpu.roll(after, 4, 0), pltpu.roll(before, 4, 0)
             tails.append(jnp.where(row < 4, after, before))
             tail_ref[x] = tails[-1]
         edge_ref[g, 0:size_y, :] = part_ref[g]
         edge_ref[g, size_y:, :] = edge_group(tails)
+        here = (place >= DEEP * g) & (place < DEEP * (g + 1))
+        down = jnp.where(here, pltpu.roll(edge_ref[g], (DEEP * g - 4) % LANES, 1), down)
+        up = jnp.where(here, pltpu.roll(edge_ref[g], (DEEP * g + DEEP - 12) % LANES, 1), up)
+    down_ref[...], up_ref[...] = down, up
 
 
 def coarse_solve(message_refs, high_at, low_at, halves, sums):
@@ -174,12 +198,53 @@
     return jnp.take_along_axis(chosen, index, axis=1)
 
 
+def y_after(value):
+    return pltpu.roll(value, value.shape[0] - 1, 0)
+
+
+def y_before(value):
+    return pltpu.roll(value, 1, 0)
+
+
+def z_after(value, edges):
+    return jnp.where(lane_of(value.shape[0]) == LANES - 1, edges, pltpu.roll(value, LANES - 1, 1))
+
+
+def z_before(value, edges):
+    return jnp.where(lane_of(value.shape[0]) == 0, edges, pltpu.roll(value, 1, 1))
+
+
+def smooth(refs, x, after, edges, before):
+    u_ref, x_ref, y_ref, z_ref, h_ref = refs
+    value, along_x, along_y, along_z = u_ref[x], x_ref[x], y_ref[x], z_ref[x]
+    total = before + along_x * u_ref[after]
+    total = total + along_y * y_after(value) + y_before(along_y * value)
+    total = total + along_z * z_after(value, edges) + z_before(along_z * value, edges)
+    return near * value + far * (h_ref[x] * total), along_x * value
+
+
+def smooth_again(u_ref, x_ref, y_ref, z_ref, h_ref, joined_ref, applied_ref):
+    size_x, size_y, _ = applied_ref.shape
+    outer = size_x + 2 * REACH - 1
+
+    def group(g, before):
+        for sub in range(SUBS):
+            x = g * SUBS + sub
+            edges = pltpu.roll(joined_ref[g], 115 - 16 * sub, 1)
+            value, before = smooth((u_ref, x_ref, y_ref, z_ref, h_ref), x, x + 1, edges, before)
+            applied_ref[x] = value[0:size_y]
+        return before
+
+    lax.fori_loop(0, size_x // SUBS, group, x_ref[outer] * u_ref[outer])
+
+
 def main_kernel(
     sizes, records, halves, slabs, size_x, size_y,
     message_ref, other_ref, residual_ref, above_ref, below_ref, tail_ref, edge_ref, lower_ref, upper_ref,
     direction_ref, applied_ref, stat_ref,
     key_ref, code_ref, turned_ref, left_ref, right_ref, added_ref,
-    density_ref, x_ref, y_ref, z_ref, h_ref, u_ref, d_ref, inside_ref, coarse_ref, first_ref, second_ref, third_ref, fourth_ref,
+    density_ref, x_ref, y_ref, z_ref, h_ref, u_ref, d_ref, inside_ref, coarse_ref,
+    first_ref, second_ref, third_ref, fourth_ref,
 ):
     n_gx, n_gy, n_gz = sizes
     gx, gy, gz = (lax.axis_index(a) for a in AXES)
@@ -290,14 +355,15 @@
             turn = lax.rem(LANES - p, LANES)
             key = jnp.broadcast_to(roll(turned_ref[0], turn, 1)[:, 0:1], (LANES, LANES))
             edge_key = jnp.broadcast_to(roll(turned_ref[1], turn, 1)[:, 0:1], (LANES, LANES))
-            wide_rows = rows.astype(f32)
+            key = key.astype(bf16)
             for sub in range(SUBS):
-                right_ref[at, sub * LANES : (sub + 1) * LANES] = jnp.where(key == sub, wide_rows, 0.0).astype(bf16)
+                chosen = jnp.where(key == sub, rows, jnp.zeros_like(rows))
+                right_ref[at, sub * LANES : (sub + 1) * LANES] = chosen
             edges = jnp.dot(rows, chooser, preferred_element_type=f32)
             right_ref[at, SUBS * LANES :] = jnp.where(edge_key == edge_code, edges, 0.0).astype(bf16)
             return carry
 
-        lax.fori_loop(0, chunk, build, 0)
+        lax.fori_loop(0, chunk, build, 0, unroll=4)
         for n in range(0, SUBS + 1, 2):
             columns = slice(n * LANES, min(n + 2, SUBS + 1) * LANES)
             product = jnp.dot(left_ref[...], right_ref[:, columns], preferred_element_type=f32)
@@ -312,20 +378,8 @@
         k = 3 if g < groups - 1 else 4
         density_ref[wide_x + g] = inside_ref[k] + added_ref[lines, SUBS * LANES :]
 
-    def y_after(value):
-        return roll(value, wide_y - 1, 0)
-
-    def y_before(value):
-        return roll(value, 1, 0)
-
     def joined(after, before):
         return jnp.where(place == 13, roll(before, 10, 1), after)
-
-    def z_after(value, edges):
-        return jnp.where(lane == LANES - 1, edges, roll(value, LANES - 1, 1))
-
-    def z_before(value, edges):
-        return jnp.where(lane == 0, edges, roll(value, 1, 1))
 
     def edge_x_after(value, other):
         return jnp.where(lane >= LANES - 16, roll(other, LANES - 16, 1), roll(value, LANES - 16, 1))
@@ -373,8 +427,10 @@
         h = inside_ref[3 if g < groups - 1 else 4] / diagonal
         h_ref[j] = h
         residual = edge_ref[g]
-        residual = jnp.where(place < 4, roll(lower_ref[g], LANES - 8, 1), residual)
-        residual = jnp.where(place >= 12, roll(upper_ref[g], 8, 1), residual)
+        lower = roll(lower_ref[...], (4 - DEEP - DEEP * g) % LANES, 1)
+        upper = roll(upper_ref[...], 12 - DEEP * g, 1)
+        residual = jnp.where((place >= 4 - DEEP) & (place < 4), lower, residual)
+        residual = jnp.where((place >= 12) & (place < 12 + DEEP), upper, residual)
         u_ref[j] = residual * h * (1.0 / theta)
         first_ref[g] = joined(density_ref[j], z_ref[j])
 
@@ -403,28 +459,28 @@
 
     def faces(x, after, k, edges, before):
         value = density_ref[x]
-        along_x = beta(value, density_ref[after])
-        along_y = beta(value, y_after(value))
-        along_z = beta(value, z_after(value, edges))
+        sum_x, sum_y, sum_z = (
+            jnp.maximum(value + other, 0.5)
+            for other in (density_ref[after], y_after(value), z_after(value, edges))
+        )
+        both = sum_x * sum_y
+        common = 2.0 / (both * sum_z)
+        along_z = common * both
+        common = common * sum_z
+        along_x = common * sum_y
+        along_y = common * sum_x
         diagonal = before + along_x + along_y + y_before(along_y) + along_z + z_before(along_z, edges)
         h = inside_ref[k] / diagonal
         x_ref[x], y_ref[x], z_ref[x], h_ref[x] = along_x, along_y, along_z, h
-        residual = (residual_ref, above_ref, below_ref)[k][x - (0, size_x, size_x + REACH)[k]]
+        residual = residual_ref[x] if k == 0 else beside(x - size_x, above_ref, below_ref)[...]
         u_ref[x, 0:size_y, :] = residual * h[0:size_y] * (1.0 / theta)
         u_ref[x, size_y:wide_y, :] = tail_ref[x] * h[size_y:wide_y] * (1.0 / theta)
         return along_x
 
     sweep(REACH, faces, jnp.ones((wide_y, LANES), f32), first_ref, edge_direct)
 
-    def smooth(x, after, edges, before):
-        value, along_x, along_y, along_z = u_ref[x], x_ref[x], y_ref[x], z_ref[x]
-        beside = before + along_x * u_ref[after]
-        beside = beside + along_y * y_after(value) + y_before(along_y * value)
-        beside = beside + along_z * z_after(value, edges) + z_before(along_z * value, edges)
-        return near * value + far * (h_ref[x] * beside), along_x * value
-
     def direct(x, after, k, edges, before):
-        value, product = smooth(x, after, edges, before)
+        value, product = smooth((u_ref, x_ref, y_ref, z_ref, h_ref), x, after, edges, before)
         d_ref[x] = value + coarse_ref[k]
         return product
 
@@ -469,12 +525,7 @@
 
     lax.fori_loop(0, stat_ref.shape[0], spread, 0, unroll=4)
 
-    def second(x, after, k, edges, before):
-        value, product = smooth(x, after, edges, before)
-        applied_ref[x] = value[0:size_y]
-        return product
-
-    sweep(0, second, x_ref[wide_x - 1] * u_ref[wide_x - 1], fourth_ref)
+    smooth_again(u_ref, x_ref, y_ref, z_ref, h_ref, fourth_ref, applied_ref)
 
 
 def finish_kernel(
@@ -509,6 +560,16 @@
     return lax.ppermute(value, axis, [(i, (i + step) % size) for i in range(size)])
 
 
+def swap_within(value, axis):
+    return lax.ppermute(value, axis, [(i, i ^ 1) for i in range(lax.axis_size(axis))])
+
+
+def swap_across(value, axis):
+    size = lax.axis_size(axis)
+    to = {i: i if i in (0, size - 1) else i + 1 if i % 2 else i - 1 for i in range(size)}
+    return lax.ppermute(value, axis, sorted(to.items()))
+
+
 def exchange(value, axis, stride):
     size = lax.axis_size(axis)
     return lax.ppermute(value, axis, [(i, i ^ stride) for i in range(size)])
@@ -518,7 +579,7 @@
     steps = []
     for axis in ("gy", "gx", "gz"):
         strides = [1 << k for k in range(lax.axis_size(axis).bit_length() - 1)]
-        steps += [(axis, stride) for stride in (strides[::-1] if axis == "gz" else strides)]
+        steps += [(axis, stride) for stride in strides[::-1]]
     return steps
 
 
@@ -535,7 +596,7 @@
     _, _, meta_at, meta_rows = message_rows(records, halves)
     shape = jax.ShapeDtypeStruct
 
-    def call(kernel, out_shape, operands, scratch=(), results=pltpu.VMEM, mib=8):
+    def call(kernel, out_shape, operands, scratch=(), results=pltpu.VMEM, mib=8, left=()):
         outs = [results(o.shape, o.dtype) for o in out_shape]
         return pl.pallas_call(
             kernel,
@@ -544,13 +605,16 @@
             out_specs=[VMEM] * len(outs),
             scratch_shapes=list(scratch),
             compiler_params=pltpu.CompilerParams(vmem_limit_bytes=mib << 20),
-        )(*(pltpu.with_memory_space_constraint(o, pltpu.VMEM) for o in operands))
-
-    (message,) = call(
+        )(*(pltpu.with_memory_space_constraint(o, pltpu.HBM if i in left else pltpu.VMEM) for i, o in enumerate(operands)))
+
+    planes_sent = shape((DEEP, size_y, LANES), f32)
+    swap = sizes[0] == 2
+    message, *margin = call(
         functools.partial(pack_kernel, sizes),
-        (shape((meta_at + meta_rows, LANES), bf16),),
+        (shape((meta_at + meta_rows, LANES), bf16),) + (planes_sent,) * (1 if swap else 2),
         (right_side, coarse_inverse, sphere_rows, margin_block.reshape(1, records), margin_column.reshape(1, records)),
         (pltpu.VMEM((8, LANES), f32),),
+        left=(1, 2, 3, 4),
     )
     steps = doublings()
 
@@ -559,29 +623,28 @@
 
     held = message[None]
     received = join(0, held)
-    first, last = right_side[:REACH], right_side[size_x - REACH :]
-    if sizes[0] == 2:
-        above = below = cycle(jnp.where(lax.axis_index("gx") == 0, last, first), "gx", 1)
+    if swap:
+        above = below = cycle(margin[0], "gx", 1)
     else:
-        above, below = cycle(first, "gx", -1), cycle(last, "gx", 1)
+        above, below = cycle(margin[0], "gx", -1), cycle(margin[1], "gx", 1)
     held, received, above, below = lax.optimization_barrier((held, received, above, below))
     held = jnp.concatenate([held, received], axis=0)
     received = join(1, held)
     pairs = shape((wide_x // 2, 8, LANES), f32)
-    down, up = call(margin_y_kernel, (pairs, pairs), (right_side, above, below))
-    after = cycle(down, "gy", -1)
-    before = cycle(up, "gy", 1)
+    within, across = call(margin_y_kernel, (pairs, pairs), (right_side, above, below))
+    within = swap_within(within, "gy")
+    across = swap_across(across, "gy")
     (part,) = call(edge_own_kernel, (shape((groups, size_y, LANES), f32),), (right_side, above, below))
-    held, received, after, before = lax.optimization_barrier((held, received, after, before))
     held = jnp.concatenate([held, received], axis=0)
     received = join(2, held)
-    tail, edge = call(
+    line = shape((wide_y, LANES), f32)
+    tail, edge, down, up = call(
         edge_tail_kernel,
-        (shape((wide_x, 8, LANES), f32), shape((groups, wide_y, LANES), f32)),
-        (part, after, before),
+        (shape((wide_x, 8, LANES), f32), shape((groups, wide_y, LANES), f32), line, line),
+        (part, within, across),
     )
-    lower = cycle(edge, "gz", 1)
-    upper = cycle(edge, "gz", -1)
+    lower = cycle(up, "gz", 1)
+    upper = cycle(down, "gz", -1)
     for k in range(3, len(steps)):
         held = jnp.concatenate([held, received], axis=0)
         received = join(k, held)
@@ -590,7 +653,8 @@
     depth = min(half, 16) * LANES
     rows_all = 16 * pl.cdiv(groups * wide_y, 16)
     field = pltpu.VMEM((planes, wide_y, LANES), f32)
-    margin = pltpu.VMEM((groups, wide_y, LANES), f32)
+    edges = (groups, wide_y, LANES)
+    margin = pltpu.VMEM(edges, f32)
     kinds = pltpu.VMEM((5, wide_y, LANES), f32)
     block = shape((size_x, size_y, LANES), f32)
     direction, applied, stats = call(
@@ -604,8 +668,7 @@
             pltpu.VMEM((rows_all, depth), bf16),
             pltpu.VMEM((depth, (SUBS + 1) * LANES), bf16),
             pltpu.VMEM((rows_all, (SUBS + 1) * LANES), f32),
-            field, field, field, field, field, field, field, kinds, kinds,
-            margin, margin, margin, margin,
+            field, field, field, field, field, field, field, kinds, kinds, margin, margin, margin, margin,
         ),
         mib=28,
     )

time: 70 us -> 67.4 us (0.963)
  waiting for transfers between devices: 21.7 us -> 16.2 us
  blocking collectives: 11 us -> 14.7 us
  other arithmetic: 1.03 us -> 0.04 us
    ppermute x5 -> x3, waiting for transfers between devices: 7.16 us -> 1.64 us  [cycle(): lax.ppermute(value, axis, [(i, (i + step) % size) for i in range(size)])]
    all_to_all x1, blocking collectives: 11 us -> 14.7 us  [shards(): stats = lax.all_to_all(stats, AXES, 0, 0, tiled=True)]
    ppermute x5 -> x3, starting transfers between devices: 8.36 us -> 4.79 us  [cycle(): lax.ppermute(value, axis, [(i, (i + step) % size) for i in range(size)])]
    ppermute x0 -> x2, starting transfers between devices: none -> 2.3 us  [the longest x1 1.64 us: swap_within(): lax.ppermute(value, axis, [(i, i ^ 1) for i in range(lax.axis_size(axis))])]
    ppermute x0 -> x2, waiting for transfers between devices: none -> 1.6 us  [the longest x1 1.59 us: swap_within(): lax.ppermute(value, axis, [(i, i ^ 1) for i in range(lax.axis_size(axis))])]
    ppermute x5, waiting for transfers between devices: 14.5 us -> 13 us  [exchange(): return lax.ppermute(value, axis, [(i, i ^ stride) for i in range(size)])]
    ppermute x5, starting transfers between devices: 4.84 us -> 6.35 us  [exchange(): return lax.ppermute(value, axis, [(i, i ^ stride) for i in range(size)])]
    select_n x1 -> x0, other arithmetic: 0.99 us -> none  [shards(): jnp.where(lax.axis_index('gx') == 0, last, first)]
  transfers between devices with their start and end apart: 10 -> 10, of which waited for: 7 -> 6; matrix products, arithmetic and copies ran while one was open for 0% -> 0% of each run, Pallas kernels for 2% -> 2%
where the time goes in v4:
time: 67.4 us; the launch traced here: 67.2 us
  Pallas kernels  20.7 us (31%)
  waiting for transfers between devices  16.2 us (24%)
  blocking collectives  14.7 us (22%)
  starting transfers between devices  13.4 us (20%)
  local copies, waits for them, and re-layouts  1.28 us (2%)
  between operations  0.73 us (1%)
    pallas_call x6, Pallas kernels, call(): pl.pallas_call(kernel, out_shape=outs, in_specs=[VMEM] * len(operands), o...  20.7 us
    all_to_all x1, blocking collectives, shards(): stats = lax.all_to_all(stats, AXES, 0, 0, tiled=True)  14.7 us
    ppermute x5, waiting for transfers between devices, exchange(): return lax.ppermute(value, axis, [(i, i ^ stride) for i in range(size)])  13 us
    ppermute x5, starting transfers between devices, exchange(): return lax.ppermute(value, axis, [(i, i ^ stride) for i in range(size)])  6.35 us
    ppermute x3, starting transfers between devices, cycle(): lax.ppermute(value, axis, [(i, (i + step) % size) for i in range(size)])  4.79 us
    ppermute x3, waiting for transfers between devices, cycle(): lax.ppermute(value, axis, [(i, (i + step) % size) for i in range(size)])  1.64 us
    ppermute x1, starting transfers between devices, swap_within(): lax.ppermute(value, axis, [(i, i ^ 1) for i in range(lax.axis_size(axis))])  1.64 us
    ppermute x1, waiting for transfers between devices, swap_within(): lax.ppermute(value, axis, [(i, i ^ 1) for i in range(lax.axis_size(axis))])  1.59 us
  transfers between devices with their start and end apart: 10, of which 6 were waited for; matrix products, arithmetic and copies ran while one was open for 0% of the time, Pallas kernels for 2%

profile of v4, /device:TPU:0, one launch (start us, length us, event | category | flops | bytes accessed | tf_op | source)
XLA Modules:
  0.0 67.2 jit_solution(10507650548239089918)
XLA Ops:
  0.6 0.0 copy-start
  0.6 1.2 %copy-done = f32[32,64,128]{2,1,0:T(8,128)S(1)} copy-done((f32[32,64,128]{2,1,0:T(8,128)S(1)}, f32[32,64,128]{2,1,0:T(8,128)}, u32[]{:S(2)}) %copy-start) | copy-done | bytes 1048600
  1.9 0.0 copy-start.1
  1.9 1.1 %shard_map.68 = (bf16[96,128]{1,0:T(8,128)(2,1)S(1)}, f32[3,64,128]{2,1,0:T(8,128)S(1)}) custom-call(f32[32,64,128]{2,1,0:T(8,128)S(1)} %copy-done, f32[8,256]{1,0:T(8,128)} %inverse_ref.1, bf16[48,128]{1,0:T(8,128)(2,1)} %rows_ref.1, s32[1,48]{1,0:T(1,128)} %bitcast.8, s32[1,48]{1,0:T(1,128)} %bitcast.9), custom_call_target="tpu_custom_call" | custom-call | tf_op jit(solution)/shard_map/pallas_call | solution.py:601
  3.0 3.0 %collective-permute-start.1 = (f32[3,64,128]{2,1,0:T(8,128)S(1)}, f32[3,64,128]{2,1,0:T(8,128)S(1)}, u32[]{:S(2)}, u32[]{:S(2)}) collective-permute-start(f32[3,64,128]{2,1,0:T(8,128)S(1)} %get-tuple-element.18), channel_id=1, source_target_pairs={{0,16},{16,0},{1,17},{17,1},{2,18},{18,2},{3,19},{19,3},{4,20},{20... | collective-permute-start | bytes 294920 | tf_op jit(solution)/shard_map/ppermute | solution.py:560
  6.0 2.6 %collective-permute-start = (bf16[1,96,128]{2,1,0:T(8,128)(2,1)S(1)}, bf16[1,96,128]{2,1,0:T(8,128)(2,1)S(1)}, u32[]{:S(2)}, u32[]{:S(2)}) collective-permute-start(bf16[1,96,128]{2,1,0:T(8,128)(2,1)S(1)} %bitcast.3), channel_id=1, source_target_pairs={{0,8},{4,12},{8,0},{12,4},{1,9},{5,13},{9,1},{13,5},{2,10},{6,14},... | collective-permute-start | bytes 73736 | tf_op jit(solution)/shard_map/ppermute | solution.py:575
  8.5 2.1 %collective-permute-done = bf16[1,96,128]{2,1,0:T(8,128)(2,1)S(1)} collective-permute-done((bf16[1,96,128]{2,1,0:T(8,128)(2,1)S(1)}, bf16[1,96,128]{2,1,0:T(8,128)(2,1)S(1)}, u32[]{:S(2)}, u32[]{:S(2)}) %collective-permute-start) | collective-permute-done | bytes 24608 | tf_op jit(solution)/shard_map/ppermute | solution.py:575
  10.7 0.0 collective-permute-done.1.above_ref.below_ref
  10.7 1.6 %collective-permute-start.2 = (bf16[2,96,128]{2,1,0:T(8,128)(2,1)S(1)}, bf16[2,96,128]{2,1,0:T(8,128)(2,1)S(1)}, u32[]{:S(2)}, u32[]{:S(2)}) collective-permute-start(bf16[2,96,128]{2,1,0:T(8,128)(2,1)S(1)} %pad_maximum_fusion.2), channel_id=1, source_target_pairs={{0,4},{4,0},{8,12},{12,8},{1,5},{5,1},{9,13},{13,9},{2,6},{6,2},{1... | collective-permute-start | bytes 147464 | tf_op jit(solution)/shard_map/ppermute | solution.py:575
  12.3 2.5 %collective-permute-done.2 = bf16[2,96,128]{2,1,0:T(8,128)(2,1)S(1)} collective-permute-done((bf16[2,96,128]{2,1,0:T(8,128)(2,1)S(1)}, bf16[2,96,128]{2,1,0:T(8,128)(2,1)S(1)}, u32[]{:S(2)}, u32[]{:S(2)}) %collective-permute-start.2) | collective-permute-done | bytes 49184 | tf_op jit(solution)/shard_map/ppermute | solution.py:575
  14.9 0.5 collective-permute-start.3
  15.3 4.2 %collective-permute-done.3 = bf16[4,96,128]{2,1,0:T(8,128)(2,1)S(1)} collective-permute-done((bf16[4,96,128]{2,1,0:T(8,128)(2,1)S(1)}, bf16[4,96,128]{2,1,0:T(8,128)(2,1)S(1)}, u32[]{:S(2)}, u32[]{:S(2)}) %collective-permute-start.3) | collective-permute-done | bytes 98336 | tf_op jit(solution)/shard_map/ppermute | solution.py:575
  19.6 1.6 %collective-permute-start.4 = (bf16[8,96,128]{2,1,0:T(8,128)(2,1)S(1)}, bf16[8,96,128]{2,1,0:T(8,128)(2,1)S(1)}, u32[]{:S(2)}, u32[]{:S(2)}) collective-permute-start(bf16[8,96,128]{2,1,0:T(8,128)(2,1)S(1)} %pad_maximum_fusion), channel_id=1, source_target_pairs={{0,2},{1,3},{2,0},{3,1},{4,6},{5,7},{6,4},{7,5},{8,10},{9,11},{10,... | collective-permute-start | bytes 589832 | tf_op jit(solution)/shard_map/ppermute | solution.py:575
  21.2 4.1 %collective-permute-done.4 = bf16[8,96,128]{2,1,0:T(8,128)(2,1)S(1)} collective-permute-done((bf16[8,96,128]{2,1,0:T(8,128)(2,1)S(1)}, bf16[8,96,128]{2,1,0:T(8,128)(2,1)S(1)}, u32[]{:S(2)}, u32[]{:S(2)}) %collective-permute-start.4) | collective-permute-done | bytes 196640 | tf_op jit(solution)/shard_map/ppermute | solution.py:575
  25.3 0.1 collective-permute-start.5
  25.4 0.0 copy-done.1
  25.5 1.6 %collective-permute-start.6 = (f32[20,8,128]{2,1,0:T(8,128)S(1)}, f32[20,8,128]{2,1,0:T(8,128)S(1)}, u32[]{:S(2)}, u32[]{:S(2)}) collective-permute-start(f32[20,8,128]{2,1,0:T(8,128)S(1)} %get-tuple-element.23), channel_id=1, source_target_pairs={{0,4},{4,0},{8,12},{12,8},{1,5},{5,1},{9,13},{13,9},{2,6},{6,2},{1... | collective-permute-start | bytes 245768 | tf_op jit(solution)/shard_map/ppermute | solution.py:564
  27.1 0.7 collective-permute-start.7
  27.8 1.0 %shard_map.69.part_ref = f32[5,64,128]{2,1,0:T(8,128)S(1)} custom-call(f32[32,64,128]{2,1,0:T(8,128)S(1)} %copy-done.1, f32[3,64,128]{2,1,0:T(8,128)S(1)} %collective-permute-done.1.above_ref.below_ref, f32[3,64,128]{2,1,0:T(8,128)S(1)} %collective-permute-done.1.above_ref.below_ref), custom_call_target="tpu_custom_call" | custom-call | tf_op jit(solution)/shard_map/pallas_call | solution.py:601
  28.8 1.6 %collective-permute-done.6.within_ref = f32[20,8,128]{2,1,0:T(8,128)S(1)} collective-permute-done((f32[20,8,128]{2,1,0:T(8,128)S(1)}, f32[20,8,128]{2,1,0:T(8,128)S(1)}, u32[]{:S(2)}, u32[]{:S(2)}) %collective-permute-start.6) | collective-permute-done | bytes 81952 | tf_op jit(solution)/shard_map/ppermute | solution.py:564
  30.4 0.0 collective-permute-done.7.across_ref
  30.4 0.3 shard_map.71
  30.7 0.1 collective-permute-start.8
  30.8 1.7 %collective-permute-start.9 = (f32[72,128]{1,0:T(8,128)S(1)}, f32[72,128]{1,0:T(8,128)S(1)}, u32[]{:S(2)}, u32[]{:S(2)}) collective-permute-start(f32[72,128]{1,0:T(8,128)S(1)} %get-tuple-element.28), channel_id=1, source_target_pairs={{0,3},{1,0},{2,1},{3,2},{4,7},{5,4},{6,5},{7,6},{8,11},{9,8},{10,9... | collective-permute-start | bytes 110600 | tf_op jit(solution)/shard_map/ppermute | solution.py:560
  32.5 1.6 %collective-permute-done.8.lower_ref = f32[72,128]{1,0:T(8,128)S(1)} collective-permute-done((f32[72,128]{1,0:T(8,128)S(1)}, f32[72,128]{1,0:T(8,128)S(1)}, u32[]{:S(2)}, u32[]{:S(2)}) %collective-permute-start.8) | collective-permute-done | bytes 36896 | tf_op jit(solution)/shard_map/ppermute | solution.py:560
  34.1 0.0 collective-permute-done.9.upper_ref
  34.1 0.0 collective-permute-done.5.other_ref
  34.1 16.3 %shard_map.72 = (f32[32,64,128]{2,1,0:T(8,128)S(1)}, f32[32,64,128]{2,1,0:T(8,128)S(1)}, f32[32,3,128]{2,1,0:T(4,128)S(1)}) custom-call(bf16[16,96,128]{2,1,0:T(8,128)(2,1)S(1)} %constant_dynamic-update-slice_fusion.message_ref, bf16[16,96,128]{2,1,0:T(8,128)(2,1)S(1)} %collective-permute-done.5.other_ref, f32[32,64,128]{2,1,0:T(8,128)S(1)} %copy-done.1, ...), custom_call_target="tpu_custom_call" | custom-call | tf_op jit(solution)/shard_map/pallas_call | solution.py:601
  50.4 14.7 %all_to_all.5.stat_ref = f32[32,3,128]{2,1,0:T(4,128)S(1)} all-to-all(f32[32,3,128]{2,1,0:T(4,128)S(1)} %get-tuple-element.29), channel_id=1, replica_groups=mesh['gx'=2,'gy'=4,'gz'=4] {'gx','gy','gz'}, dimensions={0} | all-to-all | bytes 98304 | tf_op jit(solution)/shard_map/all_to_all | solution.py:675
  65.1 2.0 %shard_map.73 = (f32[32,64,128]{2,1,0:T(8,128)}, f32[32,64,128]{2,1,0:T(8,128)}) custom-call(f32[32,3,128]{2,1,0:T(4,128)S(1)} %all_to_all.5.stat_ref, bf16[16,96,128]{2,1,0:T(8,128)(2,1)S(1)} %constant_dynamic-update-slice_fusion.message_ref, bf16[16,96,128]{2,1,0:T(8,128)(2,1)S(1)} %collective-permute-done.5.other_ref, ...), custom_call_target="tpu_custom_call" | custom-call | tf_op jit(solution)/shard_map/pallas_call | solution.py:601
  (9 shorter events, 0.1 us)
Async XLA Ops:
  0.6 1.2 %copy-start = (f32[32,64,128]{2,1,0:T(8,128)S(1)}, f32[32,64,128]{2,1,0:T(8,128)}, u32[]{:S(2)}) copy-start(f32[32,64,128]{2,1,0:T(8,128)} %residual_ref.7) | copy-start | bytes 3145732
  1.9 23.6 %copy-start.1 = (f32[32,64,128]{2,1,0:T(8,128)S(1)}, f32[32,64,128]{2,1,0:T(8,128)}, u32[]{:S(2)}) copy-start(f32[32,64,128]{2,1,0:T(8,128)} %residual_ref.7) | copy-start | bytes 3145732
  3.0 7.7 %collective-permute-start.1 = (f32[3,64,128]{2,1,0:T(8,128)S(1)}, f32[3,64,128]{2,1,0:T(8,128)S(1)}, u32[]{:S(2)}, u32[]{:S(2)}) collective-permute-start(f32[3,64,128]{2,1,0:T(8,128)S(1)} %get-tuple-element.18), channel_id=1, source_target_pairs={{0,16},{16,0},{1,17},{17,1},{2,18},{18,2},{3,19},{19,3},{4,20},{20... | collective-permute-start | bytes 294920 | tf_op jit(solution)/shard_map/ppermute | solution.py:560
  6.0 4.7 %collective-permute-start = (bf16[1,96,128]{2,1,0:T(8,128)(2,1)S(1)}, bf16[1,96,128]{2,1,0:T(8,128)(2,1)S(1)}, u32[]{:S(2)}, u32[]{:S(2)}) collective-permute-start(bf16[1,96,128]{2,1,0:T(8,128)(2,1)S(1)} %bitcast.3), channel_id=1, source_target_pairs={{0,8},{4,12},{8,0},{12,4},{1,9},{5,13},{9,1},{13,5},{2,10},{6,14},... | collective-permute-start | bytes 73736 | tf_op jit(solution)/shard_map/ppermute | solution.py:575
  10.7 4.2 %collective-permute-start.2 = (bf16[2,96,128]{2,1,0:T(8,128)(2,1)S(1)}, bf16[2,96,128]{2,1,0:T(8,128)(2,1)S(1)}, u32[]{:S(2)}, u32[]{:S(2)}) collective-permute-start(bf16[2,96,128]{2,1,0:T(8,128)(2,1)S(1)} %pad_maximum_fusion.2), channel_id=1, source_target_pairs={{0,4},{4,0},{8,12},{12,8},{1,5},{5,1},{9,13},{13,9},{2,6},{6,2},{1... | collective-permute-start | bytes 147464 | tf_op jit(solution)/shard_map/ppermute | solution.py:575
  14.9 4.7 %collective-permute-start.3 = (bf16[4,96,128]{2,1,0:T(8,128)(2,1)S(1)}, bf16[4,96,128]{2,1,0:T(8,128)(2,1)S(1)}, u32[]{:S(2)}, u32[]{:S(2)}) collective-permute-start(bf16[4,96,128]{2,1,0:T(8,128)(2,1)S(1)} %pad_maximum_fusion.1), channel_id=1, source_target_pairs={{0,16},{16,0},{1,17},{17,1},{2,18},{18,2},{3,19},{19,3},{4,20},{20... | collective-permute-start | bytes 294920 | tf_op jit(solution)/shard_map/ppermute | solution.py:575
  19.6 5.7 %collective-permute-start.4 = (bf16[8,96,128]{2,1,0:T(8,128)(2,1)S(1)}, bf16[8,96,128]{2,1,0:T(8,128)(2,1)S(1)}, u32[]{:S(2)}, u32[]{:S(2)}) collective-permute-start(bf16[8,96,128]{2,1,0:T(8,128)(2,1)S(1)} %pad_maximum_fusion), channel_id=1, source_target_pairs={{0,2},{1,3},{2,0},{3,1},{4,6},{5,7},{6,4},{7,5},{8,10},{9,11},{10,... | collective-permute-start | bytes 589832 | tf_op jit(solution)/shard_map/ppermute | solution.py:575
  25.3 8.8 %collective-permute-start.5 = (bf16[16,96,128]{2,1,0:T(8,128)(2,1)S(1)}, bf16[16,96,128]{2,1,0:T(8,128)(2,1)S(1)}, u32[]{:S(2)}, u32[]{:S(2)}) collective-permute-start(bf16[16,96,128]{2,1,0:T(8,128)(2,1)S(1)} %constant_dynamic-update-slice_fusion.message_ref), channel_id=1, source_target_pairs={{0,1},{1,0},{2,3},{3,2},{4,5},{5,4},{6,7},{7,6},{8,9},{9,8},{10,11... | collective-permute-start | bytes 1179656 | tf_op jit(solution)/shard_map/ppermute | solution.py:575
  25.5 4.9 %collective-permute-start.6 = (f32[20,8,128]{2,1,0:T(8,128)S(1)}, f32[20,8,128]{2,1,0:T(8,128)S(1)}, u32[]{:S(2)}, u32[]{:S(2)}) collective-permute-start(f32[20,8,128]{2,1,0:T(8,128)S(1)} %get-tuple-element.23), channel_id=1, source_target_pairs={{0,4},{4,0},{8,12},{12,8},{1,5},{5,1},{9,13},{13,9},{2,6},{6,2},{1... | collective-permute-start | bytes 245768 | tf_op jit(solution)/shard_map/ppermute | solution.py:564
  27.1 3.3 %collective-permute-start.7 = (f32[20,8,128]{2,1,0:T(8,128)S(1)}, f32[20,8,128]{2,1,0:T(8,128)S(1)}, u32[]{:S(2)}, u32[]{:S(2)}) collective-permute-start(f32[20,8,128]{2,1,0:T(8,128)S(1)} %get-tuple-element.24), channel_id=1, source_target_pairs={{0,0},{4,8},{8,4},{12,12},{1,1},{5,9},{9,5},{13,13},{2,2},{6,10},{... | collective-permute-start | bytes 245768 | tf_op jit(solution)/shard_map/ppermute | solution.py:570
  30.7 3.4 %collective-permute-start.8 = (f32[72,128]{1,0:T(8,128)S(1)}, f32[72,128]{1,0:T(8,128)S(1)}, u32[]{:S(2)}, u32[]{:S(2)}) collective-permute-start(f32[72,128]{1,0:T(8,128)S(1)} %get-tuple-element.27), channel_id=1, source_target_pairs={{0,1},{1,2},{2,3},{3,0},{4,5},{5,6},{6,7},{7,4},{8,9},{9,10},{10,1... | collective-permute-start | bytes 110600 | tf_op jit(solution)/shard_map/ppermute | solution.py:560
  30.8 3.4 %collective-permute-start.9 = (f32[72,128]{1,0:T(8,128)S(1)}, f32[72,128]{1,0:T(8,128)S(1)}, u32[]{:S(2)}, u32[]{:S(2)}) collective-permute-start(f32[72,128]{1,0:T(8,128)S(1)} %get-tuple-element.28), channel_id=1, source_target_pairs={{0,3},{1,0},{2,1},{3,2},{4,7},{5,4},{6,5},{7,6},{8,11},{9,8},{10,9... | collective-permute-start | bytes 110600 | tf_op jit(solution)/shard_map/ppermute | solution.py:560

commit v5 on v4

--- a/solution.py
+++ b/solution.py
@@ -348,13 +348,16 @@
     for c in range(half // chunk):
         def build(q, carry, c=c):
             p = q + c * chunk
-            at = pl.ds(pl.multiple_of(q * LANES, LANES), LANES)
+            at = pl.ds(q * LANES if isinstance(q, int) else pl.multiple_of(q * LANES, LANES), LANES)
             code = code_ref[pl.ds(p, 1), :]
             left_ref[:, at] = jnp.where(row_number == code, 1.0, 0.0).astype(bf16)
             rows = jnp.concatenate([message_ref[p, 0:SLOT, :], other_ref[p, 0:SLOT, :]], axis=0)
-            turn = lax.rem(LANES - p, LANES)
-            key = jnp.broadcast_to(roll(turned_ref[0], turn, 1)[:, 0:1], (LANES, LANES))
-            edge_key = jnp.broadcast_to(roll(turned_ref[1], turn, 1)[:, 0:1], (LANES, LANES))
+            if isinstance(p, int):
+                columns = [turned_ref[k, :, p : p + 1] for k in range(2)]
+            else:
+                turn = lax.rem(LANES - p, LANES)
+                columns = [roll(turned_ref[k], turn, 1)[:, 0:1] for k in range(2)]
+            key, edge_key = (jnp.broadcast_to(column, (LANES, LANES)) for column in columns)
             key = key.astype(bf16)
             for sub in range(SUBS):
                 chosen = jnp.where(key == sub, rows, jnp.zeros_like(rows))
@@ -363,7 +366,11 @@
             right_ref[at, SUBS * LANES :] = jnp.where(edge_key == edge_code, edges, 0.0).astype(bf16)
             return carry
 
-        lax.fori_loop(0, chunk, build, 0, unroll=4)
+        if chunk == half:
+            for q in range(chunk):
+                build(q, 0)
+        else:
+            lax.fori_loop(0, chunk, build, 0)
         for n in range(0, SUBS + 1, 2):
             columns = slice(n * LANES, min(n + 2, SUBS + 1) * LANES)
             product = jnp.dot(left_ref[...], right_ref[:, columns], preferred_element_type=f32)
@@ -509,21 +516,16 @@
     zero = jnp.zeros((8, LANES), f32)
     _, *found = sweep(1, image_of, (x_ref[outer] * (d_ref[outer] - d_ref[outer + 1]), zero, zero, zero), third_ref)
 
-    device = device_number(sizes)
     folded = [jnp.sum(f, axis=0, keepdims=True) for f in found]
-    image_sums = place_sums(jnp.broadcast_to(folded[2], (8, LANES)), device, slabs)[0:1]
-    gamma = jnp.sum(folded[0], axis=1, keepdims=True)
-    curvature = jnp.sum(folded[1], axis=1, keepdims=True)
-    last = jnp.where(lane8[0:1] == 0, gamma, jnp.where(lane8[0:1] == 1, curvature, 0.0))
-    own_half = device // (LANES // slabs)
+    line = place_sums(jnp.broadcast_to(folded[2], (8, LANES)), 0, slabs)[0:1]
+    line = jnp.where(lane8[0:1] == slabs, jnp.sum(folded[0], axis=1, keepdims=True), line)
+    line = jnp.where(lane8[0:1] == slabs + 1, jnp.sum(folded[1], axis=1, keepdims=True), line)
 
     def spread(i, carry):
-        for h in range(halves):
-            stat_ref[i, h : h + 1, :] = jnp.where(own_half == h, image_sums, 0.0)
-        stat_ref[i, halves : halves + 1, :] = last
+        stat_ref[i] = line
         return carry
 
-    lax.fori_loop(0, stat_ref.shape[0], spread, 0, unroll=4)
+    lax.fori_loop(0, stat_ref.shape[0], spread, 0, unroll=8)
 
     smooth_again(u_ref, x_ref, y_ref, z_ref, h_ref, fourth_ref, applied_ref)
 
@@ -533,15 +535,23 @@
     stat_ref, message_ref, other_ref, direction_ref, applied_ref, pressure_ref, preconditioned_ref,
 ):
     high_at, low_at, _, _ = message_rows(records, halves)
-    total = lax.fori_loop(
-        1, stat_ref.shape[0], lambda i, acc: acc + stat_ref[i], stat_ref[0], unroll=4
-    )
-    sums = [total[h : h + 1] for h in range(halves)]
+    per_half = LANES // slabs
+    lane1 = lane_of(1)
+
+    def place(i, carry):
+        last, *sums = carry
+        for h in range(halves):
+            line = stat_ref[h * per_half + i]
+            last = last + line
+            sums[h] = sums[h] + pltpu.roll(jnp.where(lane1 < slabs, line, 0.0), i * slabs, 1)
+        return (last, *sums)
+
+    zero = jnp.zeros((1, LANES), jnp.float32)
+    last, *sums = lax.fori_loop(0, per_half, place, (zero,) * (1 + halves), unroll=8)
     coarse = coarse_solve((message_ref, other_ref), high_at, low_at, halves, sums)
     lane8 = lane_of(8)
     own = pick(coarse, device_number(sizes), lane8 // (LANES // slabs), slabs)
-    last = total[halves : halves + 1]
-    alpha = last[:, 0:1] / last[:, 1:2]
+    alpha = last[:, slabs : slabs + 1] / last[:, slabs + 1 : slabs + 2]
     size_x, size_y, _ = direction_ref.shape
     alpha = jnp.broadcast_to(alpha, (size_y, LANES))
     own = jnp.concatenate([own] * (size_y // 8), axis=0)
@@ -659,7 +669,7 @@
     block = shape((size_x, size_y, LANES), f32)
     direction, applied, stats = call(
         functools.partial(main_kernel, sizes, records, halves, slabs, size_x, size_y),
-        (block, block, shape((devices, halves + 1, LANES), f32)),
+        (block, block, shape((devices, 1, LANES), f32)),
         (held, received, right_side, above, below, tail, edge, lower, upper),
         (
             pltpu.VMEM((3, devices, LANES), f32),

time: 67.4 us -> 65 us (0.964)
  Pallas kernels: 20.7 us -> 18.6 us
    pallas_call x6, Pallas kernels: 20.7 us -> 18.6 us  [call(): pl.pallas_call(kernel, out_shape=outs, in_specs=[VMEM] * len(operands), o...]
where the time goes in v5:
time: 65 us; the launch traced here: 64.8 us
  Pallas kernels  18.6 us (29%)
  waiting for transfers between devices  16.2 us (25%)
  blocking collectives  14.5 us (22%)
  starting transfers between devices  13.4 us (21%)
  local copies, waits for them, and re-layouts  1.28 us (2%)
  between operations  0.73 us (1%)
    pallas_call x6, Pallas kernels, call(): pl.pallas_call(kernel, out_shape=outs, in_specs=[VMEM] * len(operands), o...  18.6 us
    all_to_all x1, blocking collectives, shards(): stats = lax.all_to_all(stats, AXES, 0, 0, tiled=True)  14.5 us
    ppermute x5, waiting for transfers between devices, exchange(): return lax.ppermute(value, axis, [(i, i ^ stride) for i in range(size)])  13 us
    ppermute x5, starting transfers between devices, exchange(): return lax.ppermute(value, axis, [(i, i ^ stride) for i in range(size)])  6.35 us
    ppermute x3, starting transfers between devices, cycle(): lax.ppermute(value, axis, [(i, (i + step) % size) for i in range(size)])  4.79 us
    ppermute x3, waiting for transfers between devices, cycle(): lax.ppermute(value, axis, [(i, (i + step) % size) for i in range(size)])  1.64 us
    ppermute x1, starting transfers between devices, swap_within(): lax.ppermute(value, axis, [(i, i ^ 1) for i in range(lax.axis_size(axis))])  1.64 us
    ppermute x1, waiting for transfers between devices, swap_within(): lax.ppermute(value, axis, [(i, i ^ 1) for i in range(lax.axis_size(axis))])  1.59 us
  transfers between devices with their start and end apart: 10, of which 6 were waited for; matrix products, arithmetic and copies ran while one was open for 0% of the time, Pallas kernels for 2%

profile of v5, /device:TPU:0, one launch (start us, length us, event | category | flops | bytes accessed | tf_op | source)
XLA Modules:
  0.0 64.8 jit_solution(665486388456851363)
XLA Ops:
  0.6 0.0 copy-start
  0.6 1.2 %copy-done = f32[32,64,128]{2,1,0:T(8,128)S(1)} copy-done((f32[32,64,128]{2,1,0:T(8,128)S(1)}, f32[32,64,128]{2,1,0:T(8,128)}, u32[]{:S(2)}) %copy-start) | copy-done | bytes 1048600
  1.9 0.0 copy-start.1
  1.9 1.1 %shard_map.68 = (bf16[96,128]{1,0:T(8,128)(2,1)S(1)}, f32[3,64,128]{2,1,0:T(8,128)S(1)}) custom-call(f32[32,64,128]{2,1,0:T(8,128)S(1)} %copy-done, f32[8,256]{1,0:T(8,128)} %inverse_ref.1, bf16[48,128]{1,0:T(8,128)(2,1)} %rows_ref.1, s32[1,48]{1,0:T(1,128)} %bitcast.8, s32[1,48]{1,0:T(1,128)} %bitcast.9), custom_call_target="tpu_custom_call" | custom-call | tf_op jit(solution)/shard_map/pallas_call | solution.py:611
  3.0 3.0 %collective-permute-start.1 = (f32[3,64,128]{2,1,0:T(8,128)S(1)}, f32[3,64,128]{2,1,0:T(8,128)S(1)}, u32[]{:S(2)}, u32[]{:S(2)}) collective-permute-start(f32[3,64,128]{2,1,0:T(8,128)S(1)} %get-tuple-element.18), channel_id=1, source_target_pairs={{0,16},{16,0},{1,17},{17,1},{2,18},{18,2},{3,19},{19,3},{4,20},{20... | collective-permute-start | bytes 294920 | tf_op jit(solution)/shard_map/ppermute | solution.py:570
  6.0 2.6 %collective-permute-start = (bf16[1,96,128]{2,1,0:T(8,128)(2,1)S(1)}, bf16[1,96,128]{2,1,0:T(8,128)(2,1)S(1)}, u32[]{:S(2)}, u32[]{:S(2)}) collective-permute-start(bf16[1,96,128]{2,1,0:T(8,128)(2,1)S(1)} %bitcast.3), channel_id=1, source_target_pairs={{0,8},{4,12},{8,0},{12,4},{1,9},{5,13},{9,1},{13,5},{2,10},{6,14},... | collective-permute-start | bytes 73736 | tf_op jit(solution)/shard_map/ppermute | solution.py:585
  8.5 2.1 %collective-permute-done = bf16[1,96,128]{2,1,0:T(8,128)(2,1)S(1)} collective-permute-done((bf16[1,96,128]{2,1,0:T(8,128)(2,1)S(1)}, bf16[1,96,128]{2,1,0:T(8,128)(2,1)S(1)}, u32[]{:S(2)}, u32[]{:S(2)}) %collective-permute-start) | collective-permute-done | bytes 24608 | tf_op jit(solution)/shard_map/ppermute | solution.py:585
  10.7 0.0 collective-permute-done.1.above_ref.below_ref
  10.7 1.6 %collective-permute-start.2 = (bf16[2,96,128]{2,1,0:T(8,128)(2,1)S(1)}, bf16[2,96,128]{2,1,0:T(8,128)(2,1)S(1)}, u32[]{:S(2)}, u32[]{:S(2)}) collective-permute-start(bf16[2,96,128]{2,1,0:T(8,128)(2,1)S(1)} %pad_maximum_fusion.2), channel_id=1, source_target_pairs={{0,4},{4,0},{8,12},{12,8},{1,5},{5,1},{9,13},{13,9},{2,6},{6,2},{1... | collective-permute-start | bytes 147464 | tf_op jit(solution)/shard_map/ppermute | solution.py:585
  12.3 2.5 %collective-permute-done.2 = bf16[2,96,128]{2,1,0:T(8,128)(2,1)S(1)} collective-permute-done((bf16[2,96,128]{2,1,0:T(8,128)(2,1)S(1)}, bf16[2,96,128]{2,1,0:T(8,128)(2,1)S(1)}, u32[]{:S(2)}, u32[]{:S(2)}) %collective-permute-start.2) | collective-permute-done | bytes 49184 | tf_op jit(solution)/shard_map/ppermute | solution.py:585
  14.9 0.5 collective-permute-start.3
  15.3 4.2 %collective-permute-done.3 = bf16[4,96,128]{2,1,0:T(8,128)(2,1)S(1)} collective-permute-done((bf16[4,96,128]{2,1,0:T(8,128)(2,1)S(1)}, bf16[4,96,128]{2,1,0:T(8,128)(2,1)S(1)}, u32[]{:S(2)}, u32[]{:S(2)}) %collective-permute-start.3) | collective-permute-done | bytes 98336 | tf_op jit(solution)/shard_map/ppermute | solution.py:585
  19.6 1.6 %collective-permute-start.4 = (bf16[8,96,128]{2,1,0:T(8,128)(2,1)S(1)}, bf16[8,96,128]{2,1,0:T(8,128)(2,1)S(1)}, u32[]{:S(2)}, u32[]{:S(2)}) collective-permute-start(bf16[8,96,128]{2,1,0:T(8,128)(2,1)S(1)} %pad_maximum_fusion), channel_id=1, source_target_pairs={{0,2},{1,3},{2,0},{3,1},{4,6},{5,7},{6,4},{7,5},{8,10},{9,11},{10,... | collective-permute-start | bytes 589832 | tf_op jit(solution)/shard_map/ppermute | solution.py:585
  21.2 4.1 %collective-permute-done.4 = bf16[8,96,128]{2,1,0:T(8,128)(2,1)S(1)} collective-permute-done((bf16[8,96,128]{2,1,0:T(8,128)(2,1)S(1)}, bf16[8,96,128]{2,1,0:T(8,128)(2,1)S(1)}, u32[]{:S(2)}, u32[]{:S(2)}) %collective-permute-start.4) | collective-permute-done | bytes 196640 | tf_op jit(solution)/shard_map/ppermute | solution.py:585
  25.3 0.1 collective-permute-start.5
  25.4 0.0 copy-done.1
  25.5 1.6 %collective-permute-start.6 = (f32[20,8,128]{2,1,0:T(8,128)S(1)}, f32[20,8,128]{2,1,0:T(8,128)S(1)}, u32[]{:S(2)}, u32[]{:S(2)}) collective-permute-start(f32[20,8,128]{2,1,0:T(8,128)S(1)} %get-tuple-element.23), channel_id=1, source_target_pairs={{0,4},{4,0},{8,12},{12,8},{1,5},{5,1},{9,13},{13,9},{2,6},{6,2},{1... | collective-permute-start | bytes 245768 | tf_op jit(solution)/shard_map/ppermute | solution.py:574
  27.1 0.7 %collective-permute-start.7 = (f32[20,8,128]{2,1,0:T(8,128)S(1)}, f32[20,8,128]{2,1,0:T(8,128)S(1)}, u32[]{:S(2)}, u32[]{:S(2)}) collective-permute-start(f32[20,8,128]{2,1,0:T(8,128)S(1)} %get-tuple-element.24), channel_id=1, source_target_pairs={{0,0},{4,8},{8,4},{12,12},{1,1},{5,9},{9,5},{13,13},{2,2},{6,10},{... | collective-permute-start | bytes 245768 | tf_op jit(solution)/shard_map/ppermute | solution.py:580
  27.8 1.0 %shard_map.69.part_ref = f32[5,64,128]{2,1,0:T(8,128)S(1)} custom-call(f32[32,64,128]{2,1,0:T(8,128)S(1)} %copy-done.1, f32[3,64,128]{2,1,0:T(8,128)S(1)} %collective-permute-done.1.above_ref.below_ref, f32[3,64,128]{2,1,0:T(8,128)S(1)} %collective-permute-done.1.above_ref.below_ref), custom_call_target="tpu_custom_call" | custom-call | tf_op jit(solution)/shard_map/pallas_call | solution.py:611
  28.8 1.6 %collective-permute-done.6.within_ref = f32[20,8,128]{2,1,0:T(8,128)S(1)} collective-permute-done((f32[20,8,128]{2,1,0:T(8,128)S(1)}, f32[20,8,128]{2,1,0:T(8,128)S(1)}, u32[]{:S(2)}, u32[]{:S(2)}) %collective-permute-start.6) | collective-permute-done | bytes 81952 | tf_op jit(solution)/shard_map/ppermute | solution.py:574
  30.4 0.0 collective-permute-done.7.across_ref
  30.4 0.3 shard_map.71
  30.7 0.1 collective-permute-start.8
  30.8 1.7 %collective-permute-start.9 = (f32[72,128]{1,0:T(8,128)S(1)}, f32[72,128]{1,0:T(8,128)S(1)}, u32[]{:S(2)}, u32[]{:S(2)}) collective-permute-start(f32[72,128]{1,0:T(8,128)S(1)} %get-tuple-element.28), channel_id=1, source_target_pairs={{0,3},{1,0},{2,1},{3,2},{4,7},{5,4},{6,5},{7,6},{8,11},{9,8},{10,9... | collective-permute-start | bytes 110600 | tf_op jit(solution)/shard_map/ppermute | solution.py:570
  32.5 1.6 %collective-permute-done.8.lower_ref = f32[72,128]{1,0:T(8,128)S(1)} collective-permute-done((f32[72,128]{1,0:T(8,128)S(1)}, f32[72,128]{1,0:T(8,128)S(1)}, u32[]{:S(2)}, u32[]{:S(2)}) %collective-permute-start.8) | collective-permute-done | bytes 36896 | tf_op jit(solution)/shard_map/ppermute | solution.py:570
  34.1 0.0 collective-permute-done.9.upper_ref
  34.1 0.0 collective-permute-done.5.other_ref
  34.1 14.1 %shard_map.72 = (f32[32,64,128]{2,1,0:T(8,128)S(1)}, f32[32,64,128]{2,1,0:T(8,128)S(1)}, f32[32,1,128]{2,1,0:T(1,128)S(1)}) custom-call(bf16[16,96,128]{2,1,0:T(8,128)(2,1)S(1)} %constant_dynamic-update-slice_fusion.message_ref, bf16[16,96,128]{2,1,0:T(8,128)(2,1)S(1)} %collective-permute-done.5.other_ref, f32[32,64,128]{2,1,0:T(8,128)S(1)} %copy-done.1, ...), custom_call_target="tpu_custom_call" | custom-call | tf_op jit(solution)/shard_map/pallas_call | solution.py:611
  48.2 14.5 %all_to_all.5.stat_ref = f32[32,1,128]{2,1,0:T(1,128)S(1)} all-to-all(f32[32,1,128]{2,1,0:T(1,128)S(1)} %get-tuple-element.29), channel_id=1, replica_groups=mesh['gx'=2,'gy'=4,'gz'=4] {'gx','gy','gz'}, dimensions={0} | all-to-all | bytes 32768 | tf_op jit(solution)/shard_map/all_to_all | solution.py:685
  62.7 2.2 %shard_map.73 = (f32[32,64,128]{2,1,0:T(8,128)}, f32[32,64,128]{2,1,0:T(8,128)}) custom-call(f32[32,1,128]{2,1,0:T(1,128)S(1)} %all_to_all.5.stat_ref, bf16[16,96,128]{2,1,0:T(8,128)(2,1)S(1)} %constant_dynamic-update-slice_fusion.message_ref, bf16[16,96,128]{2,1,0:T(8,128)(2,1)S(1)} %collective-permute-done.5.other_ref, ...), custom_call_target="tpu_custom_call" | custom-call | tf_op jit(solution)/shard_map/pallas_call | solution.py:611
  (9 shorter events, 0.1 us)
Async XLA Ops:
  0.6 1.2 %copy-start = (f32[32,64,128]{2,1,0:T(8,128)S(1)}, f32[32,64,128]{2,1,0:T(8,128)}, u32[]{:S(2)}) copy-start(f32[32,64,128]{2,1,0:T(8,128)} %residual_ref.7) | copy-start | bytes 3145732
  1.9 23.6 %copy-start.1 = (f32[32,64,128]{2,1,0:T(8,128)S(1)}, f32[32,64,128]{2,1,0:T(8,128)}, u32[]{:S(2)}) copy-start(f32[32,64,128]{2,1,0:T(8,128)} %residual_ref.7) | copy-start | bytes 3145732
  3.0 7.7 %collective-permute-start.1 = (f32[3,64,128]{2,1,0:T(8,128)S(1)}, f32[3,64,128]{2,1,0:T(8,128)S(1)}, u32[]{:S(2)}, u32[]{:S(2)}) collective-permute-start(f32[3,64,128]{2,1,0:T(8,128)S(1)} %get-tuple-element.18), channel_id=1, source_target_pairs={{0,16},{16,0},{1,17},{17,1},{2,18},{18,2},{3,19},{19,3},{4,20},{20... | collective-permute-start | bytes 294920 | tf_op jit(solution)/shard_map/ppermute | solution.py:570
  6.0 4.7 %collective-permute-start = (bf16[1,96,128]{2,1,0:T(8,128)(2,1)S(1)}, bf16[1,96,128]{2,1,0:T(8,128)(2,1)S(1)}, u32[]{:S(2)}, u32[]{:S(2)}) collective-permute-start(bf16[1,96,128]{2,1,0:T(8,128)(2,1)S(1)} %bitcast.3), channel_id=1, source_target_pairs={{0,8},{4,12},{8,0},{12,4},{1,9},{5,13},{9,1},{13,5},{2,10},{6,14},... | collective-permute-start | bytes 73736 | tf_op jit(solution)/shard_map/ppermute | solution.py:585
  10.7 4.2 %collective-permute-start.2 = (bf16[2,96,128]{2,1,0:T(8,128)(2,1)S(1)}, bf16[2,96,128]{2,1,0:T(8,128)(2,1)S(1)}, u32[]{:S(2)}, u32[]{:S(2)}) collective-permute-start(bf16[2,96,128]{2,1,0:T(8,128)(2,1)S(1)} %pad_maximum_fusion.2), channel_id=1, source_target_pairs={{0,4},{4,0},{8,12},{12,8},{1,5},{5,1},{9,13},{13,9},{2,6},{6,2},{1... | collective-permute-start | bytes 147464 | tf_op jit(solution)/shard_map/ppermute | solution.py:585
  14.9 4.7 %collective-permute-start.3 = (bf16[4,96,128]{2,1,0:T(8,128)(2,1)S(1)}, bf16[4,96,128]{2,1,0:T(8,128)(2,1)S(1)}, u32[]{:S(2)}, u32[]{:S(2)}) collective-permute-start(bf16[4,96,128]{2,1,0:T(8,128)(2,1)S(1)} %pad_maximum_fusion.1), channel_id=1, source_target_pairs={{0,16},{16,0},{1,17},{17,1},{2,18},{18,2},{3,19},{19,3},{4,20},{20... | collective-permute-start | bytes 294920 | tf_op jit(solution)/shard_map/ppermute | solution.py:585
  19.6 5.7 %collective-permute-start.4 = (bf16[8,96,128]{2,1,0:T(8,128)(2,1)S(1)}, bf16[8,96,128]{2,1,0:T(8,128)(2,1)S(1)}, u32[]{:S(2)}, u32[]{:S(2)}) collective-permute-start(bf16[8,96,128]{2,1,0:T(8,128)(2,1)S(1)} %pad_maximum_fusion), channel_id=1, source_target_pairs={{0,2},{1,3},{2,0},{3,1},{4,6},{5,7},{6,4},{7,5},{8,10},{9,11},{10,... | collective-permute-start | bytes 589832 | tf_op jit(solution)/shard_map/ppermute | solution.py:585
  25.3 8.8 %collective-permute-start.5 = (bf16[16,96,128]{2,1,0:T(8,128)(2,1)S(1)}, bf16[16,96,128]{2,1,0:T(8,128)(2,1)S(1)}, u32[]{:S(2)}, u32[]{:S(2)}) collective-permute-start(bf16[16,96,128]{2,1,0:T(8,128)(2,1)S(1)} %constant_dynamic-update-slice_fusion.message_ref), channel_id=1, source_target_pairs={{0,1},{1,0},{2,3},{3,2},{4,5},{5,4},{6,7},{7,6},{8,9},{9,8},{10,11... | collective-permute-start | bytes 1179656 | tf_op jit(solution)/shard_map/ppermute | solution.py:585
  25.5 4.9 %collective-permute-start.6 = (f32[20,8,128]{2,1,0:T(8,128)S(1)}, f32[20,8,128]{2,1,0:T(8,128)S(1)}, u32[]{:S(2)}, u32[]{:S(2)}) collective-permute-start(f32[20,8,128]{2,1,0:T(8,128)S(1)} %get-tuple-element.23), channel_id=1, source_target_pairs={{0,4},{4,0},{8,12},{12,8},{1,5},{5,1},{9,13},{13,9},{2,6},{6,2},{1... | collective-permute-start | bytes 245768 | tf_op jit(solution)/shard_map/ppermute | solution.py:574
  27.1 3.3 %collective-permute-start.7 = (f32[20,8,128]{2,1,0:T(8,128)S(1)}, f32[20,8,128]{2,1,0:T(8,128)S(1)}, u32[]{:S(2)}, u32[]{:S(2)}) collective-permute-start(f32[20,8,128]{2,1,0:T(8,128)S(1)} %get-tuple-element.24), channel_id=1, source_target_pairs={{0,0},{4,8},{8,4},{12,12},{1,1},{5,9},{9,5},{13,13},{2,2},{6,10},{... | collective-permute-start | bytes 245768 | tf_op jit(solution)/shard_map/ppermute | solution.py:580
  30.7 3.4 %collective-permute-start.8 = (f32[72,128]{1,0:T(8,128)S(1)}, f32[72,128]{1,0:T(8,128)S(1)}, u32[]{:S(2)}, u32[]{:S(2)}) collective-permute-start(f32[72,128]{1,0:T(8,128)S(1)} %get-tuple-element.27), channel_id=1, source_target_pairs={{0,1},{1,2},{2,3},{3,0},{4,5},{5,6},{6,7},{7,4},{8,9},{9,10},{10,1... | collective-permute-start | bytes 110600 | tf_op jit(solution)/shard_map/ppermute | solution.py:570
  30.8 3.4 %collective-permute-start.9 = (f32[72,128]{1,0:T(8,128)S(1)}, f32[72,128]{1,0:T(8,128)S(1)}, u32[]{:S(2)}, u32[]{:S(2)}) collective-permute-start(f32[72,128]{1,0:T(8,128)S(1)} %get-tuple-element.28), channel_id=1, source_target_pairs={{0,3},{1,0},{2,1},{3,2},{4,7},{5,4},{6,5},{7,6},{8,11},{9,8},{10,9... | collective-permute-start | bytes 110600 | tf_op jit(solution)/shard_map/ppermute | solution.py:570

commit v6 on v5

--- a/solution.py
+++ b/solution.py
@@ -184,7 +184,7 @@
     zero = jnp.zeros((8, LANES), jnp.float32)
     total = (zero,) * halves
     for ref in message_refs:
-        total = lax.fori_loop(0, ref.shape[0], functools.partial(body, ref), total, unroll=8)
+        total = lax.fori_loop(0, ref.shape[0], functools.partial(body, ref), total, unroll=16)
     return [jnp.broadcast_to(jnp.sum(t, axis=0, keepdims=True), (8, LANES)) for t in total]
 
 
@@ -268,7 +268,7 @@
             total = total + tile
         return total
 
-    total = lax.fori_loop(0, half, read_meta, jnp.zeros((meta_rows, LANES), f32), unroll=4)
+    total = lax.fori_loop(0, half, read_meta, jnp.zeros((meta_rows, LANES), f32), unroll=16)
     sums = [
         total[3 + h : 4 + h] + total[3 + halves + h : 4 + halves + h] + total[3 + 2 * halves + h : 4 + 2 * halves + h]
         for h in range(halves)
@@ -562,7 +562,7 @@
         preconditioned_ref[x] = direction - alpha * (applied_ref[x] + own)
         return carry
 
-    lax.fori_loop(0, size_x, body, 0, unroll=2)
+    lax.fori_loop(0, size_x, body, 0, unroll=8)
 
 
 def cycle(value, axis, step):

time: 65 us -> 64.4 us (level)
    pallas_call x6, Pallas kernels: 18.6 us -> 18 us  [call(): pl.pallas_call(kernel, out_shape=outs, in_specs=[VMEM] * len(operands), o...]
where the time goes in v6:
time: 64.4 us; the launch traced here: 64.2 us
  Pallas kernels  18 us (28%)
  waiting for transfers between devices  16.2 us (25%)
  blocking collectives  14.5 us (23%)
  starting transfers between devices  13.4 us (21%)
  local copies, waits for them, and re-layouts  1.28 us (2%)
  between operations  0.73 us (1%)
    pallas_call x6, Pallas kernels, call(): pl.pallas_call(kernel, out_shape=outs, in_specs=[VMEM] * len(operands), o...  18 us
    all_to_all x1, blocking collectives, shards(): stats = lax.all_to_all(stats, AXES, 0, 0, tiled=True)  14.5 us
    ppermute x5, waiting for transfers between devices, exchange(): return lax.ppermute(value, axis, [(i, i ^ stride) for i in range(size)])  13 us
    ppermute x5, starting transfers between devices, exchange(): return lax.ppermute(value, axis, [(i, i ^ stride) for i in range(size)])  6.35 us
    ppermute x3, starting transfers between devices, cycle(): lax.ppermute(value, axis, [(i, (i + step) % size) for i in range(size)])  4.79 us
    ppermute x3, waiting for transfers between devices, cycle(): lax.ppermute(value, axis, [(i, (i + step) % size) for i in range(size)])  1.64 us
    ppermute x1, starting transfers between devices, swap_within(): lax.ppermute(value, axis, [(i, i ^ 1) for i in range(lax.axis_size(axis))])  1.64 us
    ppermute x1, waiting for transfers between devices, swap_within(): lax.ppermute(value, axis, [(i, i ^ 1) for i in range(lax.axis_size(axis))])  1.59 us
  transfers between devices with their start and end apart: 10, of which 6 were waited for; matrix products, arithmetic and copies ran while one was open for 0% of the time, Pallas kernels for 2%

profile of v6, /device:TPU:0, one launch (start us, length us, event | category | flops | bytes accessed | tf_op | source)
XLA Modules:
  0.0 64.2 jit_solution(15661430265754293287)
XLA Ops:
  0.6 0.0 copy-start
  0.6 1.2 %copy-done = f32[32,64,128]{2,1,0:T(8,128)S(1)} copy-done((f32[32,64,128]{2,1,0:T(8,128)S(1)}, f32[32,64,128]{2,1,0:T(8,128)}, u32[]{:S(2)}) %copy-start) | copy-done | bytes 1048600
  1.9 0.0 copy-start.1
  1.9 1.1 %shard_map.68 = (bf16[96,128]{1,0:T(8,128)(2,1)S(1)}, f32[3,64,128]{2,1,0:T(8,128)S(1)}) custom-call(f32[32,64,128]{2,1,0:T(8,128)S(1)} %copy-done, f32[8,256]{1,0:T(8,128)} %inverse_ref.1, bf16[48,128]{1,0:T(8,128)(2,1)} %rows_ref.1, s32[1,48]{1,0:T(1,128)} %bitcast.8, s32[1,48]{1,0:T(1,128)} %bitcast.9), custom_call_target="tpu_custom_call" | custom-call | tf_op jit(solution)/shard_map/pallas_call | solution.py:611
  3.0 3.0 %collective-permute-start.1 = (f32[3,64,128]{2,1,0:T(8,128)S(1)}, f32[3,64,128]{2,1,0:T(8,128)S(1)}, u32[]{:S(2)}, u32[]{:S(2)}) collective-permute-start(f32[3,64,128]{2,1,0:T(8,128)S(1)} %get-tuple-element.18), channel_id=1, source_target_pairs={{0,16},{16,0},{1,17},{17,1},{2,18},{18,2},{3,19},{19,3},{4,20},{20... | collective-permute-start | bytes 294920 | tf_op jit(solution)/shard_map/ppermute | solution.py:570
  6.0 2.6 %collective-permute-start = (bf16[1,96,128]{2,1,0:T(8,128)(2,1)S(1)}, bf16[1,96,128]{2,1,0:T(8,128)(2,1)S(1)}, u32[]{:S(2)}, u32[]{:S(2)}) collective-permute-start(bf16[1,96,128]{2,1,0:T(8,128)(2,1)S(1)} %bitcast.3), channel_id=1, source_target_pairs={{0,8},{4,12},{8,0},{12,4},{1,9},{5,13},{9,1},{13,5},{2,10},{6,14},... | collective-permute-start | bytes 73736 | tf_op jit(solution)/shard_map/ppermute | solution.py:585
  8.5 2.1 %collective-permute-done = bf16[1,96,128]{2,1,0:T(8,128)(2,1)S(1)} collective-permute-done((bf16[1,96,128]{2,1,0:T(8,128)(2,1)S(1)}, bf16[1,96,128]{2,1,0:T(8,128)(2,1)S(1)}, u32[]{:S(2)}, u32[]{:S(2)}) %collective-permute-start) | collective-permute-done | bytes 24608 | tf_op jit(solution)/shard_map/ppermute | solution.py:585
  10.7 0.0 collective-permute-done.1.above_ref.below_ref
  10.7 1.6 %collective-permute-start.2 = (bf16[2,96,128]{2,1,0:T(8,128)(2,1)S(1)}, bf16[2,96,128]{2,1,0:T(8,128)(2,1)S(1)}, u32[]{:S(2)}, u32[]{:S(2)}) collective-permute-start(bf16[2,96,128]{2,1,0:T(8,128)(2,1)S(1)} %pad_maximum_fusion.2), channel_id=1, source_target_pairs={{0,4},{4,0},{8,12},{12,8},{1,5},{5,1},{9,13},{13,9},{2,6},{6,2},{1... | collective-permute-start | bytes 147464 | tf_op jit(solution)/shard_map/ppermute | solution.py:585
  12.3 2.5 %collective-permute-done.2 = bf16[2,96,128]{2,1,0:T(8,128)(2,1)S(1)} collective-permute-done((bf16[2,96,128]{2,1,0:T(8,128)(2,1)S(1)}, bf16[2,96,128]{2,1,0:T(8,128)(2,1)S(1)}, u32[]{:S(2)}, u32[]{:S(2)}) %collective-permute-start.2) | collective-permute-done | bytes 49184 | tf_op jit(solution)/shard_map/ppermute | solution.py:585
  14.9 0.5 collective-permute-start.3
  15.3 4.2 %collective-permute-done.3 = bf16[4,96,128]{2,1,0:T(8,128)(2,1)S(1)} collective-permute-done((bf16[4,96,128]{2,1,0:T(8,128)(2,1)S(1)}, bf16[4,96,128]{2,1,0:T(8,128)(2,1)S(1)}, u32[]{:S(2)}, u32[]{:S(2)}) %collective-permute-start.3) | collective-permute-done | bytes 98336 | tf_op jit(solution)/shard_map/ppermute | solution.py:585
  19.6 1.6 %collective-permute-start.4 = (bf16[8,96,128]{2,1,0:T(8,128)(2,1)S(1)}, bf16[8,96,128]{2,1,0:T(8,128)(2,1)S(1)}, u32[]{:S(2)}, u32[]{:S(2)}) collective-permute-start(bf16[8,96,128]{2,1,0:T(8,128)(2,1)S(1)} %pad_maximum_fusion), channel_id=1, source_target_pairs={{0,2},{1,3},{2,0},{3,1},{4,6},{5,7},{6,4},{7,5},{8,10},{9,11},{10,... | collective-permute-start | bytes 589832 | tf_op jit(solution)/shard_map/ppermute | solution.py:585
  21.2 4.1 %collective-permute-done.4 = bf16[8,96,128]{2,1,0:T(8,128)(2,1)S(1)} collective-permute-done((bf16[8,96,128]{2,1,0:T(8,128)(2,1)S(1)}, bf16[8,96,128]{2,1,0:T(8,128)(2,1)S(1)}, u32[]{:S(2)}, u32[]{:S(2)}) %collective-permute-start.4) | collective-permute-done | bytes 196640 | tf_op jit(solution)/shard_map/ppermute | solution.py:585
  25.3 0.1 collective-permute-start.5
  25.4 0.0 copy-done.1
  25.5 1.6 %collective-permute-start.6 = (f32[20,8,128]{2,1,0:T(8,128)S(1)}, f32[20,8,128]{2,1,0:T(8,128)S(1)}, u32[]{:S(2)}, u32[]{:S(2)}) collective-permute-start(f32[20,8,128]{2,1,0:T(8,128)S(1)} %get-tuple-element.23), channel_id=1, source_target_pairs={{0,4},{4,0},{8,12},{12,8},{1,5},{5,1},{9,13},{13,9},{2,6},{6,2},{1... | collective-permute-start | bytes 245768 | tf_op jit(solution)/shard_map/ppermute | solution.py:574
  27.1 0.7 %collective-permute-start.7 = (f32[20,8,128]{2,1,0:T(8,128)S(1)}, f32[20,8,128]{2,1,0:T(8,128)S(1)}, u32[]{:S(2)}, u32[]{:S(2)}) collective-permute-start(f32[20,8,128]{2,1,0:T(8,128)S(1)} %get-tuple-element.24), channel_id=1, source_target_pairs={{0,0},{4,8},{8,4},{12,12},{1,1},{5,9},{9,5},{13,13},{2,2},{6,10},{... | collective-permute-start | bytes 245768 | tf_op jit(solution)/shard_map/ppermute | solution.py:580
  27.8 1.0 %shard_map.69.part_ref = f32[5,64,128]{2,1,0:T(8,128)S(1)} custom-call(f32[32,64,128]{2,1,0:T(8,128)S(1)} %copy-done.1, f32[3,64,128]{2,1,0:T(8,128)S(1)} %collective-permute-done.1.above_ref.below_ref, f32[3,64,128]{2,1,0:T(8,128)S(1)} %collective-permute-done.1.above_ref.below_ref), custom_call_target="tpu_custom_call" | custom-call | tf_op jit(solution)/shard_map/pallas_call | solution.py:611
  28.8 1.6 %collective-permute-done.6.within_ref = f32[20,8,128]{2,1,0:T(8,128)S(1)} collective-permute-done((f32[20,8,128]{2,1,0:T(8,128)S(1)}, f32[20,8,128]{2,1,0:T(8,128)S(1)}, u32[]{:S(2)}, u32[]{:S(2)}) %collective-permute-start.6) | collective-permute-done | bytes 81952 | tf_op jit(solution)/shard_map/ppermute | solution.py:574
  30.4 0.0 collective-permute-done.7.across_ref
  30.4 0.3 shard_map.71
  30.7 0.1 collective-permute-start.8
  30.8 1.7 %collective-permute-start.9 = (f32[72,128]{1,0:T(8,128)S(1)}, f32[72,128]{1,0:T(8,128)S(1)}, u32[]{:S(2)}, u32[]{:S(2)}) collective-permute-start(f32[72,128]{1,0:T(8,128)S(1)} %get-tuple-element.28), channel_id=1, source_target_pairs={{0,3},{1,0},{2,1},{3,2},{4,7},{5,4},{6,5},{7,6},{8,11},{9,8},{10,9... | collective-permute-start | bytes 110600 | tf_op jit(solution)/shard_map/ppermute | solution.py:570
  32.5 1.6 %collective-permute-done.8.lower_ref = f32[72,128]{1,0:T(8,128)S(1)} collective-permute-done((f32[72,128]{1,0:T(8,128)S(1)}, f32[72,128]{1,0:T(8,128)S(1)}, u32[]{:S(2)}, u32[]{:S(2)}) %collective-permute-start.8) | collective-permute-done | bytes 36896 | tf_op jit(solution)/shard_map/ppermute | solution.py:570
  34.1 0.0 collective-permute-done.9.upper_ref
  34.1 0.0 collective-permute-done.5.other_ref
  34.1 13.7 %shard_map.72 = (f32[32,64,128]{2,1,0:T(8,128)S(1)}, f32[32,64,128]{2,1,0:T(8,128)S(1)}, f32[32,1,128]{2,1,0:T(1,128)S(1)}) custom-call(bf16[16,96,128]{2,1,0:T(8,128)(2,1)S(1)} %constant_dynamic-update-slice_fusion.message_ref, bf16[16,96,128]{2,1,0:T(8,128)(2,1)S(1)} %collective-permute-done.5.other_ref, f32[32,64,128]{2,1,0:T(8,128)S(1)} %copy-done.1, ...), custom_call_target="tpu_custom_call" | custom-call | tf_op jit(solution)/shard_map/pallas_call | solution.py:611
  47.8 14.5 %all_to_all.5.stat_ref = f32[32,1,128]{2,1,0:T(1,128)S(1)} all-to-all(f32[32,1,128]{2,1,0:T(1,128)S(1)} %get-tuple-element.29), channel_id=1, replica_groups=mesh['gx'=2,'gy'=4,'gz'=4] {'gx','gy','gz'}, dimensions={0} | all-to-all | bytes 32768 | tf_op jit(solution)/shard_map/all_to_all | solution.py:685
  62.3 1.9 %shard_map.73 = (f32[32,64,128]{2,1,0:T(8,128)}, f32[32,64,128]{2,1,0:T(8,128)}) custom-call(f32[32,1,128]{2,1,0:T(1,128)S(1)} %all_to_all.5.stat_ref, bf16[16,96,128]{2,1,0:T(8,128)(2,1)S(1)} %constant_dynamic-update-slice_fusion.message_ref, bf16[16,96,128]{2,1,0:T(8,128)(2,1)S(1)} %collective-permute-done.5.other_ref, ...), custom_call_target="tpu_custom_call" | custom-call | tf_op jit(solution)/shard_map/pallas_call | solution.py:611
  (9 shorter events, 0.1 us)
Async XLA Ops:
  0.6 1.2 %copy-start = (f32[32,64,128]{2,1,0:T(8,128)S(1)}, f32[32,64,128]{2,1,0:T(8,128)}, u32[]{:S(2)}) copy-start(f32[32,64,128]{2,1,0:T(8,128)} %residual_ref.7) | copy-start | bytes 3145732
  1.9 23.6 %copy-start.1 = (f32[32,64,128]{2,1,0:T(8,128)S(1)}, f32[32,64,128]{2,1,0:T(8,128)}, u32[]{:S(2)}) copy-start(f32[32,64,128]{2,1,0:T(8,128)} %residual_ref.7) | copy-start | bytes 3145732
  3.0 7.7 %collective-permute-start.1 = (f32[3,64,128]{2,1,0:T(8,128)S(1)}, f32[3,64,128]{2,1,0:T(8,128)S(1)}, u32[]{:S(2)}, u32[]{:S(2)}) collective-permute-start(f32[3,64,128]{2,1,0:T(8,128)S(1)} %get-tuple-element.18), channel_id=1, source_target_pairs={{0,16},{16,0},{1,17},{17,1},{2,18},{18,2},{3,19},{19,3},{4,20},{20... | collective-permute-start | bytes 294920 | tf_op jit(solution)/shard_map/ppermute | solution.py:570
  6.0 4.7 %collective-permute-start = (bf16[1,96,128]{2,1,0:T(8,128)(2,1)S(1)}, bf16[1,96,128]{2,1,0:T(8,128)(2,1)S(1)}, u32[]{:S(2)}, u32[]{:S(2)}) collective-permute-start(bf16[1,96,128]{2,1,0:T(8,128)(2,1)S(1)} %bitcast.3), channel_id=1, source_target_pairs={{0,8},{4,12},{8,0},{12,4},{1,9},{5,13},{9,1},{13,5},{2,10},{6,14},... | collective-permute-start | bytes 73736 | tf_op jit(solution)/shard_map/ppermute | solution.py:585
  10.7 4.2 %collective-permute-start.2 = (bf16[2,96,128]{2,1,0:T(8,128)(2,1)S(1)}, bf16[2,96,128]{2,1,0:T(8,128)(2,1)S(1)}, u32[]{:S(2)}, u32[]{:S(2)}) collective-permute-start(bf16[2,96,128]{2,1,0:T(8,128)(2,1)S(1)} %pad_maximum_fusion.2), channel_id=1, source_target_pairs={{0,4},{4,0},{8,12},{12,8},{1,5},{5,1},{9,13},{13,9},{2,6},{6,2},{1... | collective-permute-start | bytes 147464 | tf_op jit(solution)/shard_map/ppermute | solution.py:585
  14.9 4.7 %collective-permute-start.3 = (bf16[4,96,128]{2,1,0:T(8,128)(2,1)S(1)}, bf16[4,96,128]{2,1,0:T(8,128)(2,1)S(1)}, u32[]{:S(2)}, u32[]{:S(2)}) collective-permute-start(bf16[4,96,128]{2,1,0:T(8,128)(2,1)S(1)} %pad_maximum_fusion.1), channel_id=1, source_target_pairs={{0,16},{16,0},{1,17},{17,1},{2,18},{18,2},{3,19},{19,3},{4,20},{20... | collective-permute-start | bytes 294920 | tf_op jit(solution)/shard_map/ppermute | solution.py:585
  19.6 5.7 %collective-permute-start.4 = (bf16[8,96,128]{2,1,0:T(8,128)(2,1)S(1)}, bf16[8,96,128]{2,1,0:T(8,128)(2,1)S(1)}, u32[]{:S(2)}, u32[]{:S(2)}) collective-permute-start(bf16[8,96,128]{2,1,0:T(8,128)(2,1)S(1)} %pad_maximum_fusion), channel_id=1, source_target_pairs={{0,2},{1,3},{2,0},{3,1},{4,6},{5,7},{6,4},{7,5},{8,10},{9,11},{10,... | collective-permute-start | bytes 589832 | tf_op jit(solution)/shard_map/ppermute | solution.py:585
  25.3 8.8 %collective-permute-start.5 = (bf16[16,96,128]{2,1,0:T(8,128)(2,1)S(1)}, bf16[16,96,128]{2,1,0:T(8,128)(2,1)S(1)}, u32[]{:S(2)}, u32[]{:S(2)}) collective-permute-start(bf16[16,96,128]{2,1,0:T(8,128)(2,1)S(1)} %constant_dynamic-update-slice_fusion.message_ref), channel_id=1, source_target_pairs={{0,1},{1,0},{2,3},{3,2},{4,5},{5,4},{6,7},{7,6},{8,9},{9,8},{10,11... | collective-permute-start | bytes 1179656 | tf_op jit(solution)/shard_map/ppermute | solution.py:585
  25.5 4.9 %collective-permute-start.6 = (f32[20,8,128]{2,1,0:T(8,128)S(1)}, f32[20,8,128]{2,1,0:T(8,128)S(1)}, u32[]{:S(2)}, u32[]{:S(2)}) collective-permute-start(f32[20,8,128]{2,1,0:T(8,128)S(1)} %get-tuple-element.23), channel_id=1, source_target_pairs={{0,4},{4,0},{8,12},{12,8},{1,5},{5,1},{9,13},{13,9},{2,6},{6,2},{1... | collective-permute-start | bytes 245768 | tf_op jit(solution)/shard_map/ppermute | solution.py:574
  27.1 3.3 %collective-permute-start.7 = (f32[20,8,128]{2,1,0:T(8,128)S(1)}, f32[20,8,128]{2,1,0:T(8,128)S(1)}, u32[]{:S(2)}, u32[]{:S(2)}) collective-permute-start(f32[20,8,128]{2,1,0:T(8,128)S(1)} %get-tuple-element.24), channel_id=1, source_target_pairs={{0,0},{4,8},{8,4},{12,12},{1,1},{5,9},{9,5},{13,13},{2,2},{6,10},{... | collective-permute-start | bytes 245768 | tf_op jit(solution)/shard_map/ppermute | solution.py:580
  30.7 3.4 %collective-permute-start.8 = (f32[72,128]{1,0:T(8,128)S(1)}, f32[72,128]{1,0:T(8,128)S(1)}, u32[]{:S(2)}, u32[]{:S(2)}) collective-permute-start(f32[72,128]{1,0:T(8,128)S(1)} %get-tuple-element.27), channel_id=1, source_target_pairs={{0,1},{1,2},{2,3},{3,0},{4,5},{5,6},{6,7},{7,4},{8,9},{9,10},{10,1... | collective-permute-start | bytes 110600 | tf_op jit(solution)/shard_map/ppermute | solution.py:570
  30.8 3.4 %collective-permute-start.9 = (f32[72,128]{1,0:T(8,128)S(1)}, f32[72,128]{1,0:T(8,128)S(1)}, u32[]{:S(2)}, u32[]{:S(2)}) collective-permute-start(f32[72,128]{1,0:T(8,128)S(1)} %get-tuple-element.28), channel_id=1, source_target_pairs={{0,3},{1,0},{2,1},{3,2},{4,7},{5,4},{6,5},{7,6},{8,11},{9,8},{10,9... | collective-permute-start | bytes 110600 | tf_op jit(solution)/shard_map/ppermute | solution.py:570
